TPU v7x, 256 devices: a whole 4x4x8 slice. The times are simulated.
256 devices in a mesh: rel: 4 (over y), ent: 64 (over x, z, core).
Axes of the slice: x: 4, y: 4, z: 8, core: 2. Of those that a mesh axis runs over, the one named last changes fastest.
Arguments:
- factor: bfloat16 [16384, 512], P('ent'), may hold values from -1 to 1
- core_tensors: bfloat16 [32, 512, 512], P('rel'), may hold values from -0.25 to 0.25
- tile_values: bfloat16 [4, 4608, 128, 128], P('rel', 'ent'), may hold values from -4096 to 4096
- tile_rel: int32 [4, 4608], P('rel', 'ent'), may hold values from 0 to 7
- tile_block: int32 [4, 4608], P('rel', 'ent'), may hold values from 0 to 1
- tile_col: int32 [4, 4608], P('rel', 'ent'), may hold values from 0 to 127, as said below
- tile_flip: int32 [4, 4608], P('rel', 'ent'), may hold values from 0 to 1
- tile_count: int32 [4, 64], P('rel', 'ent'), may hold values from 64 to 72, as said below
Outputs:
- updated: float32 [16384, 512], P('ent')
Inputs may be any that keep to these rules, and one draw needn't show every extreme that they name: `tile_count`: live slots per device; the first 64 slots of every device are live, and in every group one device has all 72 slots live. `tile_col`: all slots of one device whose column blocks lie on one index of ent (column block // 2) name the same column block; the first 64 slots of a device name every index of ent once.
All inputs are finite; a program needn't handle non-finite values.
Results may differ from a plain program's by a relative error of at most 0.0036.
Values may be sent and summed in bfloat16 or wider, within the bound.
No kernel may reach another device: no remote copies, remote signals or barrier semaphores. Data moves between devices by JAX's collectives and lax.ppermute only.
A program may use at most 128 MiB of HBM per device.

v0:
```python
import jax
import jax.numpy as jnp
from jax import lax
from jax.sharding import PartitionSpec as P

ridge_weight = 16.0
top_precision = lax.Precision.HIGHEST


def accumulate(values, flip_bits, selected_entries, targets, live_slot, target_shape):
    direction_aligned = jnp.where(
        (flip_bits == 1)[:, None, None], jnp.swapaxes(values, 1, 2), values
    )
    tile_contributions = jnp.einsum(
        "ujl,uld->ujd", direction_aligned, selected_entries, preferred_element_type=jnp.float32
    )
    target_total = target_shape[0] * target_shape[1] * target_shape[2]
    indicator_matrix = (
        (targets[None, :] == jnp.arange(target_total)[:, None]) & live_slot[None, :]
    ).astype(jnp.float32)
    indicator_matrix = indicator_matrix.reshape(
        target_shape[0], target_shape[1], target_shape[2], targets.shape[0]
    )
    return jnp.einsum(
        "byvr,rex->beyvx", indicator_matrix, tile_contributions, precision=top_precision
    )


def local(factor, core_tensors, tile_values, tile_rel, tile_block, tile_col, tile_flip, tile_count):
    rank_width = factor.shape[1]
    tile_side = tile_values.shape[2]
    slot_count = tile_values.shape[1]
    block_count = factor.shape[0] // tile_side
    rel_local = core_tensors.shape[0]
    peer_count = lax.axis_size("ent")
    live_slot = jnp.arange(slot_count) < tile_count[0, 0]
    owners = tile_col[0] // block_count
    inner_block = tile_col[0] % block_count
    matches = (owners[None, :] == jnp.arange(peer_count)[:, None]) & live_slot[None, :]
    wanted = jnp.max(jnp.where(matches, inner_block[None, :], 0), axis=1)
    requested = lax.all_to_all(
        wanted.reshape(peer_count, 1), "ent", split_axis=0, concat_axis=0, tiled=True
    )
    outgoing = jnp.take(factor.reshape(block_count, tile_side, rank_width), requested[:, 0], axis=0)
    factor_panels = lax.all_to_all(outgoing, "ent", split_axis=0, concat_axis=0, tiled=True)
    targets = (tile_block[0] * 2 + tile_flip[0]) * rel_local + tile_rel[0]
    gram_local = lax.dot_general(
        factor, factor, (((0,), (0,)), ((), ())), preferred_element_type=jnp.float32
    )
    gram_matrix = lax.psum(gram_local, "ent")
    position = lax.axis_index("ent")
    row_splits = peer_count // rel_local
    row_width = rank_width // row_splits
    relation = position % rel_local
    row_part = position // rel_local
    core_matrix = lax.dynamic_index_in_dim(core_tensors, relation, 0, keepdims=False).astype(
        jnp.float32
    )
    core_rows = lax.dynamic_slice_in_dim(core_matrix, row_part * row_width, row_width, 0)
    core_cols = lax.dynamic_slice_in_dim(core_matrix, row_part * row_width, row_width, 1)
    system_rows = jnp.dot(
        jnp.dot(core_rows, gram_matrix, precision=top_precision),
        core_matrix.T,
        precision=top_precision,
    )
    system_rows = system_rows + jnp.dot(
        jnp.dot(core_cols.T, gram_matrix, precision=top_precision),
        core_matrix,
        precision=top_precision,
    )
    placed = lax.dynamic_update_slice_in_dim(
        jnp.zeros((rank_width, rank_width), jnp.float32), system_rows, row_part * row_width, 0
    )
    system = lax.psum(placed, ("rel", "ent")) + ridge_weight * jnp.eye(
        rank_width, dtype=jnp.float32
    )
    lower_factor = jnp.linalg.cholesky(system)
    target_shape = (block_count, 2, rel_local)
    selected_entries = jnp.take(factor_panels, owners, axis=0)
    block_totals_sum = accumulate(
        tile_values[0], tile_flip[0], selected_entries, targets, live_slot, target_shape
    )
    flat_sums = block_totals_sum.astype(jnp.bfloat16).reshape(
        block_count * tile_side, 2 * rel_local * rank_width
    )
    weights = jnp.concatenate([jnp.swapaxes(core_tensors, 1, 2), core_tensors], axis=0)
    weights = weights.reshape(2 * rel_local * rank_width, rank_width)
    partial_rows = jnp.dot(flat_sums, weights, preferred_element_type=jnp.float32)
    totals = lax.psum(partial_rows, "rel")
    updated = jax.scipy.linalg.cho_solve((lower_factor, True), totals.T).T
    return updated


def solution(mesh):
    in_specs = (
        P("ent", None),
        P("rel", None, None),
        P("rel", "ent", None, None),
        P("rel", "ent"),
        P("rel", "ent"),
        P("rel", "ent"),
        P("rel", "ent"),
        P("rel", "ent"),
    )
    out_specs = P("ent", None)
    return jax.shard_map(local, mesh=mesh, in_specs=in_specs, out_specs=out_specs, check_vma=False)
```

profile of v0, /device:TPU:1, one launch (start us, length us, event | category | flops | bytes accessed | tf_op | source)
XLA Modules:
  0.0 779.8 jit_solution(14711024798869153278)
XLA Ops:
  7.4 0.7 fusion.80
  9.0 22.1 %all_to_all.20 = s32[64,1,1]{2,1,0:T(1,128)S(1)} all-to-all(s32[64,1,1]{2,1,0:T(1,128)S(1)} %copy.101), channel_id=1, replica_groups=mesh['rel'=4,'ent'=64] {'ent'}, dimensions={0} | all-to-all | bytes 512 | tf_op jit(solution)/shard_map/all_to_all | solution.py:41
  31.0 1.2 reduce.24
  32.3 5.4 gather_fusion
  37.7 7.5 broadcast_select_fusion
  45.1 5.9 all-to-all-start.1
  51.1 1.3 fusion.88
  52.6 2.5 copy.100
  55.1 6.4 copy.99
  61.7 221.1 %all-reduce.5.cloned.1.call-done = f32[512,512]{1,0:T(8,128)} async-done(((f32[512,512]{1,0:T(8,128)}), f32[512,512]{1,0:T(8,128)}) %all-reduce.5.cloned.1.call-update) | async-done | bytes 1048592 | tf_op jit(solution)/shard_map/psum | solution.py:50
  282.8 1.8 fusion.56
  284.6 1.6 fusion.14
  286.2 1.9 fusion.46
  288.1 1.4 convolution_add_fusion
  289.7 1.1 broadcast_in_dim.55
  290.8 1.8 dynamic_update_slice.3
  292.9 7.5 pad_maximum_fusion
  300.4 246.3 %all-reduce.7.cloned.1.call-done = f32[512,512]{0,1:T(8,128)} async-done(((f32[512,512]{0,1:T(8,128)}), f32[512,512]{0,1:T(8,128)}) %all-reduce.7.cloned.1.call-update) | async-done | bytes 1048592 | tf_op jit(solution)/shard_map/psum | solution.py:74
  546.7 2.4 select_add_fusion
  549.0 2.6 copy.90
  551.6 1.8 fusion.12
  553.4 1.0 copy-done.4
  554.4 11.7 %cholesky.103 = f32[128,128]{1,0:T(8,128)S(1)} custom-call(f32[128,128]{1,0:T(8,128)S(1)} %cholesky.263), custom_call_target="Cholesky" | custom-call | tf_op jit(solution)/shard_map/jit(cholesky)/cholesky | solution.py:77
  566.2 9.8 %custom-call.34 = f32[1,128,128]{1,2,0:T(8,128)S(1)} custom-call(f32[1,128,128]{2,1,0:T(8,128)S(1)} %get-tuple-element.52), custom_call_target="InvertDiagBlocksLowerTriangular" | custom-call | tf_op jit(solution)/shard_map/jit(cholesky)/cholesky | solution.py:77
  576.0 1.2 fusion.38
  577.4 1.3 convolution_subtract_fusion
  578.7 11.7 %cholesky.215 = f32[128,128]{1,0:T(8,128)S(1)} custom-call(f32[128,128]{1,0:T(8,128)S(1)} %cholesky.267), custom_call_target="Cholesky" | custom-call | tf_op jit(solution)/shard_map/jit(cholesky)/cholesky | solution.py:77
  590.4 1.2 cholesky.222
  591.7 10.2 %custom-call.35 = f32[1,128,128]{1,2,0:T(8,128)S(1)} custom-call(f32[1,128,128]{2,1,0:T(8,128)S(1)} %get-tuple-element.50), custom_call_target="InvertDiagBlocksLowerTriangular" | custom-call | tf_op jit(solution)/shard_map/jit(cholesky)/cholesky | solution.py:77
  601.9 0.7 constant_dynamic-update-slice_fusion.1
  602.6 0.6 constant_dynamic-update-slice_fusion.3
  603.3 1.0 convolution_dynamic-update-slice_fusion
  604.2 1.6 convolution_subtract_fusion.5
  605.9 11.7 %cholesky.236 = f32[128,128]{1,0:T(8,128)S(1)} custom-call(f32[128,128]{1,0:T(8,128)S(1)} %cholesky.272), custom_call_target="Cholesky" | custom-call | tf_op jit(solution)/shard_map/jit(cholesky)/cholesky | solution.py:77
  617.7 9.8 %custom-call.36 = f32[1,128,128]{1,2,0:T(8,128)S(1)} custom-call(f32[1,128,128]{2,1,0:T(8,128)S(1)} %get-tuple-element.48), custom_call_target="InvertDiagBlocksLowerTriangular" | custom-call | tf_op jit(solution)/shard_map/jit(cholesky)/cholesky | solution.py:77
  627.6 0.6 constant_dynamic-update-slice_fusion
  628.2 0.9 convolution_dynamic-update-slice_fusion.1
  629.1 1.5 convolution_subtract_fusion.8
  630.7 11.9 %cholesky.253 = f32[128,128]{1,0:T(8,128)S(1)} custom-call(f32[128,128]{1,0:T(8,128)S(1)} %convolution_subtract_fusion.8), custom_call_target="Cholesky" | custom-call | tf_op jit(solution)/shard_map/jit(cholesky)/cholesky | solution.py:77
  642.6 0.6 compare_reduce_fusion.2
  644.5 0.6 compare_reduce_fusion.1
  645.8 0.6 compare_reduce_fusion
  647.1 0.7 constant_dynamic-update-slice_fusion.2
  647.8 2.3 select_select_fusion
  650.1 9.4 %gather_fusion.1 = bf16[72,128,512]{2,1,0:T(8,128)(2,1)} fusion(bf16[64,128,512]{2,1,0:T(8,128)(2,1)} %all-to-all-done.1, s32[1024]{0:T(1024)S(1)} %pad_clamp_fusion), kind=kCustom, calls=%fused_computation.1 | custom fusion | bytes 18874656 | tf_op jit(solution)/shard_map/jit(_take)/gather | solution.py:79
  659.5 13.7 %fusion.5 = f32[72,128,512,1,1]{2,1,0,4,3:T(8,128)} fusion(bf16[72,128,512]{2,1,0:T(8,128)(2,1)} %gather_fusion.1, pred[72]{0:T(512)(128)(4,1)S(1)} %compare_and_fusion.1, bf16[72,128,128]{1,2,0:T(8,128)(2,1)} %copy.100, pred[72]{0:T(512)(128)(4,1)S(1)} %compare_bitcast_fusion, bf16[1,72,128,128]{3,2,1,0:T(8,128)(2,1)S(1)} %copy-done.2), kind=kOutput, calls=%fused_computation.9 | convolution fusion | flops 1213857792 | bytes 33030288 | tf_op jit(solution)/shard_map/ujl,uld->ujd/dot_general | solution.py:14
  673.2 23.8 %convert_bitcast_fusion = bf16[2,128,2,8,512]{4,3,2,0,1:T(8,128)(2,1)S(1)} fusion(f32[72,128,512,1,1]{2,1,0,4,3:T(8,128)} %fusion.5, s32[2,2,8]{2,1,0:T(2,128)S(1)} %multiply_add_fusion, s32[72]{0:T(128)S(1)} %add_bitcast_fusion, pred[72]{0:T(512)(128)(4,1)S(1)} %iota_compare_fusion.5), kind=kOutput, calls=%fused_computation.13 | convolution fusion | flops 1814041088 | bytes 23069160 | tf_op jit(solution)/shard_map/byvr,rex->beyvx/dot_general | solution.py:24
  697.0 2.4 copy.103
  699.4 7.6 reshape.219
  707.0 7.8 %fusion.89 = f32[512,256]{1,0:T(8,128)} fusion(bf16[8192,512]{1,0:T(8,128)(2,1)} %bitcast.136, bf16[256,8192]{1,0:T(8,128)(2,1)} %reshape.219), kind=kOutput, calls=%fused_computation.162 | convolution fusion | flops 2147483648 | bytes 13107200 | tf_op jit(solution)/shard_map/dot_general | solution.py:88
  714.9 8.6 %while.1 = (s32[]{:T(128)}, f32[512,512]{0,1:T(8,128)S(1)}, s32[4,2]{0,1:T(2,128)S(1)}, f32[4,128,128]{2,1,0:T(8,128)S(1)}, s32[]{:T(128)}) while((s32[]{:T(128)}, f32[512,512]{0,1:T(8,128)S(1)}, s32[4,2]{0,1:T(2,128)S(1)}, f32[4,128,128]{2,1,0:T(8,128)S(1)}, s32[]{:T(128)}) %tuple.39), condition=%wide.while_cond, body=%wide.while_body.sunk | while | flops 2 | bytes 393321 | solution.py:90
  715.0 0.6 fusion.109
  715.6 1.3 dynamic-slice.11
  717.2 0.6 fusion.109
  717.8 1.3 dynamic-slice.11
  719.3 0.6 fusion.109
  719.9 1.3 dynamic-slice.11
  722.1 1.3 dynamic-slice.11
  723.6 39.3 %custom-call.37 = f32[4,128,128]{1,2,0:T(8,128)S(1)} custom-call(f32[4,128,128]{2,1,0:T(8,128)S(1)} %get-tuple-element.12), custom_call_target="InvertDiagBlocksLowerTriangular" | custom-call | tf_op jit(solution)/shard_map/jit(_cho_solve)/triangular_solve | solution.py:90
  762.9 1.2 fusion.42
  764.2 1.2 convolution_subtract_fusion.7
  765.7 1.3 convolution_subtract_fusion.4
  767.3 1.4 convolution_subtract_fusion.3
  771.1 1.0 copy.104
  (77 shorter events, 5.8 us)
Async XLA Ops:
  7.4 24.9 %copy-start = (bf16[256,512]{1,0:T(8,128)(2,1)S(1)}, bf16[256,512]{1,0:T(8,128)(2,1)}, u32[]{:S(2)}) copy-start(bf16[256,512]{1,0:T(8,128)(2,1)} %param.8) | copy-start | bytes 786436
  45.1 7.4 copy-start.2
  45.1 604.9 %all-to-all-start.1 = ((bf16[64,128,512]{2,1,0:T(8,128)(2,1)}), bf16[64,128,512]{2,1,0:T(8,128)(2,1)}, u32[]{:S(2)}, u32[]{:S(2)}) async-start(bf16[64,128,512]{2,1,0:T(8,128)(2,1)} %broadcast_select_fusion), calls=%async_computation.1 | async-start | bytes 16777216 | tf_op jit(solution)/shard_map/all_to_all | solution.py:45
  51.0 10.5 %copy-start.8 = (s32[1,72]{1,0:T(1,128)S(1)}, s32[1,72]{1,0:T(1,128)}, u32[]{:S(2)}) copy-start(s32[1,72]{1,0:T(1,128)} %param.13) | copy-start | bytes 868
  51.0 10.6 %copy-start.5 = (s32[1,72]{1,0:T(1,128)S(1)}, s32[1,72]{1,0:T(1,128)}, u32[]{:S(2)}) copy-start(s32[1,72]{1,0:T(1,128)} %param.14) | copy-start | bytes 868
  51.0 10.6 %copy-start.6 = (s32[1,72]{1,0:T(1,128)S(1)}, s32[1,72]{1,0:T(1,128)}, u32[]{:S(2)}) copy-start(s32[1,72]{1,0:T(1,128)} %param.11) | copy-start | bytes 868
  51.1 10.6 %copy-start.7 = (s32[1,72]{1,0:T(1,128)S(1)}, s32[1,72]{1,0:T(1,128)}, u32[]{:S(2)}) copy-start(s32[1,72]{1,0:T(1,128)} %param.12) | copy-start | bytes 868
  51.1 231.7 %all-reduce.5.cloned.1.call-start = ((), (), s32[]{:S(2)}) async-start(), calls=%async_computation.2 | async-start | bytes 2097152 | tf_op jit(solution)/shard_map/psum | solution.py:50
  52.5 494.2 %all-reduce.7.cloned.1.call-start = ((), (), s32[]{:S(2)}) async-start(), calls=%async_computation.3 | async-start | bytes 2097152 | tf_op jit(solution)/shard_map/psum | solution.py:74
  292.7 470.3 %all-reduce.9.cloned.1.call-start = ((), (), s32[]{:S(2)}) async-start(), calls=%async_computation.4 | async-start | bytes 1048576 | tf_op jit(solution)/shard_map/psum | solution.py:89
  553.4 1.0 copy-start.4
  707.0 7.9 %copy-start.3 = (f32[512,512]{0,1:T(8,128)S(1)}, f32[512,512]{0,1:T(8,128)}, u32[]{:S(2)}) copy-start(f32[512,512]{0,1:T(8,128)} %select_select_fusion) | copy-start | bytes 3145732
  707.0 65.1 %copy-start.1 = (bf16[256,512]{1,0:T(8,128)(2,1)S(1)}, bf16[256,512]{1,0:T(8,128)(2,1)}, u32[]{:S(2)}) copy-start(bf16[256,512]{1,0:T(8,128)(2,1)} %param.8) | copy-start | bytes 786436
Sparse Core Ops, SparseCore 0:
  55.3 227.4 all-reduce.4
  292.8 253.8 all-reduce.6
Sparse Core Ops, SparseCore 1:
  715.0 46.3 all-reduce.8
where the time goes:
time: 787 us; the launch traced here: 780 us
  waiting for transfers between devices  467 us (59%)
  other arithmetic  142 us (18%)
  matrix products  69 us (9%)
  local copies, waits for them, and re-layouts  54.4 us (7%)
  blocking collectives  22.1 us (3%)
  between operations  18.8 us (2%)
    psum x1, waiting for transfers between devices, local(): lax.psum(placed, ('rel', 'ent'))  246 us
    psum x1, waiting for transfers between devices, local(): gram_matrix = lax.psum(gram_local, 'ent')  221 us
    another operation x14, other arithmetic, local(): lower_factor = jnp.linalg.cholesky(system)  78.9 us
    another operation x3, other arithmetic, local(): updated = jax.scipy.linalg.cho_solve((lower_factor, True), totals.T).T  41.6 us
    dot_general x1, matrix products, accumulate(): jnp.einsum('byvr,rex->beyvx', indicator_matrix, tile_contributions, preci...  23.8 us
    all_to_all x1, blocking collectives, local(): lax.all_to_all(wanted.reshape(peer_count, 1), 'ent', split_axis=0, concat...  22.1 us
  transfers between devices with their start and end apart: 4, of which 2 were waited for; matrix products, arithmetic and copies ran while one was open for 22% of the time, Pallas kernels for 0%

commit v1 on v0

v1 whole, which is shorter than its diff:
```python
import jax
import jax.numpy as jnp
from jax import lax
from jax.experimental import pallas as pl
from jax.experimental.pallas import tpu as pltpu
from jax.sharding import PartitionSpec as P

HI = lax.Precision.HIGHEST
VM = 60 * 1024 * 1024

def dg(a, b, ca, cb):
    return lax.dot_general(a, b, (((ca,), (cb,)), ((), ())), preferred_element_type=jnp.float32)

def system_kernel(a_ref, core_ref, out_ref, d0_ref, d1_ref, low_ref, c0_ref, c1_ref):
    rows = a_ref[...]
    sums = (d0_ref, d1_ref, low_ref, c0_ref, c1_ref)
    for ref in sums:
        ref[...] = jnp.zeros_like(ref)

    def body(step, carry):
        core = core_ref[step]
        term = jnp.concatenate([dg(rows, core, 1, 1), dg(rows, core, 1, 0)], axis=0)
        high = term.astype(jnp.bfloat16)
        low = (term - high.astype(jnp.float32)).astype(jnp.bfloat16)
        h0, h1 = high[:, :256], high[:, 256:]
        l0, l1 = low[:, :256], low[:, 256:]
        h0t, h1t, l1t = h0.T, h1.T, l1.T
        d0_ref[...] += jnp.dot(h0t, h0, preferred_element_type=jnp.float32)
        d1_ref[...] += jnp.dot(h1t, h1, preferred_element_type=jnp.float32)
        c0_ref[...] += jnp.dot(h0t, l0, preferred_element_type=jnp.float32)
        c1_ref[...] += jnp.dot(h1t, l1, preferred_element_type=jnp.float32)
        low_ref[...] += (
            jnp.dot(h1t, h0, preferred_element_type=jnp.float32)
            + jnp.dot(h1t, l0, preferred_element_type=jnp.float32)
            + jnp.dot(l1t, h0, preferred_element_type=jnp.float32)
        )
        return carry

    lax.fori_loop(0, core_ref.shape[0], body, 0)
    first = d0_ref[...] + (c0_ref[...] + c0_ref[...].T)
    last = d1_ref[...] + (c1_ref[...] + c1_ref[...].T)
    mixed = low_ref[...]
    parts = (
        first[:128, :128], first[128:, :128], first[128:, 128:],
        mixed[:128, :128], mixed[:128, 128:], last[:128, :128],
        mixed[128:, :128], mixed[128:, 128:], last[128:, :128], last[128:, 128:],
    )
    for index, part in enumerate(parts):
        out_ref[pl.ds(index * 128, 128), :] = part

def system_term(factor, cores):
    return pl.pallas_call(
        system_kernel,
        out_shape=jax.ShapeDtypeStruct((1280, 128), jnp.float32),
        in_specs=[pl.BlockSpec(memory_space=pltpu.VMEM)] * 2,
        out_specs=pl.BlockSpec(memory_space=pltpu.VMEM),
        scratch_shapes=[pltpu.VMEM((256, 256), jnp.float32)] * 5,
        compiler_params=pltpu.CompilerParams(vmem_limit_bytes=VM),
        cost_estimate=pl.CostEstimate(flops=6500000000, bytes_accessed=5000000, transcendentals=0),
    )(factor, cores)

def invert_block(m):
    rows = lax.broadcasted_iota(jnp.int32, (128, 128), 0)
    lanes = lax.broadcasted_iota(jnp.int32, (128, 128), 1)
    lane1 = lax.broadcasted_iota(jnp.int32, (1, 128), 1)
    for k in range(128):
        row = m[k:k + 1, :]
        col = m[:, k:k + 1]
        inv = 1.0 / m[k:k + 1, k:k + 1]
        scaled = jnp.where(lane1 == k, 1.0, row) * inv
        rest = jnp.where(lanes == k, 0.0, m)
        m = jnp.where(rows == k, scaled, rest - col * scaled)
    return m

def inverse_kernel(packed_ref, out_ref, blk_ref):
    index = 0
    for i in range(4):
        for j in range(i + 1):
            blk = packed_ref[pl.ds(index * 128, 128), :]
            if i == j:
                eye = lax.broadcasted_iota(jnp.int32, (128, 128), 0) == lax.broadcasted_iota(jnp.int32, (128, 128), 1)
                blk = blk + jnp.where(eye, 16.0, 0.0)
            out_ref[pl.ds(i * 128, 128), pl.ds(j * 128, 128)] = blk
            if i != j:
                out_ref[pl.ds(j * 128, 128), pl.ds(i * 128, 128)] = blk.T
            index += 1

    lane_block = lax.broadcasted_iota(jnp.int32, (512, 512), 1) // 128
    row_lane = lax.broadcasted_iota(jnp.int32, (128, 512), 1)
    sub_lane = lax.broadcasted_iota(jnp.int32, (128, 512), 0)

    def stage(p, carry):
        start = pl.multiple_of(p * 128, 128)
        col = out_ref[:, pl.ds(start, 128)]
        pivot = invert_block(out_ref[pl.ds(start, 128), pl.ds(start, 128)])
        row = out_ref[pl.ds(start, 128), :]
        eye = (row_lane - start == sub_lane).astype(jnp.float32)
        row = jnp.where(row_lane // 128 == p, eye, row)
        scaled = jnp.dot(pivot, row, precision=HI, preferred_element_type=jnp.float32)
        rest = jnp.where(lane_block == p, 0.0, out_ref[...])
        out_ref[...] = rest - jnp.dot(col, scaled, precision=HI, preferred_element_type=jnp.float32)
        out_ref[pl.ds(start, 128), :] = scaled
        return carry

    lax.fori_loop(0, 4, stage, 0)

def inverse(packed):
    return pl.pallas_call(
        inverse_kernel,
        out_shape=jax.ShapeDtypeStruct((512, 512), jnp.float32),
        in_specs=[pl.BlockSpec(memory_space=pltpu.VMEM)],
        out_specs=pl.BlockSpec(memory_space=pltpu.VMEM),
        scratch_shapes=[pltpu.VMEM((128, 128), jnp.float32)],
        compiler_params=pltpu.CompilerParams(vmem_limit_bytes=VM),
        cost_estimate=pl.CostEstimate(flops=3000000000, bytes_accessed=2000000, transcendentals=0),
    )(packed)

def align_kernel(rel_ref, block_ref, col_ref, flip_ref, values_ref, out_ref, place_ref, order_ref):
    def note(slot, carry):
        order_ref[col_ref[slot] // 2] = slot
        return carry

    lax.fori_loop(0, 64, note, 0)

    def move(index, carry):
        slot = jnp.where(index < 64, order_ref[jnp.minimum(index, 63)], index)
        flip = flip_ref[slot]
        place_ref[0, index] = col_ref[slot]
        place_ref[1, index] = flip * 8 + rel_ref[slot]
        place_ref[2, index] = block_ref[slot]
        tile = values_ref[slot]
        out_ref[index] = jnp.where(flip == 1, tile.T, tile)
        return carry

    lax.fori_loop(0, values_ref.shape[0], move, 0)


def align(tile_rel, tile_block, tile_col, tile_flip, values):
    slots = values.shape[0]
    scalar = pl.BlockSpec(memory_space=pltpu.SMEM)
    vector = pl.BlockSpec(memory_space=pltpu.VMEM)
    return pl.pallas_call(
        align_kernel,
        out_shape=(
            jax.ShapeDtypeStruct(values.shape, values.dtype),
            jax.ShapeDtypeStruct((3, slots), jnp.int32),
        ),
        in_specs=[scalar] * 4 + [vector],
        out_specs=(vector, scalar),
        scratch_shapes=[pltpu.SMEM((64,), jnp.int32)],
        compiler_params=pltpu.CompilerParams(vmem_limit_bytes=VM),
        cost_estimate=pl.CostEstimate(flops=100000000, bytes_accessed=4800000, transcendentals=0),
    )(tile_rel, tile_block, tile_col, tile_flip, values)


def rows_kernel(count_ref, place_ref, values_ref, panel_ref, core_ref, out_ref, sums_ref):
    chunk = pl.program_id(0)

    @pl.when(chunk == 0)
    def _():
        sums_ref[...] = jnp.zeros_like(sums_ref)

    def add(index, base):
        start = pl.multiple_of((place_ref[0, index] - base) * 128, 128)
        place = pl.multiple_of(place_ref[2, index] * 128, 128)
        term = jnp.dot(
            values_ref[index], panel_ref[pl.ds(start, 128), :], preferred_element_type=jnp.float32
        )
        where = (place_ref[1, index], pl.ds(place, 128), slice(None))
        sums_ref[where] = sums_ref[where] + term

    for owner in range(8):
        add(chunk * 8 + owner, chunk * 16)

    def extra(index, carry):
        @pl.when(place_ref[0, index] // 16 == chunk)
        def _():
            add(index, chunk * 16)

        return carry

    lax.fori_loop(64, count_ref[0], extra, 0)

    @pl.when(chunk == pl.num_programs(0) - 1)
    def _():
        out_ref[...] = jnp.zeros_like(out_ref)

        def relation(k, carry):
            core = core_ref[k]
            straight = sums_ref[k].astype(jnp.bfloat16)
            turned = sums_ref[k + 8].astype(jnp.bfloat16)
            out_ref[...] += dg(straight, core, 1, 1) + dg(turned, core, 1, 0)
            return carry

        lax.fori_loop(0, 8, relation, 0)


def partial_rows(count, place, values, panels, cores):
    slots = values.shape[0]
    return pl.pallas_call(
        rows_kernel,
        out_shape=jax.ShapeDtypeStruct((256, 512), jnp.float32),
        grid=(8,),
        in_specs=[
            pl.BlockSpec(memory_space=pltpu.SMEM),
            pl.BlockSpec(memory_space=pltpu.SMEM),
            pl.BlockSpec((slots, 128, 128), lambda i: (0, 0, 0)),
            pl.BlockSpec((2048, 512), lambda i: (i, 0)),
            pl.BlockSpec((8, 512, 512), lambda i: (0, 0, 0)),
        ],
        out_specs=pl.BlockSpec((256, 512), lambda i: (0, 0)),
        scratch_shapes=[pltpu.VMEM((16, 256, 512), jnp.float32)],
        compiler_params=pltpu.CompilerParams(vmem_limit_bytes=VM),
        cost_estimate=pl.CostEstimate(flops=5000000000, bytes_accessed=24000000, transcendentals=0),
    )(count, place, values, panels, cores)


def ent_shift(dx, dz, dc):
    pairs = []
    for x in range(4):
        for z in range(8):
            for c in range(2):
                there = (((x + dx) % 4) * 8 + (z + dz) % 8) * 2 + (c + dc) % 2
                pairs.append(((x * 8 + z) * 2 + c, there))
    return pairs


def ent_swap_z(bit):
    return [(e, e ^ (bit * 2)) for e in range(64)]


def rel_shift(d):
    return [(y, (y + d) % 4) for y in range(4)]


def scatter_sum(pieces, position, send):
    arrived = [send(lax.dynamic_index_in_dim(pieces, (position + d) % 4, 0, False), d) for d in (1, 2, 3)]
    own = lax.dynamic_index_in_dim(pieces, position, 0, False)
    return (own + arrived[1]) + (arrived[0] + arrived[2])


def gather(piece, position, send):
    parts = [piece] + [send(piece, d) for d in (1, 2, 3)]
    stack = jnp.stack(parts[:1] + parts[:0:-1] + parts[:1] + parts[:0:-1])
    return lax.dynamic_slice_in_dim(stack, (4 - position) % 4, 4, 0)


def sum_everywhere(packed):
    ent = lax.axis_index("ent")
    y = lax.axis_index("rel")
    x, core = ent // 16, ent % 2
    over_y = lambda v, d: lax.ppermute(v, "rel", rel_shift(d))
    over_x = lambda v, d: lax.ppermute(v, "ent", ent_shift(d, 0, 0))
    over_core = lambda v: lax.ppermute(v, "ent", ent_shift(0, 0, 1))
    halves = packed.reshape(2, 640, 128)
    part = lax.dynamic_index_in_dim(halves, core, 0, False) + over_core(
        lax.dynamic_index_in_dim(halves, 1 - core, 0, False)
    )
    part = scatter_sum(part.reshape(4, 160, 128), y, over_y)
    part = scatter_sum(part.reshape(4, 40, 128), x, over_x)
    for bit in (1, 2, 4):
        part = part + lax.ppermute(part, "ent", ent_swap_z(bit))
    part = gather(part, x, over_x).reshape(160, 128)
    part = gather(part, y, over_y).reshape(640, 128)
    other = over_core(part)
    first = jnp.where(core == 0, part, other)
    last = jnp.where(core == 0, other, part)
    return jnp.concatenate([first, last], axis=0)


def local(factor, core_tensors, tile_values, tile_rel, tile_block, tile_col, tile_flip, tile_count):
    panels = lax.all_gather(factor, "ent", tiled=True)
    system = sum_everywhere(system_term(factor, core_tensors))
    inverted = inverse(system)
    values, place = align(tile_rel[0], tile_block[0], tile_col[0], tile_flip[0], tile_values[0])
    rows = partial_rows(tile_count[0], place, values, panels, core_tensors)
    y = lax.axis_index("rel")
    over_y = lambda v, d: lax.ppermute(v, "rel", rel_shift(d))
    mine = scatter_sum(rows.reshape(4, 64, 512), y, over_y)
    updated = jnp.dot(mine, inverted, precision=HI)
    return gather(updated, y, over_y).reshape(256, 512)


def solution(mesh):
    in_specs = (
        P("ent", None),
        P("rel", None, None),
        P("rel", "ent", None, None),
        P("rel", "ent"),
        P("rel", "ent"),
        P("rel", "ent"),
        P("rel", "ent"),
        P("rel", "ent"),
    )
    out_specs = P("ent", None)
    return jax.shard_map(local, mesh=mesh, in_specs=in_specs, out_specs=out_specs, check_vma=False)
```

time: 787 us -> 206 us (0.26)
  waiting for transfers between devices: 467 us -> 50.2 us
  other arithmetic: 142 us -> 1.99 us
  Pallas kernels: 0 us -> 88.8 us
  matrix products: 69 us -> 2.07 us
  local copies, waits for them, and re-layouts: 54.4 us -> 3.14 us
  starting transfers between devices: 6.17 us -> 44.7 us
  blocking collectives: 22.1 us -> 0 us
    psum x3 -> x0, waiting for transfers between devices: 467 us -> none  [the longest x1 246 us: local(): lax.psum(placed, ('rel', 'ent'))]
    another operation x17 -> x0, other arithmetic: 120 us -> none  [the longest x14 78.9 us: local(): lower_factor = jnp.linalg.cholesky(system)]
    pallas_call x0 -> x4, Pallas kernels: none -> 88.8 us  [the longest x1 51.2 us: inverse(): pl.pallas_call(inverse_kernel, out_shape=jax.ShapeDtypeStruct((512, 512),...]
    dot_general x8 -> x1, matrix products: 53.4 us -> 2.07 us  [local(): updated = jnp.dot(mine, inverted, precision=HI)]
    ppermute x0 -> x23, starting transfers between devices: none -> 44.7 us  [the longest x2 12.7 us: sum_everywhere(): over_core = lambda v: lax.ppermute(v, 'ent', ent_shift(0, 0, 1))]
    all_gather x0 -> x1, waiting for transfers between devices: none -> 25.3 us  [local(): panels = lax.all_gather(factor, 'ent', tiled=True)]
    ppermute x0 -> x23, waiting for transfers between devices: none -> 24.2 us  [the longest x6 7.45 us: sum_everywhere(): over_y = lambda v, d: lax.ppermute(v, 'rel', rel_shift(d))]
    all_to_all x1 -> x0, blocking collectives: 22.1 us -> none  [local(): lax.all_to_all(wanted.reshape(peer_count, 1), 'ent', split_axis=0, concat...]
  transfers between devices with their start and end apart: 4 -> 24, of which waited for: 2 -> 13; matrix products, arithmetic and copies ran while one was open for 22% -> 2% of each run, Pallas kernels for 0% -> 35%
where the time goes in v1:
time: 206 us; the launch traced here: 205 us
  Pallas kernels  88.8 us (43%)
  waiting for transfers between devices  50.2 us (24%)
  starting transfers between devices  44.7 us (22%)
  between operations  14.3 us (7%)
  local copies, waits for them, and re-layouts  3.14 us (2%)
  matrix products  2.07 us (1%)
    pallas_call x1, Pallas kernels, inverse(): pl.pallas_call(inverse_kernel, out_shape=jax.ShapeDtypeStruct((512, 512),...  51.2 us
    all_gather x1, waiting for transfers between devices, local(): panels = lax.all_gather(factor, 'ent', tiled=True)  25.3 us
    pallas_call x1, Pallas kernels, partial_rows(): pl.pallas_call(rows_kernel, out_shape=jax.ShapeDtypeStruct((256, 512), jn...  16 us
    ppermute x2, starting transfers between devices, sum_everywhere(): over_core = lambda v: lax.ppermute(v, 'ent', ent_shift(0, 0, 1))  12.7 us
    pallas_call x1, Pallas kernels, system_term(): pl.pallas_call(system_kernel, out_shape=jax.ShapeDtypeStruct((1280, 128),...  12.4 us
    ppermute x3, starting transfers between devices, sum_everywhere(): part = part + lax.ppermute(part, 'ent', ent_swap_z(bit))  10.4 us
    pallas_call x1, Pallas kernels, align(): pl.pallas_call(align_kernel, out_shape=(jax.ShapeDtypeStruct(values.shape...  9.2 us
    ppermute x6, starting transfers between devices, sum_everywhere(): over_x = lambda v, d: lax.ppermute(v, 'ent', ent_shift(d, 0, 0))  7.93 us
  transfers between devices with their start and end apart: 24, of which 13 were waited for; matrix products, arithmetic and copies ran while one was open for 2% of the time, Pallas kernels for 35%

profile of v1, /device:TPU:1, one launch (start us, length us, event | category | flops | bytes accessed | tf_op | source)
XLA Modules:
  0.0 205.3 jit_solution(4471155484197509454)
XLA Ops:
  6.5 0.0 all-gather.2.cloned.1.call-start
  6.5 0.7 all-gather.2.cloned.1.call-update
  7.3 12.4 %shard_map.84 = f32[1280,128]{1,0:T(8,128)} custom-call(bf16[256,512]{1,0:T(8,128)(2,1)} %a_ref.1, bf16[8,512,512]{2,1,0:T(8,128)(2,1)} %core_ref.3), custom_call_target="tpu_custom_call" | custom-call | flops 6499999744 | bytes 5000000 | tf_op jit(solution)/shard_map/pallas_call | solution.py:52
  19.6 1.0 dynamic-slice_bitcast_fusion
  20.6 3.3 %collective-permute-start.3 = (f32[640,128]{1,0:T(8,128)S(1)}, f32[640,128]{1,0:T(8,128)S(1)}, u32[]{:S(2)}, u32[]{:S(2)}) collective-permute-start(f32[640,128]{1,0:T(8,128)S(1)} %dynamic-slice_bitcast_fusion), channel_id=1, source_target_pairs={{0,1},{1,0},{2,3},{3,2},{4,5},{5,4},{6,7},{7,6},{8,9},{9,8},{10,11... | collective-permute-start | bytes 983048 | tf_op jit(solution)/shard_map/ppermute | solution.py:254
  24.0 1.3 collective-permute-done.3
  25.2 1.0 bitcast_add_fusion
  26.3 1.1 collective-permute-start.6
  27.3 0.5 collective-permute-start.5
  27.8 1.2 collective-permute-start.4
  29.0 1.1 collective-permute-done.6
  30.1 2.1 %collective-permute-done.5 = f32[160,128]{1,0:T(8,128)S(1)} collective-permute-done((f32[160,128]{1,0:T(8,128)S(1)}, f32[160,128]{1,0:T(8,128)S(1)}, u32[]{:S(2)}, u32[]{:S(2)}) %collective-permute-start.5) | collective-permute-done | bytes 81952 | tf_op jit(solution)/shard_map/ppermute | solution.py:252
  32.3 0.6 collective-permute-done.4
  32.9 3.0 %collective-permute-start.9 = (f32[40,128]{1,0:T(8,128)S(1)}, f32[40,128]{1,0:T(8,128)S(1)}, u32[]{:S(2)}, u32[]{:S(2)}) collective-permute-start(f32[40,128]{1,0:T(8,128)S(1)} %get-tuple-element.19), channel_id=1, source_target_pairs={{0,48},{1,49},{2,50},{3,51},{4,52},{5,53},{6,54},{7,55},{8,56},{9,... | collective-permute-start | bytes 61448 | tf_op jit(solution)/shard_map/ppermute | solution.py:253
  35.9 0.0 collective-permute-start.8
  35.9 1.7 collective-permute-start.7
  37.7 0.0 collective-permute-done.9
  37.7 2.5 %collective-permute-done.8 = f32[40,128]{1,0:T(8,128)S(1)} collective-permute-done((f32[40,128]{1,0:T(8,128)S(1)}, f32[40,128]{1,0:T(8,128)S(1)}, u32[]{:S(2)}, u32[]{:S(2)}) %collective-permute-start.8) | collective-permute-done | bytes 20512 | tf_op jit(solution)/shard_map/ppermute | solution.py:253
  40.2 0.0 collective-permute-done.7
  40.2 1.6 collective-permute-start.10
  41.8 1.8 collective-permute-done.10
  43.6 2.6 %collective-permute-start.11 = (f32[40,128]{1,0:T(8,128)S(1)}, f32[40,128]{1,0:T(8,128)S(1)}, u32[]{:S(2)}, u32[]{:S(2)}) collective-permute-start(f32[40,128]{1,0:T(8,128)S(1)} %add.172), channel_id=1, source_target_pairs={{0,4},{1,5},{2,6},{3,7},{4,0},{5,1},{6,2},{7,3},{8,12},{9,13},{10,... | collective-permute-start | bytes 61448 | tf_op jit(solution)/shard_map/ppermute | solution.py:262
  46.2 2.1 %collective-permute-done.11 = f32[40,128]{1,0:T(8,128)S(1)} collective-permute-done((f32[40,128]{1,0:T(8,128)S(1)}, f32[40,128]{1,0:T(8,128)S(1)}, u32[]{:S(2)}, u32[]{:S(2)}) %collective-permute-start.11) | collective-permute-done | bytes 20512 | tf_op jit(solution)/shard_map/ppermute | solution.py:262
  48.3 6.2 %collective-permute-start.12 = (f32[40,128]{1,0:T(8,128)S(1)}, f32[40,128]{1,0:T(8,128)S(1)}, u32[]{:S(2)}, u32[]{:S(2)}) collective-permute-start(f32[40,128]{1,0:T(8,128)S(1)} %add.173), channel_id=1, source_target_pairs={{0,8},{1,9},{2,10},{3,11},{4,12},{5,13},{6,14},{7,15},{8,0},{9,1},... | collective-permute-start | bytes 61448 | tf_op jit(solution)/shard_map/ppermute | solution.py:262
  54.5 1.4 collective-permute-done.12
  55.9 1.8 collective-permute-start.13
  57.7 0.0 collective-permute-start.15
  57.7 1.4 collective-permute-start.14
  59.1 0.0 collective-permute-done.13
  59.1 2.8 %collective-permute-done.14 = f32[40,128]{1,0:T(8,128)S(1)} collective-permute-done((f32[40,128]{1,0:T(8,128)S(1)}, f32[40,128]{1,0:T(8,128)S(1)}, u32[]{:S(2)}, u32[]{:S(2)}) %collective-permute-start.14) | collective-permute-done | bytes 20512 | tf_op jit(solution)/shard_map/ppermute | solution.py:253
  61.8 0.0 collective-permute-done.15
  61.9 0.1 collective-permute-start.18
  62.0 3.1 %collective-permute-start.17 = (f32[160,128]{1,0:T(8,128)S(1)}, f32[160,128]{1,0:T(8,128)S(1)}, u32[]{:S(2)}, u32[]{:S(2)}) collective-permute-start(f32[160,128]{1,0:T(8,128)S(1)} %bitcast.99), channel_id=1, source_target_pairs={{0,128},{64,192},{128,0},{192,64},{1,129},{65,193},{129,1},{193,65... | collective-permute-start | bytes 245768 | tf_op jit(solution)/shard_map/ppermute | solution.py:252
  65.1 0.1 collective-permute-start.16
  65.3 3.6 %collective-permute-done.16 = f32[160,128]{1,0:T(8,128)S(1)} collective-permute-done((f32[160,128]{1,0:T(8,128)S(1)}, f32[160,128]{1,0:T(8,128)S(1)}, u32[]{:S(2)}, u32[]{:S(2)}) %collective-permute-start.16) | collective-permute-done | bytes 81952 | tf_op jit(solution)/shard_map/ppermute | solution.py:252
  68.8 0.0 collective-permute-done.17
  68.9 0.0 collective-permute-done.18
  69.0 9.4 %collective-permute-start.19 = (f32[640,128]{1,0:T(8,128)S(1)}, f32[640,128]{1,0:T(8,128)S(1)}, u32[]{:S(2)}, u32[]{:S(2)}) collective-permute-start(f32[640,128]{1,0:T(8,128)S(1)} %bitcast.97), channel_id=1, source_target_pairs={{0,1},{1,0},{2,3},{3,2},{4,5},{5,4},{6,7},{7,6},{8,9},{9,8},{10,11... | collective-permute-start | bytes 983048 | tf_op jit(solution)/shard_map/ppermute | solution.py:254
  79.0 9.2 %shard_map.82 = (bf16[72,128,128]{2,1,0:T(8,128)(2,1)}, s32[3,72]{1,0:T(4,128)}) custom-call(s32[72]{0:T(128)} %bitcast.107, s32[72]{0:T(128)} %bitcast.108, s32[72]{0:T(128)} %bitcast.109, s32[72]{0:T(128)} %bitcast.110, bf16[72,128,128]{2,1,0:T(8,128)(2,1)} %bitcast.92), custom_call_target="tpu_custom_call" | custom-call | flops 100000000 | bytes 4800000 | tf_op jit(solution)/shard_map/pallas_call | solution.py:142
  88.2 0.0 collective-permute-done.19
  88.3 0.9 pad_maximum_fusion.packed_ref
  89.2 25.3 %all-gather.2.cloned.1.call-done.panel_ref = bf16[16384,512]{1,0:T(8,128)(2,1)} async-done(((bf16[256,512]{1,0:T(8,128)(2,1)}), bf16[16384,512]{1,0:T(8,128)(2,1)}) %all-gather.2.cloned.1.call-update) | async-done | bytes 16777232 | tf_op jit(solution)/shard_map/all_gather | solution.py:272
  114.5 16.0 %shard_map.83 = f32[256,512]{1,0:T(8,128)} custom-call(s32[1]{0:T(128)} %bitcast.91.count_ref, s32[3,72]{1,0:T(4,128)} %get-tuple-element.7.place_ref, bf16[72,128,128]{2,1,0:T(8,128)(2,1)} %get-tuple-element.8.values_ref, bf16[16384,512]{1,0:T(8,128)(2,1)} %all-gather.2.cloned.1.call-done.panel_ref, bf16[8,512,512]{2,1,0:T(8,128)(2,1)} %core_ref.3), custom_call_target="tpu_custom_call" | custom-call | flops 5000000000 | bytes 24000000 | tf_op jit(solution)/shard_map/pallas_call | solution.py:200
  130.5 1.1 dynamic-slice_bitcast_fusion.1
  131.6 2.5 %collective-permute-start.2 = (f32[64,512]{1,0:T(8,128)S(1)}, f32[64,512]{1,0:T(8,128)S(1)}, u32[]{:S(2)}, u32[]{:S(2)}) collective-permute-start(f32[64,512]{1,0:T(8,128)S(1)} %get-tuple-element.13), channel_id=1, source_target_pairs={{0,192},{64,0},{128,64},{192,128},{1,193},{65,1},{129,65},{193,129... | collective-permute-start | bytes 393224 | tf_op jit(solution)/shard_map/ppermute | solution.py:278
  134.1 0.0 collective-permute-start.1
  134.1 1.9 collective-permute-start
  136.1 51.2 %shard_map.85 = f32[512,512]{1,0:T(8,128)} custom-call(f32[1280,128]{1,0:T(8,128)} %pad_maximum_fusion.packed_ref), custom_call_target="tpu_custom_call" | custom-call | flops 3000000000 | bytes 2000000 | tf_op jit(solution)/shard_map/pallas_call | solution.py:108
  187.3 0.0 collective-permute-done.2
  187.3 0.0 collective-permute-done.1
  187.3 0.0 collective-permute-done
  187.3 2.1 %bitcast_dynamic-update-slice_fusion.6 = (f32[8,64,512]{2,1,0:T(8,128)S(1)}, f32[64,512]{1,0:T(8,128)S(1)}) fusion(f32[512,512]{1,0:T(8,128)} %shard_map.85, f32[64,512]{1,0:T(8,128)S(1)} %collective-permute-done, f32[64,512]{1,0:T(8,128)S(1)} %collective-permute-done.1, f32[64,512]{1,0:T(8,128)S(1)} %collective-permute-done.2, f32[4,64,512]{2,1,0:T(8,128)} %bitcast.94, ...), kind=kOutput, calls=%fused_computation.11 | convolution fusion | flops 201424896 | bytes 1835012 | tf_op jit(solution)/shard_map/dot_general | solution.py:280
  189.3 0.9 collective-permute-start.20
  190.3 0.6 collective-permute-start.22
  190.9 1.6 collective-permute-start.21
  192.5 0.7 collective-permute-done.20
  193.3 4.2 %collective-permute-done.21 = f32[64,512]{1,0:T(8,128)S(1)} collective-permute-done((f32[64,512]{1,0:T(8,128)S(1)}, f32[64,512]{1,0:T(8,128)S(1)}, u32[]{:S(2)}, u32[]{:S(2)}) %collective-permute-start.21) | collective-permute-done | bytes 131104 | tf_op jit(solution)/shard_map/ppermute | solution.py:278
  197.5 0.0 collective-permute-done.22
  197.6 0.8 constant_dynamic-slice_fusion
  (32 shorter events, 0.3 us)
Async XLA Ops:
  6.5 108.0 %all-gather.2.cloned.1.call-start = ((), (), s32[]{:S(2)}) async-start(), calls=%async_computation | async-start | bytes 17039360 | tf_op jit(solution)/shard_map/all_gather | solution.py:272
  20.6 4.6 %collective-permute-start.3 = (f32[640,128]{1,0:T(8,128)S(1)}, f32[640,128]{1,0:T(8,128)S(1)}, u32[]{:S(2)}, u32[]{:S(2)}) collective-permute-start(f32[640,128]{1,0:T(8,128)S(1)} %dynamic-slice_bitcast_fusion), channel_id=1, source_target_pairs={{0,1},{1,0},{2,3},{3,2},{4,5},{5,4},{6,7},{7,6},{8,9},{9,8},{10,11... | collective-permute-start | bytes 983048 | tf_op jit(solution)/shard_map/ppermute | solution.py:254
  26.3 3.9 %collective-permute-start.6 = (f32[160,128]{1,0:T(8,128)S(1)}, f32[160,128]{1,0:T(8,128)S(1)}, u32[]{:S(2)}, u32[]{:S(2)}) collective-permute-start(f32[160,128]{1,0:T(8,128)S(1)} %get-tuple-element.16), channel_id=1, source_target_pairs={{0,192},{64,0},{128,64},{192,128},{1,193},{65,1},{129,65},{193,129... | collective-permute-start | bytes 245768 | tf_op jit(solution)/shard_map/ppermute | solution.py:252
  27.3 4.9 %collective-permute-start.5 = (f32[160,128]{1,0:T(8,128)S(1)}, f32[160,128]{1,0:T(8,128)S(1)}, u32[]{:S(2)}, u32[]{:S(2)}) collective-permute-start(f32[160,128]{1,0:T(8,128)S(1)} %get-tuple-element.17), channel_id=1, source_target_pairs={{0,64},{64,128},{128,192},{192,0},{1,65},{65,129},{129,193},{193,1... | collective-permute-start | bytes 245768 | tf_op jit(solution)/shard_map/ppermute | solution.py:252
  27.8 5.0 %collective-permute-start.4 = (f32[160,128]{1,0:T(8,128)S(1)}, f32[160,128]{1,0:T(8,128)S(1)}, u32[]{:S(2)}, u32[]{:S(2)}) collective-permute-start(f32[160,128]{1,0:T(8,128)S(1)} %get-tuple-element.18), channel_id=1, source_target_pairs={{0,128},{64,192},{128,0},{192,64},{1,129},{65,193},{129,1},{193,65... | collective-permute-start | bytes 245768 | tf_op jit(solution)/shard_map/ppermute | solution.py:252
  32.9 4.7 %collective-permute-start.9 = (f32[40,128]{1,0:T(8,128)S(1)}, f32[40,128]{1,0:T(8,128)S(1)}, u32[]{:S(2)}, u32[]{:S(2)}) collective-permute-start(f32[40,128]{1,0:T(8,128)S(1)} %get-tuple-element.19), channel_id=1, source_target_pairs={{0,48},{1,49},{2,50},{3,51},{4,52},{5,53},{6,54},{7,55},{8,56},{9,... | collective-permute-start | bytes 61448 | tf_op jit(solution)/shard_map/ppermute | solution.py:253
  35.9 4.2 %collective-permute-start.8 = (f32[40,128]{1,0:T(8,128)S(1)}, f32[40,128]{1,0:T(8,128)S(1)}, u32[]{:S(2)}, u32[]{:S(2)}) collective-permute-start(f32[40,128]{1,0:T(8,128)S(1)} %get-tuple-element.20), channel_id=1, source_target_pairs={{0,16},{1,17},{2,18},{3,19},{4,20},{5,21},{6,22},{7,23},{8,24},{9,... | collective-permute-start | bytes 61448 | tf_op jit(solution)/shard_map/ppermute | solution.py:253
  35.9 4.2 %collective-permute-start.7 = (f32[40,128]{1,0:T(8,128)S(1)}, f32[40,128]{1,0:T(8,128)S(1)}, u32[]{:S(2)}, u32[]{:S(2)}) collective-permute-start(f32[40,128]{1,0:T(8,128)S(1)} %get-tuple-element.21), channel_id=1, source_target_pairs={{0,32},{1,33},{2,34},{3,35},{4,36},{5,37},{6,38},{7,39},{8,40},{9,... | collective-permute-start | bytes 61448 | tf_op jit(solution)/shard_map/ppermute | solution.py:253
  40.2 3.4 %collective-permute-start.10 = (f32[40,128]{1,0:T(8,128)S(1)}, f32[40,128]{1,0:T(8,128)S(1)}, u32[]{:S(2)}, u32[]{:S(2)}) collective-permute-start(f32[40,128]{1,0:T(8,128)S(1)} %fusion.6), channel_id=1, source_target_pairs={{0,2},{1,3},{2,0},{3,1},{4,6},{5,7},{6,4},{7,5},{8,10},{9,11},{10,... | collective-permute-start | bytes 61448 | tf_op jit(solution)/shard_map/ppermute | solution.py:262
  43.6 4.7 %collective-permute-start.11 = (f32[40,128]{1,0:T(8,128)S(1)}, f32[40,128]{1,0:T(8,128)S(1)}, u32[]{:S(2)}, u32[]{:S(2)}) collective-permute-start(f32[40,128]{1,0:T(8,128)S(1)} %add.172), channel_id=1, source_target_pairs={{0,4},{1,5},{2,6},{3,7},{4,0},{5,1},{6,2},{7,3},{8,12},{9,13},{10,... | collective-permute-start | bytes 61448 | tf_op jit(solution)/shard_map/ppermute | solution.py:262
  48.3 7.6 %collective-permute-start.12 = (f32[40,128]{1,0:T(8,128)S(1)}, f32[40,128]{1,0:T(8,128)S(1)}, u32[]{:S(2)}, u32[]{:S(2)}) collective-permute-start(f32[40,128]{1,0:T(8,128)S(1)} %add.173), channel_id=1, source_target_pairs={{0,8},{1,9},{2,10},{3,11},{4,12},{5,13},{6,14},{7,15},{8,0},{9,1},... | collective-permute-start | bytes 61448 | tf_op jit(solution)/shard_map/ppermute | solution.py:262
  55.9 3.2 %collective-permute-start.13 = (f32[40,128]{1,0:T(8,128)S(1)}, f32[40,128]{1,0:T(8,128)S(1)}, u32[]{:S(2)}, u32[]{:S(2)}) collective-permute-start(f32[40,128]{1,0:T(8,128)S(1)} %get-tuple-element.10), channel_id=1, source_target_pairs={{0,48},{1,49},{2,50},{3,51},{4,52},{5,53},{6,54},{7,55},{8,56},{9,... | collective-permute-start | bytes 61448 | tf_op jit(solution)/shard_map/ppermute | solution.py:253
  57.7 4.1 %collective-permute-start.15 = (f32[40,128]{1,0:T(8,128)S(1)}, f32[40,128]{1,0:T(8,128)S(1)}, u32[]{:S(2)}, u32[]{:S(2)}) collective-permute-start(f32[40,128]{1,0:T(8,128)S(1)} %get-tuple-element.10), channel_id=1, source_target_pairs={{0,16},{1,17},{2,18},{3,19},{4,20},{5,21},{6,22},{7,23},{8,24},{9,... | collective-permute-start | bytes 61448 | tf_op jit(solution)/shard_map/ppermute | solution.py:253
  57.7 4.1 %collective-permute-start.14 = (f32[40,128]{1,0:T(8,128)S(1)}, f32[40,128]{1,0:T(8,128)S(1)}, u32[]{:S(2)}, u32[]{:S(2)}) collective-permute-start(f32[40,128]{1,0:T(8,128)S(1)} %get-tuple-element.10), channel_id=1, source_target_pairs={{0,32},{1,33},{2,34},{3,35},{4,36},{5,37},{6,38},{7,39},{8,40},{9,... | collective-permute-start | bytes 61448 | tf_op jit(solution)/shard_map/ppermute | solution.py:253
  61.9 6.9 %collective-permute-start.18 = (f32[160,128]{1,0:T(8,128)S(1)}, f32[160,128]{1,0:T(8,128)S(1)}, u32[]{:S(2)}, u32[]{:S(2)}) collective-permute-start(f32[160,128]{1,0:T(8,128)S(1)} %bitcast.98), channel_id=1, source_target_pairs={{0,64},{64,128},{128,192},{192,0},{1,65},{65,129},{129,193},{193,1... | collective-permute-start | bytes 245768 | tf_op jit(solution)/shard_map/ppermute | solution.py:252
  62.0 6.8 %collective-permute-start.17 = (f32[160,128]{1,0:T(8,128)S(1)}, f32[160,128]{1,0:T(8,128)S(1)}, u32[]{:S(2)}, u32[]{:S(2)}) collective-permute-start(f32[160,128]{1,0:T(8,128)S(1)} %bitcast.99), channel_id=1, source_target_pairs={{0,128},{64,192},{128,0},{192,64},{1,129},{65,193},{129,1},{193,65... | collective-permute-start | bytes 245768 | tf_op jit(solution)/shard_map/ppermute | solution.py:252
  65.1 3.7 %collective-permute-start.16 = (f32[160,128]{1,0:T(8,128)S(1)}, f32[160,128]{1,0:T(8,128)S(1)}, u32[]{:S(2)}, u32[]{:S(2)}) collective-permute-start(f32[160,128]{1,0:T(8,128)S(1)} %bitcast.100), channel_id=1, source_target_pairs={{0,192},{64,0},{128,64},{192,128},{1,193},{65,1},{129,65},{193,129... | collective-permute-start | bytes 245768 | tf_op jit(solution)/shard_map/ppermute | solution.py:252
  69.0 19.2 %collective-permute-start.19 = (f32[640,128]{1,0:T(8,128)S(1)}, f32[640,128]{1,0:T(8,128)S(1)}, u32[]{:S(2)}, u32[]{:S(2)}) collective-permute-start(f32[640,128]{1,0:T(8,128)S(1)} %bitcast.97), channel_id=1, source_target_pairs={{0,1},{1,0},{2,3},{3,2},{4,5},{5,4},{6,7},{7,6},{8,9},{9,8},{10,11... | collective-permute-start | bytes 983048 | tf_op jit(solution)/shard_map/ppermute | solution.py:254
  131.6 55.7 %collective-permute-start.2 = (f32[64,512]{1,0:T(8,128)S(1)}, f32[64,512]{1,0:T(8,128)S(1)}, u32[]{:S(2)}, u32[]{:S(2)}) collective-permute-start(f32[64,512]{1,0:T(8,128)S(1)} %get-tuple-element.13), channel_id=1, source_target_pairs={{0,192},{64,0},{128,64},{192,128},{1,193},{65,1},{129,65},{193,129... | collective-permute-start | bytes 393224 | tf_op jit(solution)/shard_map/ppermute | solution.py:278
  134.1 53.1 %collective-permute-start.1 = (f32[64,512]{1,0:T(8,128)S(1)}, f32[64,512]{1,0:T(8,128)S(1)}, u32[]{:S(2)}, u32[]{:S(2)}) collective-permute-start(f32[64,512]{1,0:T(8,128)S(1)} %get-tuple-element.14), channel_id=1, source_target_pairs={{0,64},{64,128},{128,192},{192,0},{1,65},{65,129},{129,193},{193,1... | collective-permute-start | bytes 393224 | tf_op jit(solution)/shard_map/ppermute | solution.py:278
  134.1 53.1 %collective-permute-start = (f32[64,512]{1,0:T(8,128)S(1)}, f32[64,512]{1,0:T(8,128)S(1)}, u32[]{:S(2)}, u32[]{:S(2)}) collective-permute-start(f32[64,512]{1,0:T(8,128)S(1)} %get-tuple-element.15), channel_id=1, source_target_pairs={{0,128},{64,192},{128,0},{192,64},{1,129},{65,193},{129,1},{193,65... | collective-permute-start | bytes 393224 | tf_op jit(solution)/shard_map/ppermute | solution.py:278
  189.3 3.9 %collective-permute-start.20 = (f32[64,512]{1,0:T(8,128)S(1)}, f32[64,512]{1,0:T(8,128)S(1)}, u32[]{:S(2)}, u32[]{:S(2)}) collective-permute-start(f32[64,512]{1,0:T(8,128)S(1)} %get-tuple-element.23), channel_id=1, source_target_pairs={{0,192},{64,0},{128,64},{192,128},{1,193},{65,1},{129,65},{193,129... | collective-permute-start | bytes 393224 | tf_op jit(solution)/shard_map/ppermute | solution.py:278
  190.3 7.2 %collective-permute-start.22 = (f32[64,512]{1,0:T(8,128)S(1)}, f32[64,512]{1,0:T(8,128)S(1)}, u32[]{:S(2)}, u32[]{:S(2)}) collective-permute-start(f32[64,512]{1,0:T(8,128)S(1)} %get-tuple-element.23), channel_id=1, source_target_pairs={{0,64},{64,128},{128,192},{192,0},{1,65},{65,129},{129,193},{193,1... | collective-permute-start | bytes 393224 | tf_op jit(solution)/shard_map/ppermute | solution.py:278
  190.9 6.6 %collective-permute-start.21 = (f32[64,512]{1,0:T(8,128)S(1)}, f32[64,512]{1,0:T(8,128)S(1)}, u32[]{:S(2)}, u32[]{:S(2)}) collective-permute-start(f32[64,512]{1,0:T(8,128)S(1)} %get-tuple-element.23), channel_id=1, source_target_pairs={{0,128},{64,192},{128,0},{192,64},{1,129},{65,193},{129,1},{193,65... | collective-permute-start | bytes 393224 | tf_op jit(solution)/shard_map/ppermute | solution.py:278
Sparse Core Ops, SparseCore 0:
  10.1 104.3 all-gather.1

commit v2 on v0

v2 whole, which is shorter than its diff:
```python
import jax
import jax.numpy as jnp
from jax import lax
from jax.experimental import pallas as pl
from jax.experimental.pallas import tpu as pltpu
from jax.sharding import PartitionSpec as P

HIGHEST = lax.Precision.HIGHEST
MIB = 1024 * 1024
RIDGE = 16.0
IN_VMEM = pl.BlockSpec(memory_space=pltpu.VMEM)
IN_SMEM = pl.BlockSpec(memory_space=pltpu.SMEM)


def product(a, b, a_dim, b_dim):
    return lax.dot_general(a, b, (((a_dim,), (b_dim,)), ((), ())), preferred_element_type=jnp.float32)


def position():
    ent = lax.axis_index("ent")
    return ent // 16, lax.axis_index("rel"), ent % 2


def system_kernel(rows_ref, core_ref, out_ref, packed_ref, d0_ref, d1_ref, low_ref, c0_ref, c1_ref):
    rows = rows_ref[...]
    for ref in (d0_ref, d1_ref, low_ref, c0_ref, c1_ref):
        ref[...] = jnp.zeros_like(ref)

    def body(step, carry):
        core = core_ref[step]
        term = jnp.concatenate([product(rows, core, 1, 1), product(rows, core, 1, 0)], axis=0)
        high = term.astype(jnp.bfloat16)
        low = (term - high.astype(jnp.float32)).astype(jnp.bfloat16)
        h0, h1 = high[:, :256], high[:, 256:]
        l0, l1 = low[:, :256], low[:, 256:]
        h0t, h1t, l1t = h0.T, h1.T, l1.T
        d0_ref[...] += product(h0t, h0, 1, 0)
        d1_ref[...] += product(h1t, h1, 1, 0)
        c0_ref[...] += product(h0t, l0, 1, 0)
        c1_ref[...] += product(h1t, l1, 1, 0)
        low_ref[...] += product(h1t, h0, 1, 0) + product(h1t, l0, 1, 0) + product(l1t, h0, 1, 0)
        return carry

    lax.fori_loop(0, core_ref.shape[0], body, 0)
    first = d0_ref[...] + (c0_ref[...] + c0_ref[...].T)
    last = d1_ref[...] + (c1_ref[...] + c1_ref[...].T)
    mixed = low_ref[...]
    blocks = (
        first[:128, :128], first[128:, :128], first[128:, 128:],
        mixed[:128, :128], mixed[:128, 128:], last[:128, :128],
        mixed[128:, :128], mixed[128:, 128:], last[128:, :128], last[128:, 128:],
    )
    for index, block in enumerate(blocks):
        packed_ref[pl.ds(index * 128, 128), :] = block
    x, y, core = position()
    for c in range(2):
        for j in range(4):
            for k in range(4):
                start = ((c + core) % 2) * 640 + ((j - y + 4) % 4) * 160 + ((k - x + 4) % 4) * 40
                out_ref[pl.ds(pl.multiple_of(start, 8), 40), :] = packed_ref[pl.ds(c * 640 + j * 160 + k * 40, 40), :]


def system_term(factor, cores):
    return pl.pallas_call(
        system_kernel,
        out_shape=jax.ShapeDtypeStruct((1280, 128), jnp.float32),
        in_specs=[IN_VMEM] * 2,
        out_specs=IN_VMEM,
        scratch_shapes=[pltpu.VMEM((1280, 128), jnp.float32)] + [pltpu.VMEM((256, 256), jnp.float32)] * 5,
        compiler_params=pltpu.CompilerParams(vmem_limit_bytes=32 * MIB),
        cost_estimate=pl.CostEstimate(flops=12000000000, bytes_accessed=5000000, transcendentals=0),
    )(factor, cores)


def invert_block(m):
    full = (8, 128)
    blocks = [m[8 * r:8 * r + 8, :] for r in range(16)]
    lanes = lax.broadcasted_iota(jnp.int32, full, 1)
    subs = lax.broadcasted_iota(jnp.int32, full, 0)
    for q in range(16):
        panel = blocks[q]
        d = {
            (i, j): jnp.broadcast_to(panel[i:i + 1, 8 * q + j:8 * q + j + 1], full)
            for i in range(8)
            for j in range(i + 1)
        }
        entry = lambda i, j: d[max(i, j), min(i, j)]
        for k in range(8):
            inverse = 1.0 / d[k, k]
            ratio = {i: entry(i, k) * inverse for i in range(8) if i != k}
            for i in range(8):
                for j in range(i + 1):
                    if i != k and j != k:
                        d[i, j] = d[i, j] - ratio[i] * entry(j, k)
            for i in ratio:
                d[max(i, k), min(i, k)] = ratio[i]
            d[k, k] = -inverse
        inside = lanes // 8 == q
        unit = [
            jnp.broadcast_to(
                jnp.where(inside, (lanes == 8 * q + j).astype(jnp.float32), panel)[j:j + 1, :], full
            )
            for j in range(8)
        ]
        scaled = []
        for i in range(8):
            row = entry(i, 0) * unit[0]
            for j in range(1, 8):
                row = row + entry(i, j) * unit[j]
            scaled.append(row)
        for r in range(16):
            if r != q:
                old = blocks[r]
                new = jnp.where(inside, 0.0, old)
                for i in range(8):
                    new = new + jnp.broadcast_to(old[:, 8 * q + i:8 * q + i + 1], full) * scaled[i]
                blocks[r] = new
        row = scaled[0]
        for i in range(1, 8):
            row = jnp.where(subs == i, scaled[i], row)
        blocks[q] = -row
    return jnp.concatenate(blocks, axis=0)


def inverse_kernel(own_ref, other_ref, out_ref, packed_ref):
    x, y, core = position()
    for i, part_ref in enumerate((own_ref, other_ref)):
        for j in range(4):
            for k in range(4):
                start = ((core + i) % 2) * 640 + ((y - j + 4) % 4) * 160 + ((x - k + 4) % 4) * 40
                packed_ref[pl.ds(pl.multiple_of(start, 8), 40), :] = part_ref[pl.ds(j * 160 + k * 40, 40), :]
    eye = lax.broadcasted_iota(jnp.int32, (128, 128), 0) == lax.broadcasted_iota(jnp.int32, (128, 128), 1)
    index = 0
    for i in range(4):
        for j in range(i + 1):
            block = packed_ref[pl.ds(index * 128, 128), :]
            if i == j:
                block = block + jnp.where(eye, RIDGE, 0.0)
            else:
                out_ref[pl.ds(j * 128, 128), pl.ds(i * 128, 128)] = block.T
            out_ref[pl.ds(i * 128, 128), pl.ds(j * 128, 128)] = block
            index += 1
    lane_block = lax.broadcasted_iota(jnp.int32, (512, 512), 1) // 128
    row_lane = lax.broadcasted_iota(jnp.int32, (128, 512), 1)
    row_sub = lax.broadcasted_iota(jnp.int32, (128, 512), 0)

    def stage(p, carry):
        start = pl.multiple_of(p * 128, 128)
        part = pl.ds(start, 128)
        column = out_ref[:, part]
        pivot = invert_block(out_ref[part, part])
        row = jnp.where(row_lane // 128 == p, (row_lane - start == row_sub).astype(jnp.float32), out_ref[part, :])
        scaled = jnp.dot(pivot, row, precision=HIGHEST, preferred_element_type=jnp.float32)
        rest = jnp.where(lane_block == p, 0.0, out_ref[...])
        out_ref[...] = rest - jnp.dot(column, scaled, precision=HIGHEST, preferred_element_type=jnp.float32)
        out_ref[part, :] = scaled
        return carry

    lax.fori_loop(0, 4, stage, 0)


def inverse(own, other):
    return pl.pallas_call(
        inverse_kernel,
        out_shape=jax.ShapeDtypeStruct((512, 512), jnp.float32),
        in_specs=[IN_VMEM] * 2,
        out_specs=IN_VMEM,
        scratch_shapes=[pltpu.VMEM((1280, 128), jnp.float32)],
        compiler_params=pltpu.CompilerParams(vmem_limit_bytes=32 * MIB),
        cost_estimate=pl.CostEstimate(flops=30000000000, bytes_accessed=2000000, transcendentals=0),
    )(own, other)


def align_kernel(rel_ref, block_ref, col_ref, flip_ref, values_ref, out_ref, place_ref, order_ref):
    def note(slot, carry):
        order_ref[col_ref[slot] // 2] = slot
        return carry

    lax.fori_loop(0, 64, note, 0)

    def move(step, carry):
        for i in range(8):
            index = step * 8 + i
            slot = jnp.where(index < 64, order_ref[jnp.minimum(index, 63)], index)
            flip = flip_ref[slot]
            place_ref[0, index] = col_ref[slot]
            place_ref[1, index] = flip * 8 + rel_ref[slot]
            place_ref[2, index] = block_ref[slot]
            tile = values_ref[slot]
            out_ref[index] = jnp.where(flip == 1, tile.T, tile)
        return carry

    lax.fori_loop(0, values_ref.shape[0] // 8, move, 0)


def align(tile_rel, tile_block, tile_col, tile_flip, values):
    slots = values.shape[0]
    return pl.pallas_call(
        align_kernel,
        out_shape=(
            jax.ShapeDtypeStruct(values.shape, values.dtype),
            jax.ShapeDtypeStruct((3, slots), jnp.int32),
        ),
        in_specs=[IN_SMEM] * 4 + [IN_VMEM],
        out_specs=(IN_VMEM, IN_SMEM),
        scratch_shapes=[pltpu.SMEM((64,), jnp.int32)],
        compiler_params=pltpu.CompilerParams(vmem_limit_bytes=16 * MIB),
        cost_estimate=pl.CostEstimate(flops=3000000000, bytes_accessed=4800000, transcendentals=0),
    )(tile_rel, tile_block, tile_col, tile_flip, values)


def rows_kernel(count_ref, place_ref, values_ref, cores_ref, panels_ref, out_ref, sums_ref, panel_ref, core_ref, sem, core_sem):
    def fetch(owner):
        start = pl.multiple_of(place_ref[0, owner] * 128, 128)
        return pltpu.make_async_copy(panels_ref.at[pl.ds(start, 128), :], panel_ref.at[owner], sem.at[owner])

    def begin(step, carry):
        for i in range(8):
            fetch(step * 8 + i).start()
        return carry

    lax.fori_loop(0, 8, begin, 0)
    core_copy = pltpu.make_async_copy(cores_ref, core_ref, core_sem)
    core_copy.start()
    sums_ref[...] = jnp.zeros_like(sums_ref)

    def add(index, owner):
        place = pl.multiple_of(place_ref[2, index] * 128, 128)
        term = product(values_ref[index], panel_ref[owner], 1, 0)
        where = (place_ref[1, index], pl.ds(place, 128), slice(None))
        sums_ref[where] = sums_ref[where] + term

    def main(step, carry):
        for i in range(8):
            fetch(step * 8 + i).wait()
        for i in range(8):
            add(step * 8 + i, step * 8 + i)
        return carry

    lax.fori_loop(0, 8, main, 0)

    def extra(index, carry):
        add(index, place_ref[0, index] // 2)
        return carry

    lax.fori_loop(64, count_ref[0], extra, 0)
    core_copy.wait()
    total = jnp.zeros(out_ref.shape, jnp.float32)
    for k in range(8):
        core = core_ref[k]
        total += product(sums_ref[k].astype(jnp.bfloat16), core, 1, 1)
        total += product(sums_ref[k + 8].astype(jnp.bfloat16), core, 1, 0)
    out_ref[...] = total.astype(out_ref.dtype)


def partial_rows(count, place, values, cores, panels):
    return pl.pallas_call(
        rows_kernel,
        out_shape=jax.ShapeDtypeStruct((256, 512), jnp.bfloat16),
        in_specs=[IN_SMEM, IN_SMEM, IN_VMEM] + [pl.BlockSpec(memory_space=pl.ANY)] * 2,
        out_specs=IN_VMEM,
        scratch_shapes=[
            pltpu.VMEM((16, 256, 512), jnp.float32),
            pltpu.VMEM((64, 128, 512), jnp.bfloat16),
            pltpu.VMEM(cores.shape, cores.dtype),
            pltpu.SemaphoreType.DMA((64,)),
            pltpu.SemaphoreType.DMA,
        ],
        compiler_params=pltpu.CompilerParams(vmem_limit_bytes=40 * MIB),
        cost_estimate=pl.CostEstimate(flops=10000000000, bytes_accessed=16000000, transcendentals=0),
    )(count, place, values, cores, panels)


def finish_kernel(own_ref, first_ref, second_ref, third_ref, inverse_ref, out_ref):
    wide = lambda ref: ref[...].astype(jnp.float32)
    rows = (wide(own_ref) + wide(second_ref)) + (wide(first_ref) + wide(third_ref))
    out_ref[...] = jnp.dot(rows, inverse_ref[...], precision=HIGHEST, preferred_element_type=jnp.float32)


def finish(own, arrived, inverted):
    return pl.pallas_call(
        finish_kernel,
        out_shape=jax.ShapeDtypeStruct(own.shape, jnp.float32),
        in_specs=[IN_VMEM] * 5,
        out_specs=IN_VMEM,
        compiler_params=pltpu.CompilerParams(vmem_limit_bytes=16 * MIB),
        cost_estimate=pl.CostEstimate(flops=1000000000, bytes_accessed=2500000, transcendentals=0),
    )(own, *arrived, inverted)


def over_y(v, d):
    return lax.ppermute(v, "rel", [(y, (y + d) % 4) for y in range(4)])


def over_x(v, d):
    return lax.ppermute(v, "ent", [(e, (e + 16 * d) % 64) for e in range(64)])


def swap_z(v, bits):
    return lax.ppermute(v, "ent", [(e, e ^ (2 * bits)) for e in range(64)])


def swap_core(v):
    return lax.ppermute(v, "ent", [(e, e ^ 1) for e in range(64)])


def scatter_sum(part, send):
    quarter = part.shape[0] // 4
    arrived = [send(part[d * quarter:(d + 1) * quarter], d) for d in (1, 2, 3)]
    return (part[:quarter] + arrived[1]) + (arrived[0] + arrived[2])


def gather(part, send):
    return jnp.concatenate([part] + [send(part, d) for d in (1, 2, 3)], axis=0)


def sum_everywhere(placed):
    part = placed[:640] + swap_core(placed[640:])
    part = scatter_sum(part, over_y)
    part = scatter_sum(part, over_x)
    part = part + swap_z(part, 1)
    arrived = [swap_z(part, bits) for bits in (2, 4, 6)]
    part = (part + arrived[1]) + (arrived[0] + arrived[2])
    part = gather(gather(part, over_x), over_y)
    return part, swap_core(part)


def local(factor, core_tensors, tile_values, tile_rel, tile_block, tile_col, tile_flip, tile_count):
    panels = lax.all_gather(factor, "ent", tiled=True)
    inverted = inverse(*sum_everywhere(system_term(factor, core_tensors)))
    values, place = align(tile_rel[0], tile_block[0], tile_col[0], tile_flip[0], tile_values[0])
    panels, inverted, values, place = lax.optimization_barrier((panels, inverted, values, place))
    rows = partial_rows(tile_count[0], place, values, core_tensors, panels)
    return finish(rows, [over_y(rows, d) for d in (1, 2, 3)], inverted)


def solution(mesh):
    in_specs = (
        P("ent", None),
        P("rel", None, None),
        P("rel", "ent", None, None),
        P("rel", "ent"),
        P("rel", "ent"),
        P("rel", "ent"),
        P("rel", "ent"),
        P("rel", "ent"),
    )
    out_specs = P("ent", None)
    return jax.shard_map(local, mesh=mesh, in_specs=in_specs, out_specs=out_specs, check_vma=False)
```

time: 787 us -> 152 us (0.19)
  waiting for transfers between devices: 467 us -> 43.6 us
  other arithmetic: 142 us -> 0.09 us
  matrix products: 69 us -> 0 us
  Pallas kernels: 0 us -> 50 us
  local copies, waits for them, and re-layouts: 54.4 us -> 5.42 us
  starting transfers between devices: 6.17 us -> 38.2 us
  blocking collectives: 22.1 us -> 0 us
    psum x3 -> x0, waiting for transfers between devices: 467 us -> none  [the longest x1 246 us: local(): lax.psum(placed, ('rel', 'ent'))]
    another operation x17 -> x0, other arithmetic: 120 us -> none  [the longest x14 78.9 us: local(): lower_factor = jnp.linalg.cholesky(system)]
    dot_general x8 -> x0, matrix products: 53.4 us -> none  [the longest x1 23.8 us: accumulate(): jnp.einsum('byvr,rex->beyvx', indicator_matrix, tile_contributions, preci...]
    pallas_call x0 -> x5, Pallas kernels: none -> 50 us  [the longest x1 27.1 us: inverse(): pl.pallas_call(inverse_kernel, out_shape=jax.ShapeDtypeStruct((512, 512),...]
    ppermute x0 -> x21, starting transfers between devices: none -> 38.2 us  [the longest x2 12 us: swap_core(): return lax.ppermute(v, 'ent', [(e, e ^ 1) for e in range(64)])]
    ppermute x0 -> x21, waiting for transfers between devices: none -> 38 us  [the longest x9 23.2 us: over_y(): return lax.ppermute(v, 'rel', [(y, (y + d) % 4) for y in range(4)])]
    all_to_all x1 -> x0, blocking collectives: 22.1 us -> none  [local(): lax.all_to_all(wanted.reshape(peer_count, 1), 'ent', split_axis=0, concat...]
    another operation x20 -> x0, matrix products: 15.6 us -> none  [the longest x14 8.03 us: local(): updated = jax.scipy.linalg.cho_solve((lower_factor, True), totals.T).T]
  transfers between devices with their start and end apart: 4 -> 22, of which waited for: 2 -> 16; matrix products, arithmetic and copies ran while one was open for 22% -> 0% of each run, Pallas kernels for 0% -> 26%
where the time goes in v2:
time: 152 us
  Pallas kernels  50 us (33%)
  waiting for transfers between devices  43.6 us (29%)
  starting transfers between devices  38.2 us (25%)
  between operations  14.2 us (9%)
  local copies, waits for them, and re-layouts  5.42 us (4%)
    pallas_call x1, Pallas kernels, inverse(): pl.pallas_call(inverse_kernel, out_shape=jax.ShapeDtypeStruct((512, 512),...  27.1 us
    ppermute x9, waiting for transfers between devices, over_y(): return lax.ppermute(v, 'rel', [(y, (y + d) % 4) for y in range(4)])  23.2 us
    ppermute x2, starting transfers between devices, swap_core(): return lax.ppermute(v, 'ent', [(e, e ^ 1) for e in range(64)])  12 us
    ppermute x4, starting transfers between devices, swap_z(): return lax.ppermute(v, 'ent', [(e, e ^ 2 * bits) for e in range(64)])  9.59 us
    pallas_call x1, Pallas kernels, system_term(): pl.pallas_call(system_kernel, out_shape=jax.ShapeDtypeStruct((1280, 128),...  9.25 us
    ppermute x9, starting transfers between devices, over_y(): return lax.ppermute(v, 'rel', [(y, (y + d) % 4) for y in range(4)])  8.6 us
    pallas_call x1, Pallas kernels, partial_rows(): pl.pallas_call(rows_kernel, out_shape=jax.ShapeDtypeStruct((256, 512), jn...  8.39 us
    ppermute x6, starting transfers between devices, over_x(): return lax.ppermute(v, 'ent', [(e, (e + 16 * d) % 64) for e in range(64)])  8.02 us
  transfers between devices with their start and end apart: 22, of which 16 were waited for; matrix products, arithmetic and copies ran while one was open for 0% of the time, Pallas kernels for 26%

profile of v2, /device:TPU:1, one launch (start us, length us, event | category | flops | bytes accessed | tf_op | source)
XLA Modules:
  0.0 151.6 jit_solution(13604886061229817228)
XLA Ops:
  6.5 0.0 all-gather.2.cloned.1.call-start
  6.5 0.7 all-gather.2.cloned.1.call-update
  7.3 0.0 copy-start
  7.3 0.9 copy-done
  8.2 0.0 copy-start.1
  8.2 2.2 %copy-done.1 = bf16[8,512,512]{2,1,0:T(8,128)(2,1)S(1)} copy-done((bf16[8,512,512]{2,1,0:T(8,128)(2,1)S(1)}, bf16[8,512,512]{2,1,0:T(8,128)(2,1)}, u32[]{:S(2)}) %copy-start.1) | copy-done | bytes 4194328
  10.4 0.0 copy-start.3
  10.4 0.0 copy-start.4
  10.4 0.0 copy-start.5
  10.4 0.0 copy-start.7
  10.4 9.3 %shard_map.82 = f32[1280,128]{1,0:T(8,128)S(1)} custom-call(bf16[256,512]{1,0:T(8,128)(2,1)S(1)} %copy-done, bf16[8,512,512]{2,1,0:T(8,128)(2,1)S(1)} %copy-done.1), custom_call_target="tpu_custom_call" | custom-call | flops 12000000000 | bytes 5000000 | tf_op jit(solution)/shard_map/pallas_call | solution.py:64
  19.7 3.3 %collective-permute-start = (f32[640,128]{1,0:T(8,128)S(1)}, f32[640,128]{1,0:T(8,128)S(1)}, u32[]{:S(2)}, u32[]{:S(2)}) collective-permute-start(f32[640,128]{1,0:T(8,128)S(1)} %slice.41), channel_id=1, source_target_pairs={{0,1},{1,0},{2,3},{3,2},{4,5},{5,4},{6,7},{7,6},{8,9},{9,8},{10,11... | collective-permute-start | bytes 983048 | tf_op jit(solution)/shard_map/ppermute | solution.py:304
  23.0 1.3 collective-permute-done
  24.4 1.1 collective-permute-start.3
  25.4 0.5 collective-permute-start.2
  25.9 1.2 collective-permute-start.1
  27.1 1.0 collective-permute-done.3
  28.1 2.0 %collective-permute-done.2 = f32[160,128]{1,0:T(8,128)S(1)} collective-permute-done((f32[160,128]{1,0:T(8,128)S(1)}, f32[160,128]{1,0:T(8,128)S(1)}, u32[]{:S(2)}, u32[]{:S(2)}) %collective-permute-start.2) | collective-permute-done | bytes 81952 | tf_op jit(solution)/shard_map/ppermute | solution.py:292
  30.1 0.9 collective-permute-done.1
  31.0 3.0 %collective-permute-start.6 = (f32[40,128]{1,0:T(8,128)S(1)}, f32[40,128]{1,0:T(8,128)S(1)}, u32[]{:S(2)}, u32[]{:S(2)}) collective-permute-start(f32[40,128]{1,0:T(8,128)S(1)} %get-tuple-element.22), channel_id=1, source_target_pairs={{0,48},{1,49},{2,50},{3,51},{4,52},{5,53},{6,54},{7,55},{8,56},{9,... | collective-permute-start | bytes 61448 | tf_op jit(solution)/shard_map/ppermute | solution.py:296
  34.0 0.0 collective-permute-start.5
  34.0 1.7 %collective-permute-start.4 = (f32[40,128]{1,0:T(8,128)S(1)}, f32[40,128]{1,0:T(8,128)S(1)}, u32[]{:S(2)}, u32[]{:S(2)}) collective-permute-start(f32[40,128]{1,0:T(8,128)S(1)} %get-tuple-element.24), channel_id=1, source_target_pairs={{0,32},{1,33},{2,34},{3,35},{4,36},{5,37},{6,38},{7,39},{8,40},{9,... | collective-permute-start | bytes 61448 | tf_op jit(solution)/shard_map/ppermute | solution.py:296
  35.7 0.0 collective-permute-done.6
  35.7 2.1 %collective-permute-done.5 = f32[40,128]{1,0:T(8,128)S(1)} collective-permute-done((f32[40,128]{1,0:T(8,128)S(1)}, f32[40,128]{1,0:T(8,128)S(1)}, u32[]{:S(2)}, u32[]{:S(2)}) %collective-permute-start.5) | collective-permute-done | bytes 20512 | tf_op jit(solution)/shard_map/ppermute | solution.py:296
  37.9 0.3 collective-permute-done.4
  38.2 1.7 %collective-permute-start.7 = (f32[40,128]{1,0:T(8,128)S(1)}, f32[40,128]{1,0:T(8,128)S(1)}, u32[]{:S(2)}, u32[]{:S(2)}) collective-permute-start(f32[40,128]{1,0:T(8,128)S(1)} %fusion.1), channel_id=1, source_target_pairs={{0,2},{1,3},{2,0},{3,1},{4,6},{5,7},{6,4},{7,5},{8,10},{9,11},{10,... | collective-permute-start | bytes 61448 | tf_op jit(solution)/shard_map/ppermute | solution.py:300
  39.9 1.6 %collective-permute-done.7 = f32[40,128]{1,0:T(8,128)S(1)} collective-permute-done((f32[40,128]{1,0:T(8,128)S(1)}, f32[40,128]{1,0:T(8,128)S(1)}, u32[]{:S(2)}, u32[]{:S(2)}) %collective-permute-start.7) | collective-permute-done | bytes 20512 | tf_op jit(solution)/shard_map/ppermute | solution.py:300
  41.5 5.7 %collective-permute-start.10 = (f32[40,128]{1,0:T(8,128)S(1)}, f32[40,128]{1,0:T(8,128)S(1)}, u32[]{:S(2)}, u32[]{:S(2)}) collective-permute-start(f32[40,128]{1,0:T(8,128)S(1)} %add.40), channel_id=1, source_target_pairs={{0,12},{1,13},{2,14},{3,15},{4,8},{5,9},{6,10},{7,11},{8,4},{9,5},... | collective-permute-start | bytes 61448 | tf_op jit(solution)/shard_map/ppermute | solution.py:300
  47.2 1.3 collective-permute-start.9
  48.5 0.8 collective-permute-start.8
  49.4 0.0 collective-permute-done.10
  49.4 1.5 collective-permute-done.9
  50.9 4.6 %collective-permute-done.8 = f32[40,128]{1,0:T(8,128)S(1)} collective-permute-done((f32[40,128]{1,0:T(8,128)S(1)}, f32[40,128]{1,0:T(8,128)S(1)}, u32[]{:S(2)}, u32[]{:S(2)}) %collective-permute-start.8) | collective-permute-done | bytes 20512 | tf_op jit(solution)/shard_map/ppermute | solution.py:300
  55.4 2.6 %collective-permute-start.13 = (f32[40,128]{1,0:T(8,128)S(1)}, f32[40,128]{1,0:T(8,128)S(1)}, u32[]{:S(2)}, u32[]{:S(2)}) collective-permute-start(f32[40,128]{1,0:T(8,128)S(1)} %get-tuple-element.18), channel_id=1, source_target_pairs={{0,48},{1,49},{2,50},{3,51},{4,52},{5,53},{6,54},{7,55},{8,56},{9,... | collective-permute-start | bytes 61448 | tf_op jit(solution)/shard_map/ppermute | solution.py:296
  58.0 0.1 collective-permute-start.12
  58.1 0.6 collective-permute-start.11
  58.7 0.2 collective-permute-done.13
  59.0 3.3 %collective-permute-done.12 = f32[40,128]{1,0:T(8,128)S(1)} collective-permute-done((f32[40,128]{1,0:T(8,128)S(1)}, f32[40,128]{1,0:T(8,128)S(1)}, u32[]{:S(2)}, u32[]{:S(2)}) %collective-permute-start.12) | collective-permute-done | bytes 20512 | tf_op jit(solution)/shard_map/ppermute | solution.py:296
  62.2 0.0 collective-permute-done.11
  62.2 1.7 %collective-permute-start.16 = (f32[160,128]{1,0:T(8,128)S(1)}, f32[160,128]{1,0:T(8,128)S(1)}, u32[]{:S(2)}, u32[]{:S(2)}) collective-permute-start(f32[160,128]{1,0:T(8,128)S(1)} %pad_maximum_fusion), channel_id=1, source_target_pairs={{0,192},{64,0},{128,64},{192,128},{1,193},{65,1},{129,65},{193,129... | collective-permute-start | bytes 245768 | tf_op jit(solution)/shard_map/ppermute | solution.py:292
  63.9 0.0 collective-permute-start.15
  63.9 0.7 collective-permute-start.14
  64.6 5.1 %collective-permute-done.14 = f32[160,128]{1,0:T(8,128)S(1)} collective-permute-done((f32[160,128]{1,0:T(8,128)S(1)}, f32[160,128]{1,0:T(8,128)S(1)}, u32[]{:S(2)}, u32[]{:S(2)}) %collective-permute-start.14) | collective-permute-done | bytes 81952 | tf_op jit(solution)/shard_map/ppermute | solution.py:292
  69.7 0.0 collective-permute-done.15
  69.7 0.0 collective-permute-done.16
  69.8 8.7 %collective-permute-start.17 = (f32[640,128]{1,0:T(8,128)S(1)}, f32[640,128]{1,0:T(8,128)S(1)}, u32[]{:S(2)}, u32[]{:S(2)}) collective-permute-start(f32[640,128]{1,0:T(8,128)S(1)} %constant_dynamic-update-slice_fusion.own_ref), channel_id=1, source_target_pairs={{0,1},{1,0},{2,3},{3,2},{4,5},{5,4},{6,7},{7,6},{8,9},{9,8},{10,11... | collective-permute-start | bytes 983048 | tf_op jit(solution)/shard_map/ppermute | solution.py:304
  79.1 0.0 copy-done.3
  79.1 0.0 copy-done.4
  79.1 0.0 copy-done.5
  79.2 0.0 copy-done.6
  79.2 0.0 copy-done.7
  79.2 3.3 %shard_map.84 = (bf16[72,128,128]{2,1,0:T(8,128)(2,1)S(1)}, s32[3,72]{1,0:T(4,128)S(1)}) custom-call(s32[72]{0:T(128)S(1)} %bitcast.8, s32[72]{0:T(128)S(1)} %bitcast.9, s32[72]{0:T(128)S(1)} %bitcast.10, s32[72]{0:T(128)S(1)} %bitcast.11, bf16[72,128,128]{2,1,0:T(8,128)(2,1)S(1)} %bitcast.7), custom_call_target="tpu_custom_call" | custom-call | flops 3000000000 | bytes 4800000 | tf_op jit(solution)/shard_map/pallas_call | solution.py:198
  82.5 0.0 collective-permute-done.17.other_ref
  82.5 27.1 %shard_map.83.inverse_ref = f32[512,512]{1,0:T(8,128)S(1)} custom-call(f32[640,128]{1,0:T(8,128)S(1)} %constant_dynamic-update-slice_fusion.own_ref, f32[640,128]{1,0:T(8,128)S(1)} %collective-permute-done.17.other_ref), custom_call_target="tpu_custom_call" | custom-call | flops 30000001024 | bytes 2000000 | tf_op jit(solution)/shard_map/pallas_call | solution.py:163
  109.6 4.9 %all-gather.2.cloned.1.call-done.panels_ref = bf16[16384,512]{1,0:T(8,128)(2,1)} async-done(((bf16[256,512]{1,0:T(8,128)(2,1)}), bf16[16384,512]{1,0:T(8,128)(2,1)}) %all-gather.2.cloned.1.call-update) | async-done | bytes 16777232 | tf_op jit(solution)/shard_map/all_gather | solution.py:329
  114.5 2.2 %copy-done.2 = bf16[8,512,512]{2,1,0:T(8,128)(2,1)S(1)} copy-done((bf16[8,512,512]{2,1,0:T(8,128)(2,1)S(1)}, bf16[8,512,512]{2,1,0:T(8,128)(2,1)}, u32[]{:S(2)}) %copy-start.2) | copy-done | bytes 4194328
  116.7 8.4 %shard_map.85.own_ref = bf16[256,512]{1,0:T(8,128)(2,1)S(1)} custom-call(s32[1]{0:T(128)} %bitcast.6.count_ref, s32[3,72]{1,0:T(4,128)S(1)} %get-tuple-element.13.place_ref, bf16[72,128,128]{2,1,0:T(8,128)(2,1)S(1)} %get-tuple-element.14.values_ref, bf16[8,512,512]{2,1,0:T(8,128)(2,1)S(1)} %copy-done.2, ...), custom_call_target="tpu_custom_call" | custom-call | flops 10000000000 | bytes 16000000 | tf_op jit(solution)/shard_map/pallas_call | solution.py:257
  125.1 2.4 %collective-permute-start.20 = (bf16[256,512]{1,0:T(8,128)(2,1)S(1)}, bf16[256,512]{1,0:T(8,128)(2,1)S(1)}, u32[]{:S(2)}, u32[]{:S(2)}) collective-permute-start(bf16[256,512]{1,0:T(8,128)(2,1)S(1)} %shard_map.85.own_ref), channel_id=1, source_target_pairs={{0,192},{64,0},{128,64},{192,128},{1,193},{65,1},{129,65},{193,129... | collective-permute-start | bytes 786440 | tf_op jit(solution)/shard_map/ppermute | solution.py:292
  127.4 0.5 collective-permute-start.19
  128.0 0.6 collective-permute-start.18
  128.6 4.7 %collective-permute-done.20.third_ref = bf16[256,512]{1,0:T(8,128)(2,1)S(1)} collective-permute-done((bf16[256,512]{1,0:T(8,128)(2,1)S(1)}, bf16[256,512]{1,0:T(8,128)(2,1)S(1)}, u32[]{:S(2)}, u32[]{:S(2)}) %collective-permute-start.20) | collective-permute-done | bytes 262176 | tf_op jit(solution)/shard_map/ppermute | solution.py:292
  133.2 3.1 %collective-permute-done.19.second_ref = bf16[256,512]{1,0:T(8,128)(2,1)S(1)} collective-permute-done((bf16[256,512]{1,0:T(8,128)(2,1)S(1)}, bf16[256,512]{1,0:T(8,128)(2,1)S(1)}, u32[]{:S(2)}, u32[]{:S(2)}) %collective-permute-start.19) | collective-permute-done | bytes 262176 | tf_op jit(solution)/shard_map/ppermute | solution.py:292
  136.3 6.5 %collective-permute-done.18.first_ref = bf16[256,512]{1,0:T(8,128)(2,1)S(1)} collective-permute-done((bf16[256,512]{1,0:T(8,128)(2,1)S(1)}, bf16[256,512]{1,0:T(8,128)(2,1)S(1)}, u32[]{:S(2)}, u32[]{:S(2)}) %collective-permute-start.18) | collective-permute-done | bytes 262176 | tf_op jit(solution)/shard_map/ppermute | solution.py:292
  142.8 1.9 %shard_map.86 = f32[256,512]{1,0:T(8,128)} custom-call(bf16[256,512]{1,0:T(8,128)(2,1)S(1)} %shard_map.85.own_ref, bf16[256,512]{1,0:T(8,128)(2,1)S(1)} %collective-permute-done.18.first_ref, bf16[256,512]{1,0:T(8,128)(2,1)S(1)} %collective-permute-done.19.second_ref, bf16[256,512]{1,0:T(8,128)(2,1)S(1)} %collective-permute-done.20.third_ref, ...), custom_call_target="tpu_custom_call" | custom-call | flops 1000000000 | bytes 2500000 | tf_op jit(solution)/shard_map/pallas_call | solution.py:281
  (17 shorter events, 0.2 us)
Async XLA Ops:
  6.5 108.0 %all-gather.2.cloned.1.call-start = ((), (), s32[]{:S(2)}) async-start(), calls=%async_computation | async-start | bytes 17039360 | tf_op jit(solution)/shard_map/all_gather | solution.py:329
  7.3 1.0 copy-start
  8.2 2.2 %copy-start.1 = (bf16[8,512,512]{2,1,0:T(8,128)(2,1)S(1)}, bf16[8,512,512]{2,1,0:T(8,128)(2,1)}, u32[]{:S(2)}) copy-start(bf16[8,512,512]{2,1,0:T(8,128)(2,1)} %cores_ref.1) | copy-start | bytes 12582916
  10.4 68.7 %copy-start.3 = (bf16[1,72,128,128]{3,2,1,0:T(8,128)(2,1)S(1)}, bf16[1,72,128,128]{3,2,1,0:T(8,128)(2,1)}, u32[]{:S(2)}) copy-start(bf16[1,72,128,128]{3,2,1,0:T(8,128)(2,1)} %param.10) | copy-start | bytes 7077892
  10.4 68.7 %copy-start.4 = (s32[1,72]{1,0:T(1,128)S(1)}, s32[1,72]{1,0:T(1,128)}, u32[]{:S(2)}) copy-start(s32[1,72]{1,0:T(1,128)} %param.11) | copy-start | bytes 868
  10.4 68.7 %copy-start.5 = (s32[1,72]{1,0:T(1,128)S(1)}, s32[1,72]{1,0:T(1,128)}, u32[]{:S(2)}) copy-start(s32[1,72]{1,0:T(1,128)} %param.12) | copy-start | bytes 868
  10.4 68.8 %copy-start.6 = (s32[1,72]{1,0:T(1,128)S(1)}, s32[1,72]{1,0:T(1,128)}, u32[]{:S(2)}) copy-start(s32[1,72]{1,0:T(1,128)} %param.13) | copy-start | bytes 868
  10.4 68.8 %copy-start.7 = (s32[1,72]{1,0:T(1,128)S(1)}, s32[1,72]{1,0:T(1,128)}, u32[]{:S(2)}) copy-start(s32[1,72]{1,0:T(1,128)} %param.14) | copy-start | bytes 868
  19.7 4.6 %collective-permute-start = (f32[640,128]{1,0:T(8,128)S(1)}, f32[640,128]{1,0:T(8,128)S(1)}, u32[]{:S(2)}, u32[]{:S(2)}) collective-permute-start(f32[640,128]{1,0:T(8,128)S(1)} %slice.41), channel_id=1, source_target_pairs={{0,1},{1,0},{2,3},{3,2},{4,5},{5,4},{6,7},{7,6},{8,9},{9,8},{10,11... | collective-permute-start | bytes 983048 | tf_op jit(solution)/shard_map/ppermute | solution.py:304
  24.4 3.7 %collective-permute-start.3 = (f32[160,128]{1,0:T(8,128)S(1)}, f32[160,128]{1,0:T(8,128)S(1)}, u32[]{:S(2)}, u32[]{:S(2)}) collective-permute-start(f32[160,128]{1,0:T(8,128)S(1)} %get-tuple-element.19), channel_id=1, source_target_pairs={{0,192},{64,0},{128,64},{192,128},{1,193},{65,1},{129,65},{193,129... | collective-permute-start | bytes 245768 | tf_op jit(solution)/shard_map/ppermute | solution.py:292
  25.4 4.7 %collective-permute-start.2 = (f32[160,128]{1,0:T(8,128)S(1)}, f32[160,128]{1,0:T(8,128)S(1)}, u32[]{:S(2)}, u32[]{:S(2)}) collective-permute-start(f32[160,128]{1,0:T(8,128)S(1)} %get-tuple-element.20), channel_id=1, source_target_pairs={{0,64},{64,128},{128,192},{192,0},{1,65},{65,129},{129,193},{193,1... | collective-permute-start | bytes 245768 | tf_op jit(solution)/shard_map/ppermute | solution.py:292
  25.9 5.1 %collective-permute-start.1 = (f32[160,128]{1,0:T(8,128)S(1)}, f32[160,128]{1,0:T(8,128)S(1)}, u32[]{:S(2)}, u32[]{:S(2)}) collective-permute-start(f32[160,128]{1,0:T(8,128)S(1)} %get-tuple-element.21), channel_id=1, source_target_pairs={{0,128},{64,192},{128,0},{192,64},{1,129},{65,193},{129,1},{193,65... | collective-permute-start | bytes 245768 | tf_op jit(solution)/shard_map/ppermute | solution.py:292
  31.0 4.7 %collective-permute-start.6 = (f32[40,128]{1,0:T(8,128)S(1)}, f32[40,128]{1,0:T(8,128)S(1)}, u32[]{:S(2)}, u32[]{:S(2)}) collective-permute-start(f32[40,128]{1,0:T(8,128)S(1)} %get-tuple-element.22), channel_id=1, source_target_pairs={{0,48},{1,49},{2,50},{3,51},{4,52},{5,53},{6,54},{7,55},{8,56},{9,... | collective-permute-start | bytes 61448 | tf_op jit(solution)/shard_map/ppermute | solution.py:296
  34.0 3.8 %collective-permute-start.5 = (f32[40,128]{1,0:T(8,128)S(1)}, f32[40,128]{1,0:T(8,128)S(1)}, u32[]{:S(2)}, u32[]{:S(2)}) collective-permute-start(f32[40,128]{1,0:T(8,128)S(1)} %get-tuple-element.23), channel_id=1, source_target_pairs={{0,16},{1,17},{2,18},{3,19},{4,20},{5,21},{6,22},{7,23},{8,24},{9,... | collective-permute-start | bytes 61448 | tf_op jit(solution)/shard_map/ppermute | solution.py:296
  34.0 4.1 %collective-permute-start.4 = (f32[40,128]{1,0:T(8,128)S(1)}, f32[40,128]{1,0:T(8,128)S(1)}, u32[]{:S(2)}, u32[]{:S(2)}) collective-permute-start(f32[40,128]{1,0:T(8,128)S(1)} %get-tuple-element.24), channel_id=1, source_target_pairs={{0,32},{1,33},{2,34},{3,35},{4,36},{5,37},{6,38},{7,39},{8,40},{9,... | collective-permute-start | bytes 61448 | tf_op jit(solution)/shard_map/ppermute | solution.py:296
  38.2 3.4 %collective-permute-start.7 = (f32[40,128]{1,0:T(8,128)S(1)}, f32[40,128]{1,0:T(8,128)S(1)}, u32[]{:S(2)}, u32[]{:S(2)}) collective-permute-start(f32[40,128]{1,0:T(8,128)S(1)} %fusion.1), channel_id=1, source_target_pairs={{0,2},{1,3},{2,0},{3,1},{4,6},{5,7},{6,4},{7,5},{8,10},{9,11},{10,... | collective-permute-start | bytes 61448 | tf_op jit(solution)/shard_map/ppermute | solution.py:300
  41.5 7.9 %collective-permute-start.10 = (f32[40,128]{1,0:T(8,128)S(1)}, f32[40,128]{1,0:T(8,128)S(1)}, u32[]{:S(2)}, u32[]{:S(2)}) collective-permute-start(f32[40,128]{1,0:T(8,128)S(1)} %add.40), channel_id=1, source_target_pairs={{0,12},{1,13},{2,14},{3,15},{4,8},{5,9},{6,10},{7,11},{8,4},{9,5},... | collective-permute-start | bytes 61448 | tf_op jit(solution)/shard_map/ppermute | solution.py:300
  47.2 3.6 %collective-permute-start.9 = (f32[40,128]{1,0:T(8,128)S(1)}, f32[40,128]{1,0:T(8,128)S(1)}, u32[]{:S(2)}, u32[]{:S(2)}) collective-permute-start(f32[40,128]{1,0:T(8,128)S(1)} %add.40), channel_id=1, source_target_pairs={{0,4},{1,5},{2,6},{3,7},{4,0},{5,1},{6,2},{7,3},{8,12},{9,13},{10,... | collective-permute-start | bytes 61448 | tf_op jit(solution)/shard_map/ppermute | solution.py:300
  48.5 6.9 %collective-permute-start.8 = (f32[40,128]{1,0:T(8,128)S(1)}, f32[40,128]{1,0:T(8,128)S(1)}, u32[]{:S(2)}, u32[]{:S(2)}) collective-permute-start(f32[40,128]{1,0:T(8,128)S(1)} %add.40), channel_id=1, source_target_pairs={{0,8},{1,9},{2,10},{3,11},{4,12},{5,13},{6,14},{7,15},{8,0},{9,1},... | collective-permute-start | bytes 61448 | tf_op jit(solution)/shard_map/ppermute | solution.py:300
  55.4 3.5 %collective-permute-start.13 = (f32[40,128]{1,0:T(8,128)S(1)}, f32[40,128]{1,0:T(8,128)S(1)}, u32[]{:S(2)}, u32[]{:S(2)}) collective-permute-start(f32[40,128]{1,0:T(8,128)S(1)} %get-tuple-element.18), channel_id=1, source_target_pairs={{0,48},{1,49},{2,50},{3,51},{4,52},{5,53},{6,54},{7,55},{8,56},{9,... | collective-permute-start | bytes 61448 | tf_op jit(solution)/shard_map/ppermute | solution.py:296
  58.0 4.2 %collective-permute-start.12 = (f32[40,128]{1,0:T(8,128)S(1)}, f32[40,128]{1,0:T(8,128)S(1)}, u32[]{:S(2)}, u32[]{:S(2)}) collective-permute-start(f32[40,128]{1,0:T(8,128)S(1)} %get-tuple-element.18), channel_id=1, source_target_pairs={{0,32},{1,33},{2,34},{3,35},{4,36},{5,37},{6,38},{7,39},{8,40},{9,... | collective-permute-start | bytes 61448 | tf_op jit(solution)/shard_map/ppermute | solution.py:296
  58.1 4.1 %collective-permute-start.11 = (f32[40,128]{1,0:T(8,128)S(1)}, f32[40,128]{1,0:T(8,128)S(1)}, u32[]{:S(2)}, u32[]{:S(2)}) collective-permute-start(f32[40,128]{1,0:T(8,128)S(1)} %get-tuple-element.18), channel_id=1, source_target_pairs={{0,16},{1,17},{2,18},{3,19},{4,20},{5,21},{6,22},{7,23},{8,24},{9,... | collective-permute-start | bytes 61448 | tf_op jit(solution)/shard_map/ppermute | solution.py:296
  62.2 7.5 %collective-permute-start.16 = (f32[160,128]{1,0:T(8,128)S(1)}, f32[160,128]{1,0:T(8,128)S(1)}, u32[]{:S(2)}, u32[]{:S(2)}) collective-permute-start(f32[160,128]{1,0:T(8,128)S(1)} %pad_maximum_fusion), channel_id=1, source_target_pairs={{0,192},{64,0},{128,64},{192,128},{1,193},{65,1},{129,65},{193,129... | collective-permute-start | bytes 245768 | tf_op jit(solution)/shard_map/ppermute | solution.py:292
  63.9 5.8 %collective-permute-start.15 = (f32[160,128]{1,0:T(8,128)S(1)}, f32[160,128]{1,0:T(8,128)S(1)}, u32[]{:S(2)}, u32[]{:S(2)}) collective-permute-start(f32[160,128]{1,0:T(8,128)S(1)} %pad_maximum_fusion), channel_id=1, source_target_pairs={{0,128},{64,192},{128,0},{192,64},{1,129},{65,193},{129,1},{193,65... | collective-permute-start | bytes 245768 | tf_op jit(solution)/shard_map/ppermute | solution.py:292
  63.9 5.8 %collective-permute-start.14 = (f32[160,128]{1,0:T(8,128)S(1)}, f32[160,128]{1,0:T(8,128)S(1)}, u32[]{:S(2)}, u32[]{:S(2)}) collective-permute-start(f32[160,128]{1,0:T(8,128)S(1)} %pad_maximum_fusion), channel_id=1, source_target_pairs={{0,64},{64,128},{128,192},{192,0},{1,65},{65,129},{129,193},{193,1... | collective-permute-start | bytes 245768 | tf_op jit(solution)/shard_map/ppermute | solution.py:292
  69.8 12.7 %collective-permute-start.17 = (f32[640,128]{1,0:T(8,128)S(1)}, f32[640,128]{1,0:T(8,128)S(1)}, u32[]{:S(2)}, u32[]{:S(2)}) collective-permute-start(f32[640,128]{1,0:T(8,128)S(1)} %constant_dynamic-update-slice_fusion.own_ref), channel_id=1, source_target_pairs={{0,1},{1,0},{2,3},{3,2},{4,5},{5,4},{6,7},{7,6},{8,9},{9,8},{10,11... | collective-permute-start | bytes 983048 | tf_op jit(solution)/shard_map/ppermute | solution.py:304
  114.5 2.2 %copy-start.2 = (bf16[8,512,512]{2,1,0:T(8,128)(2,1)S(1)}, bf16[8,512,512]{2,1,0:T(8,128)(2,1)}, u32[]{:S(2)}) copy-start(bf16[8,512,512]{2,1,0:T(8,128)(2,1)} %cores_ref.1) | copy-start | bytes 12582916
  125.1 8.2 %collective-permute-start.20 = (bf16[256,512]{1,0:T(8,128)(2,1)S(1)}, bf16[256,512]{1,0:T(8,128)(2,1)S(1)}, u32[]{:S(2)}, u32[]{:S(2)}) collective-permute-start(bf16[256,512]{1,0:T(8,128)(2,1)S(1)} %shard_map.85.own_ref), channel_id=1, source_target_pairs={{0,192},{64,0},{128,64},{192,128},{1,193},{65,1},{129,65},{193,129... | collective-permute-start | bytes 786440 | tf_op jit(solution)/shard_map/ppermute | solution.py:292
  127.4 8.9 %collective-permute-start.19 = (bf16[256,512]{1,0:T(8,128)(2,1)S(1)}, bf16[256,512]{1,0:T(8,128)(2,1)S(1)}, u32[]{:S(2)}, u32[]{:S(2)}) collective-permute-start(bf16[256,512]{1,0:T(8,128)(2,1)S(1)} %shard_map.85.own_ref), channel_id=1, source_target_pairs={{0,128},{64,192},{128,0},{192,64},{1,129},{65,193},{129,1},{193,65... | collective-permute-start | bytes 786440 | tf_op jit(solution)/shard_map/ppermute | solution.py:292
  128.0 14.8 %collective-permute-start.18 = (bf16[256,512]{1,0:T(8,128)(2,1)S(1)}, bf16[256,512]{1,0:T(8,128)(2,1)S(1)}, u32[]{:S(2)}, u32[]{:S(2)}) collective-permute-start(bf16[256,512]{1,0:T(8,128)(2,1)S(1)} %shard_map.85.own_ref), channel_id=1, source_target_pairs={{0,64},{64,128},{128,192},{192,0},{1,65},{65,129},{129,193},{193,1... | collective-permute-start | bytes 786440 | tf_op jit(solution)/shard_map/ppermute | solution.py:292
Sparse Core Ops, SparseCore 0:
  10.1 104.3 all-gather.1

commit v3 on v2

--- a/solution.py
+++ b/solution.py
@@ -202,17 +202,23 @@
             jax.ShapeDtypeStruct((3, slots), jnp.int32),
         ),
         in_specs=[IN_SMEM] * 4 + [IN_VMEM],
-        out_specs=(IN_VMEM, IN_SMEM),
+        out_specs=(pl.BlockSpec(memory_space=pltpu.VMEM), IN_SMEM),
         scratch_shapes=[pltpu.SMEM((64,), jnp.int32)],
         compiler_params=pltpu.CompilerParams(vmem_limit_bytes=16 * MIB),
         cost_estimate=pl.CostEstimate(flops=3000000000, bytes_accessed=4800000, transcendentals=0),
     )(tile_rel, tile_block, tile_col, tile_flip, values)
 
 
-def rows_kernel(count_ref, place_ref, values_ref, cores_ref, panels_ref, out_ref, sums_ref, panel_ref, core_ref, sem, core_sem):
+def rows_kernel(
+    count_ref, place_ref, tiles_ref, cores_ref, panels_ref, upper_ref, lower_ref, sums_ref, panel_ref, core_ref, values_ref,
+    sem, core_sem, values_sem
+):
     def fetch(owner):
         start = pl.multiple_of(place_ref[0, owner] * 128, 128)
         return pltpu.make_async_copy(panels_ref.at[pl.ds(start, 128), :], panel_ref.at[owner], sem.at[owner])
+
+    values_copy = pltpu.make_async_copy(tiles_ref, values_ref, values_sem)
+    values_copy.start()
 
     def begin(step, carry):
         for i in range(8):
@@ -230,6 +236,8 @@
         where = (place_ref[1, index], pl.ds(place, 128), slice(None))
         sums_ref[where] = sums_ref[where] + term
 
+    values_copy.wait()
+
     def main(step, carry):
         for i in range(8):
             fetch(step * 8 + i).wait()
@@ -245,51 +253,61 @@
 
     lax.fori_loop(64, count_ref[0], extra, 0)
     core_copy.wait()
-    total = jnp.zeros(out_ref.shape, jnp.float32)
+    total = jnp.zeros((256, 512), jnp.float32)
     for k in range(8):
         core = core_ref[k]
         total += product(sums_ref[k].astype(jnp.bfloat16), core, 1, 1)
         total += product(sums_ref[k + 8].astype(jnp.bfloat16), core, 1, 0)
-    out_ref[...] = total.astype(out_ref.dtype)
+    rounded = total.astype(jnp.bfloat16)
+    upper_ref[...] = rounded[:128]
+    lower_ref[...] = rounded[128:]
 
 
 def partial_rows(count, place, values, cores, panels):
     return pl.pallas_call(
         rows_kernel,
-        out_shape=jax.ShapeDtypeStruct((256, 512), jnp.bfloat16),
-        in_specs=[IN_SMEM, IN_SMEM, IN_VMEM] + [pl.BlockSpec(memory_space=pl.ANY)] * 2,
-        out_specs=IN_VMEM,
+        out_shape=(jax.ShapeDtypeStruct((128, 512), jnp.bfloat16),) * 2,
+        in_specs=[IN_SMEM, IN_SMEM] + [pl.BlockSpec(memory_space=pltpu.HBM)] * 3,
+        out_specs=(IN_VMEM,) * 2,
         scratch_shapes=[
             pltpu.VMEM((16, 256, 512), jnp.float32),
             pltpu.VMEM((64, 128, 512), jnp.bfloat16),
             pltpu.VMEM(cores.shape, cores.dtype),
+            pltpu.VMEM(values.shape, values.dtype),
             pltpu.SemaphoreType.DMA((64,)),
             pltpu.SemaphoreType.DMA,
+            pltpu.SemaphoreType.DMA,
         ],
-        compiler_params=pltpu.CompilerParams(vmem_limit_bytes=40 * MIB),
+        compiler_params=pltpu.CompilerParams(vmem_limit_bytes=60 * MIB),
         cost_estimate=pl.CostEstimate(flops=10000000000, bytes_accessed=16000000, transcendentals=0),
     )(count, place, values, cores, panels)
 
 
-def finish_kernel(own_ref, first_ref, second_ref, third_ref, inverse_ref, out_ref):
+def finish_kernel(upper_ref, upper_other_ref, lower_ref, lower_other_ref, inverse_ref, out_ref):
     wide = lambda ref: ref[...].astype(jnp.float32)
-    rows = (wide(own_ref) + wide(second_ref)) + (wide(first_ref) + wide(third_ref))
+    upper = wide(upper_ref) + wide(upper_other_ref)
+    lower = wide(lower_ref) + wide(lower_other_ref)
+    rows = jnp.concatenate([upper, lower], axis=0)
     out_ref[...] = jnp.dot(rows, inverse_ref[...], precision=HIGHEST, preferred_element_type=jnp.float32)
 
 
-def finish(own, arrived, inverted):
+def finish(upper, upper_other, lower, lower_other, inverted):
     return pl.pallas_call(
         finish_kernel,
-        out_shape=jax.ShapeDtypeStruct(own.shape, jnp.float32),
+        out_shape=jax.ShapeDtypeStruct((256, 512), jnp.float32),
         in_specs=[IN_VMEM] * 5,
         out_specs=IN_VMEM,
         compiler_params=pltpu.CompilerParams(vmem_limit_bytes=16 * MIB),
         cost_estimate=pl.CostEstimate(flops=1000000000, bytes_accessed=2500000, transcendentals=0),
-    )(own, *arrived, inverted)
+    )(upper, upper_other, lower, lower_other, inverted)
 
 
 def over_y(v, d):
     return lax.ppermute(v, "rel", [(y, (y + d) % 4) for y in range(4)])
+
+
+def swap_y(v, bits):
+    return lax.ppermute(v, "rel", [(y, y ^ bits) for y in range(4)])
 
 
 def over_x(v, d):
@@ -330,8 +348,10 @@
     inverted = inverse(*sum_everywhere(system_term(factor, core_tensors)))
     values, place = align(tile_rel[0], tile_block[0], tile_col[0], tile_flip[0], tile_values[0])
     panels, inverted, values, place = lax.optimization_barrier((panels, inverted, values, place))
-    rows = partial_rows(tile_count[0], place, values, core_tensors, panels)
-    return finish(rows, [over_y(rows, d) for d in (1, 2, 3)], inverted)
+    upper, lower = partial_rows(tile_count[0], place, values, core_tensors, panels)
+    add = lambda a, b: (a.astype(jnp.float32) + b.astype(jnp.float32)).astype(jnp.bfloat16)
+    upper, lower = add(upper, swap_y(upper, 1)), add(lower, swap_y(lower, 3))
+    return finish(upper, swap_y(upper, 3), lower, swap_y(lower, 1), inverted)
 
 
 def solution(mesh):

time: 152 us -> 147 us (0.967)
  waiting for transfers between devices: 43.6 us -> 32.5 us
  starting transfers between devices: 38.2 us -> 41.6 us
  other arithmetic: 0.09 us -> 1.97 us
    ppermute x9 -> x6, waiting for transfers between devices: 23.2 us -> 8.97 us  [over_y(): return lax.ppermute(v, 'rel', [(y, (y + d) % 4) for y in range(4)])]
    ppermute x0 -> x4, starting transfers between devices: none -> 6.83 us  [swap_y(): return lax.ppermute(v, 'rel', [(y, y ^ bits) for y in range(4)])]
    ppermute x0 -> x4, waiting for transfers between devices: none -> 5.14 us  [swap_y(): return lax.ppermute(v, 'rel', [(y, y ^ bits) for y in range(4)])]
    ppermute x9 -> x6, starting transfers between devices: 8.6 us -> 5.1 us  [over_y(): return lax.ppermute(v, 'rel', [(y, (y + d) % 4) for y in range(4)])]
    all_gather x1, waiting for transfers between devices: 4.87 us -> 2.88 us  [local(): panels = lax.all_gather(factor, 'ent', tiled=True)]
    convert_element_type x0 -> x2, other arithmetic: none -> 1.87 us  [local(): (a.astype(jnp.float32) + b.astype(jnp.float32)).astype(jnp.bfloat16)]
    unnamed x21 -> x23, local copies, waits for them, and re-layouts: 5.36 us -> 5.17 us
  transfers between devices with their start and end apart: 22 -> 23, of which waited for: 16 -> 16; matrix products, arithmetic and copies ran while one was open for 0% -> 1% of each run, Pallas kernels for 26% -> 27%
where the time goes in v3:
time: 147 us
  Pallas kernels  51.5 us (35%)
  starting transfers between devices  41.6 us (28%)
  waiting for transfers between devices  32.5 us (22%)
  between operations  14.2 us (10%)
  local copies, waits for them, and re-layouts  5.23 us (4%)
  other arithmetic  1.97 us (1%)
    pallas_call x1, Pallas kernels, inverse(): pl.pallas_call(inverse_kernel, out_shape=jax.ShapeDtypeStruct((512, 512),...  27.1 us
    ppermute x2, starting transfers between devices, swap_core(): return lax.ppermute(v, 'ent', [(e, e ^ 1) for e in range(64)])  12 us
    pallas_call x1, Pallas kernels, partial_rows(): pl.pallas_call(rows_kernel, out_shape=(jax.ShapeDtypeStruct((128, 512), j...  9.96 us
    ppermute x4, starting transfers between devices, swap_z(): return lax.ppermute(v, 'ent', [(e, e ^ 2 * bits) for e in range(64)])  9.59 us
    pallas_call x1, Pallas kernels, system_term(): pl.pallas_call(system_kernel, out_shape=jax.ShapeDtypeStruct((1280, 128),...  9.25 us
    ppermute x6, waiting for transfers between devices, over_y(): return lax.ppermute(v, 'rel', [(y, (y + d) % 4) for y in range(4)])  8.97 us
    ppermute x6, starting transfers between devices, over_x(): return lax.ppermute(v, 'ent', [(e, (e + 16 * d) % 64) for e in range(64)])  8.02 us
    ppermute x4, waiting for transfers between devices, swap_z(): return lax.ppermute(v, 'ent', [(e, e ^ 2 * bits) for e in range(64)])  7.66 us
  transfers between devices with their start and end apart: 23, of which 16 were waited for; matrix products, arithmetic and copies ran while one was open for 1% of the time, Pallas kernels for 27%

profile of v3, /device:TPU:1, one launch (start us, length us, event | category | flops | bytes accessed | tf_op | source)
XLA Modules:
  0.0 147.0 jit_solution(13060797212937035438)
XLA Ops:
  6.5 0.0 all-gather.2.cloned.1.call-start
  6.5 0.7 all-gather.2.cloned.1.call-update
  7.3 0.0 copy-start
  7.3 0.9 copy-done
  8.2 2.2 %copy-done.1 = bf16[8,512,512]{2,1,0:T(8,128)(2,1)S(1)} copy-done((bf16[8,512,512]{2,1,0:T(8,128)(2,1)S(1)}, bf16[8,512,512]{2,1,0:T(8,128)(2,1)}, u32[]{:S(2)}) %copy-start.1) | copy-done | bytes 4194328
  10.4 0.0 copy-start.6
  10.4 9.3 %shard_map.82 = f32[1280,128]{1,0:T(8,128)S(1)} custom-call(bf16[256,512]{1,0:T(8,128)(2,1)S(1)} %copy-done, bf16[8,512,512]{2,1,0:T(8,128)(2,1)S(1)} %copy-done.1), custom_call_target="tpu_custom_call" | custom-call | flops 12000000000 | bytes 5000000 | tf_op jit(solution)/shard_map/pallas_call | solution.py:64
  19.7 3.3 %collective-permute-start = (f32[640,128]{1,0:T(8,128)S(1)}, f32[640,128]{1,0:T(8,128)S(1)}, u32[]{:S(2)}, u32[]{:S(2)}) collective-permute-start(f32[640,128]{1,0:T(8,128)S(1)} %slice.41), channel_id=1, source_target_pairs={{0,1},{1,0},{2,3},{3,2},{4,5},{5,4},{6,7},{7,6},{8,9},{9,8},{10,11... | collective-permute-start | bytes 983048 | tf_op jit(solution)/shard_map/ppermute | solution.py:322
  23.0 1.3 collective-permute-done
  24.4 1.1 collective-permute-start.3
  25.4 0.5 collective-permute-start.2
  25.9 1.2 collective-permute-start.1
  27.1 1.0 collective-permute-done.3
  28.1 2.0 %collective-permute-done.2 = f32[160,128]{1,0:T(8,128)S(1)} collective-permute-done((f32[160,128]{1,0:T(8,128)S(1)}, f32[160,128]{1,0:T(8,128)S(1)}, u32[]{:S(2)}, u32[]{:S(2)}) %collective-permute-start.2) | collective-permute-done | bytes 81952 | tf_op jit(solution)/shard_map/ppermute | solution.py:306
  30.1 0.9 collective-permute-done.1
  31.0 3.0 %collective-permute-start.6 = (f32[40,128]{1,0:T(8,128)S(1)}, f32[40,128]{1,0:T(8,128)S(1)}, u32[]{:S(2)}, u32[]{:S(2)}) collective-permute-start(f32[40,128]{1,0:T(8,128)S(1)} %get-tuple-element.26), channel_id=1, source_target_pairs={{0,48},{1,49},{2,50},{3,51},{4,52},{5,53},{6,54},{7,55},{8,56},{9,... | collective-permute-start | bytes 61448 | tf_op jit(solution)/shard_map/ppermute | solution.py:314
  34.0 0.0 collective-permute-start.5
  34.0 1.7 %collective-permute-start.4 = (f32[40,128]{1,0:T(8,128)S(1)}, f32[40,128]{1,0:T(8,128)S(1)}, u32[]{:S(2)}, u32[]{:S(2)}) collective-permute-start(f32[40,128]{1,0:T(8,128)S(1)} %get-tuple-element.28), channel_id=1, source_target_pairs={{0,32},{1,33},{2,34},{3,35},{4,36},{5,37},{6,38},{7,39},{8,40},{9,... | collective-permute-start | bytes 61448 | tf_op jit(solution)/shard_map/ppermute | solution.py:314
  35.7 0.0 collective-permute-done.6
  35.7 2.1 %collective-permute-done.5 = f32[40,128]{1,0:T(8,128)S(1)} collective-permute-done((f32[40,128]{1,0:T(8,128)S(1)}, f32[40,128]{1,0:T(8,128)S(1)}, u32[]{:S(2)}, u32[]{:S(2)}) %collective-permute-start.5) | collective-permute-done | bytes 20512 | tf_op jit(solution)/shard_map/ppermute | solution.py:314
  37.9 0.3 collective-permute-done.4
  38.2 1.7 %collective-permute-start.7 = (f32[40,128]{1,0:T(8,128)S(1)}, f32[40,128]{1,0:T(8,128)S(1)}, u32[]{:S(2)}, u32[]{:S(2)}) collective-permute-start(f32[40,128]{1,0:T(8,128)S(1)} %fusion.1), channel_id=1, source_target_pairs={{0,2},{1,3},{2,0},{3,1},{4,6},{5,7},{6,4},{7,5},{8,10},{9,11},{10,... | collective-permute-start | bytes 61448 | tf_op jit(solution)/shard_map/ppermute | solution.py:318
  39.9 1.6 %collective-permute-done.7 = f32[40,128]{1,0:T(8,128)S(1)} collective-permute-done((f32[40,128]{1,0:T(8,128)S(1)}, f32[40,128]{1,0:T(8,128)S(1)}, u32[]{:S(2)}, u32[]{:S(2)}) %collective-permute-start.7) | collective-permute-done | bytes 20512 | tf_op jit(solution)/shard_map/ppermute | solution.py:318
  41.5 5.7 %collective-permute-start.10 = (f32[40,128]{1,0:T(8,128)S(1)}, f32[40,128]{1,0:T(8,128)S(1)}, u32[]{:S(2)}, u32[]{:S(2)}) collective-permute-start(f32[40,128]{1,0:T(8,128)S(1)} %add.46), channel_id=1, source_target_pairs={{0,12},{1,13},{2,14},{3,15},{4,8},{5,9},{6,10},{7,11},{8,4},{9,5},... | collective-permute-start | bytes 61448 | tf_op jit(solution)/shard_map/ppermute | solution.py:318
  47.2 1.3 collective-permute-start.9
  48.5 0.8 collective-permute-start.8
  49.4 0.0 collective-permute-done.10
  49.4 1.5 collective-permute-done.9
  50.9 4.6 %collective-permute-done.8 = f32[40,128]{1,0:T(8,128)S(1)} collective-permute-done((f32[40,128]{1,0:T(8,128)S(1)}, f32[40,128]{1,0:T(8,128)S(1)}, u32[]{:S(2)}, u32[]{:S(2)}) %collective-permute-start.8) | collective-permute-done | bytes 20512 | tf_op jit(solution)/shard_map/ppermute | solution.py:318
  55.4 2.6 %collective-permute-start.13 = (f32[40,128]{1,0:T(8,128)S(1)}, f32[40,128]{1,0:T(8,128)S(1)}, u32[]{:S(2)}, u32[]{:S(2)}) collective-permute-start(f32[40,128]{1,0:T(8,128)S(1)} %get-tuple-element.22), channel_id=1, source_target_pairs={{0,48},{1,49},{2,50},{3,51},{4,52},{5,53},{6,54},{7,55},{8,56},{9,... | collective-permute-start | bytes 61448 | tf_op jit(solution)/shard_map/ppermute | solution.py:314
  58.0 0.1 collective-permute-start.12
  58.1 0.6 collective-permute-start.11
  58.7 0.2 collective-permute-done.13
  59.0 3.3 %collective-permute-done.12 = f32[40,128]{1,0:T(8,128)S(1)} collective-permute-done((f32[40,128]{1,0:T(8,128)S(1)}, f32[40,128]{1,0:T(8,128)S(1)}, u32[]{:S(2)}, u32[]{:S(2)}) %collective-permute-start.12) | collective-permute-done | bytes 20512 | tf_op jit(solution)/shard_map/ppermute | solution.py:314
  62.2 0.0 collective-permute-done.11
  62.2 1.7 %collective-permute-start.16 = (f32[160,128]{1,0:T(8,128)S(1)}, f32[160,128]{1,0:T(8,128)S(1)}, u32[]{:S(2)}, u32[]{:S(2)}) collective-permute-start(f32[160,128]{1,0:T(8,128)S(1)} %pad_maximum_fusion), channel_id=1, source_target_pairs={{0,192},{64,0},{128,64},{192,128},{1,193},{65,1},{129,65},{193,129... | collective-permute-start | bytes 245768 | tf_op jit(solution)/shard_map/ppermute | solution.py:306
  63.9 0.0 collective-permute-start.15
  63.9 0.7 collective-permute-start.14
  64.6 5.1 %collective-permute-done.14 = f32[160,128]{1,0:T(8,128)S(1)} collective-permute-done((f32[160,128]{1,0:T(8,128)S(1)}, f32[160,128]{1,0:T(8,128)S(1)}, u32[]{:S(2)}, u32[]{:S(2)}) %collective-permute-start.14) | collective-permute-done | bytes 81952 | tf_op jit(solution)/shard_map/ppermute | solution.py:306
  69.7 0.0 collective-permute-done.15
  69.7 0.0 collective-permute-done.16
  69.8 8.7 %collective-permute-start.17 = (f32[640,128]{1,0:T(8,128)S(1)}, f32[640,128]{1,0:T(8,128)S(1)}, u32[]{:S(2)}, u32[]{:S(2)}) collective-permute-start(f32[640,128]{1,0:T(8,128)S(1)} %constant_dynamic-update-slice_fusion.own_ref), channel_id=1, source_target_pairs={{0,1},{1,0},{2,3},{3,2},{4,5},{5,4},{6,7},{7,6},{8,9},{9,8},{10,11... | collective-permute-start | bytes 983048 | tf_op jit(solution)/shard_map/ppermute | solution.py:322
  79.1 0.0 copy-done.2
  79.1 0.0 copy-done.3
  79.1 0.0 copy-done.4
  79.2 0.0 copy-done.5
  79.2 3.3 %shard_map.84 = (bf16[72,128,128]{2,1,0:T(8,128)(2,1)S(1)}, s32[3,72]{1,0:T(4,128)S(1)}) custom-call(s32[72]{0:T(128)S(1)} %bitcast.8, s32[72]{0:T(128)S(1)} %bitcast.9, s32[72]{0:T(128)S(1)} %bitcast.10, s32[72]{0:T(128)S(1)} %bitcast.11, bf16[72,128,128]{2,1,0:T(8,128)(2,1)S(1)} %bitcast.7), custom_call_target="tpu_custom_call" | custom-call | flops 3000000000 | bytes 4800000 | tf_op jit(solution)/shard_map/pallas_call | solution.py:198
  82.5 1.4 copy-done.7
  83.9 0.6 copy-done.8
  84.5 0.0 collective-permute-done.17.other_ref
  84.5 27.1 %shard_map.83.inverse_ref = f32[512,512]{1,0:T(8,128)S(1)} custom-call(f32[640,128]{1,0:T(8,128)S(1)} %constant_dynamic-update-slice_fusion.own_ref, f32[640,128]{1,0:T(8,128)S(1)} %collective-permute-done.17.other_ref), custom_call_target="tpu_custom_call" | custom-call | flops 30000001024 | bytes 2000000 | tf_op jit(solution)/shard_map/pallas_call | solution.py:163
  111.6 2.9 %all-gather.2.cloned.1.call-done.panels_ref = bf16[16384,512]{1,0:T(8,128)(2,1)} async-done(((bf16[256,512]{1,0:T(8,128)(2,1)}), bf16[16384,512]{1,0:T(8,128)(2,1)}) %all-gather.2.cloned.1.call-update) | async-done | bytes 16777232 | tf_op jit(solution)/shard_map/all_gather | solution.py:347
  114.5 10.0 %shard_map.85 = (bf16[128,512]{1,0:T(8,128)(2,1)}, bf16[128,512]{1,0:T(8,128)(2,1)}) custom-call(s32[1]{0:T(128)} %bitcast.6.count_ref, s32[3,72]{1,0:T(4,128)} %copy-done.8, bf16[72,128,128]{2,1,0:T(8,128)(2,1)} %copy-done.7, bf16[8,512,512]{2,1,0:T(8,128)(2,1)} %cores_ref.1, bf16[16384,512]{1,0:T(8,128)(2,1)} %all-gather.2.cloned.1.call-done.panels_ref), custom_call_target="tpu_custom_call" | custom-call | flops 10000000000 | bytes 16000000 | tf_op jit(solution)/shard_map/pallas_call | solution.py:267
  124.5 1.0 collective-permute-start.18
  125.4 1.8 %collective-permute-start.20 = (bf16[128,512]{1,0:T(8,128)(2,1)}, bf16[128,512]{1,0:T(8,128)(2,1)S(1)}, u32[]{:S(2)}, u32[]{:S(2)}) collective-permute-start(bf16[128,512]{1,0:T(8,128)(2,1)} %get-tuple-element.19), channel_id=1, source_target_pairs={{0,192},{64,128},{128,64},{192,0},{1,193},{65,129},{129,65},{193,1... | collective-permute-start | bytes 393224 | tf_op jit(solution)/shard_map/ppermute | solution.py:310
  127.3 1.3 collective-permute-done.18
  128.6 0.9 add_convert_fusion.1.upper_ref
  129.5 4.0 %collective-permute-start.19 = (bf16[128,512]{1,0:T(8,128)(2,1)S(1)}, bf16[128,512]{1,0:T(8,128)(2,1)S(1)}, u32[]{:S(2)}, u32[]{:S(2)}) collective-permute-start(bf16[128,512]{1,0:T(8,128)(2,1)S(1)} %add_convert_fusion.1.upper_ref), channel_id=1, source_target_pairs={{0,192},{64,128},{128,64},{192,0},{1,193},{65,129},{129,65},{193,1... | collective-permute-start | bytes 393224 | tf_op jit(solution)/shard_map/ppermute | solution.py:310
  133.5 0.0 collective-permute-done.20
  133.5 0.9 add_convert_fusion.lower_ref
  134.4 0.1 collective-permute-start.21
  134.5 1.3 collective-permute-done.19.upper_other_ref
  135.8 2.5 %collective-permute-done.21.lower_other_ref = bf16[128,512]{1,0:T(8,128)(2,1)S(1)} collective-permute-done((bf16[128,512]{1,0:T(8,128)(2,1)S(1)}, bf16[128,512]{1,0:T(8,128)(2,1)S(1)}, u32[]{:S(2)}, u32[]{:S(2)}) %collective-permute-start.21) | collective-permute-done | bytes 131104 | tf_op jit(solution)/shard_map/ppermute | solution.py:310
  138.3 1.9 %shard_map.86 = f32[256,512]{1,0:T(8,128)} custom-call(bf16[128,512]{1,0:T(8,128)(2,1)S(1)} %add_convert_fusion.1.upper_ref, bf16[128,512]{1,0:T(8,128)(2,1)S(1)} %collective-permute-done.19.upper_other_ref, bf16[128,512]{1,0:T(8,128)(2,1)S(1)} %add_convert_fusion.lower_ref, bf16[128,512]{1,0:T(8,128)(2,1)S(1)} %collective-permute-done.21.lower_other_ref, ...), custom_call_target="tpu_custom_call" | custom-call | flops 1000000000 | bytes 2500000 | tf_op jit(solution)/shard_map/pallas_call | solution.py:295
  (23 shorter events, 0.2 us)
Async XLA Ops:
  6.5 108.0 %all-gather.2.cloned.1.call-start = ((), (), s32[]{:S(2)}) async-start(), calls=%async_computation | async-start | bytes 17039360 | tf_op jit(solution)/shard_map/all_gather | solution.py:347
  7.3 1.0 copy-start
  8.2 2.2 %copy-start.1 = (bf16[8,512,512]{2,1,0:T(8,128)(2,1)S(1)}, bf16[8,512,512]{2,1,0:T(8,128)(2,1)}, u32[]{:S(2)}) copy-start(bf16[8,512,512]{2,1,0:T(8,128)(2,1)} %cores_ref.1) | copy-start | bytes 12582916
  10.4 68.7 %copy-start.2 = (bf16[1,72,128,128]{3,2,1,0:T(8,128)(2,1)S(1)}, bf16[1,72,128,128]{3,2,1,0:T(8,128)(2,1)}, u32[]{:S(2)}) copy-start(bf16[1,72,128,128]{3,2,1,0:T(8,128)(2,1)} %param.10) | copy-start | bytes 7077892
  10.4 68.7 %copy-start.3 = (s32[1,72]{1,0:T(1,128)S(1)}, s32[1,72]{1,0:T(1,128)}, u32[]{:S(2)}) copy-start(s32[1,72]{1,0:T(1,128)} %param.11) | copy-start | bytes 868
  10.4 68.7 %copy-start.4 = (s32[1,72]{1,0:T(1,128)S(1)}, s32[1,72]{1,0:T(1,128)}, u32[]{:S(2)}) copy-start(s32[1,72]{1,0:T(1,128)} %param.12) | copy-start | bytes 868
  10.4 68.8 %copy-start.5 = (s32[1,72]{1,0:T(1,128)S(1)}, s32[1,72]{1,0:T(1,128)}, u32[]{:S(2)}) copy-start(s32[1,72]{1,0:T(1,128)} %param.13) | copy-start | bytes 868
  10.4 68.8 %copy-start.6 = (s32[1,72]{1,0:T(1,128)S(1)}, s32[1,72]{1,0:T(1,128)}, u32[]{:S(2)}) copy-start(s32[1,72]{1,0:T(1,128)} %param.14) | copy-start | bytes 868
  19.7 4.6 %collective-permute-start = (f32[640,128]{1,0:T(8,128)S(1)}, f32[640,128]{1,0:T(8,128)S(1)}, u32[]{:S(2)}, u32[]{:S(2)}) collective-permute-start(f32[640,128]{1,0:T(8,128)S(1)} %slice.41), channel_id=1, source_target_pairs={{0,1},{1,0},{2,3},{3,2},{4,5},{5,4},{6,7},{7,6},{8,9},{9,8},{10,11... | collective-permute-start | bytes 983048 | tf_op jit(solution)/shard_map/ppermute | solution.py:322
  24.4 3.7 %collective-permute-start.3 = (f32[160,128]{1,0:T(8,128)S(1)}, f32[160,128]{1,0:T(8,128)S(1)}, u32[]{:S(2)}, u32[]{:S(2)}) collective-permute-start(f32[160,128]{1,0:T(8,128)S(1)} %get-tuple-element.23), channel_id=1, source_target_pairs={{0,192},{64,0},{128,64},{192,128},{1,193},{65,1},{129,65},{193,129... | collective-permute-start | bytes 245768 | tf_op jit(solution)/shard_map/ppermute | solution.py:306
  25.4 4.7 %collective-permute-start.2 = (f32[160,128]{1,0:T(8,128)S(1)}, f32[160,128]{1,0:T(8,128)S(1)}, u32[]{:S(2)}, u32[]{:S(2)}) collective-permute-start(f32[160,128]{1,0:T(8,128)S(1)} %get-tuple-element.24), channel_id=1, source_target_pairs={{0,64},{64,128},{128,192},{192,0},{1,65},{65,129},{129,193},{193,1... | collective-permute-start | bytes 245768 | tf_op jit(solution)/shard_map/ppermute | solution.py:306
  25.9 5.1 %collective-permute-start.1 = (f32[160,128]{1,0:T(8,128)S(1)}, f32[160,128]{1,0:T(8,128)S(1)}, u32[]{:S(2)}, u32[]{:S(2)}) collective-permute-start(f32[160,128]{1,0:T(8,128)S(1)} %get-tuple-element.25), channel_id=1, source_target_pairs={{0,128},{64,192},{128,0},{192,64},{1,129},{65,193},{129,1},{193,65... | collective-permute-start | bytes 245768 | tf_op jit(solution)/shard_map/ppermute | solution.py:306
  31.0 4.7 %collective-permute-start.6 = (f32[40,128]{1,0:T(8,128)S(1)}, f32[40,128]{1,0:T(8,128)S(1)}, u32[]{:S(2)}, u32[]{:S(2)}) collective-permute-start(f32[40,128]{1,0:T(8,128)S(1)} %get-tuple-element.26), channel_id=1, source_target_pairs={{0,48},{1,49},{2,50},{3,51},{4,52},{5,53},{6,54},{7,55},{8,56},{9,... | collective-permute-start | bytes 61448 | tf_op jit(solution)/shard_map/ppermute | solution.py:314
  34.0 3.8 %collective-permute-start.5 = (f32[40,128]{1,0:T(8,128)S(1)}, f32[40,128]{1,0:T(8,128)S(1)}, u32[]{:S(2)}, u32[]{:S(2)}) collective-permute-start(f32[40,128]{1,0:T(8,128)S(1)} %get-tuple-element.27), channel_id=1, source_target_pairs={{0,16},{1,17},{2,18},{3,19},{4,20},{5,21},{6,22},{7,23},{8,24},{9,... | collective-permute-start | bytes 61448 | tf_op jit(solution)/shard_map/ppermute | solution.py:314
  34.0 4.1 %collective-permute-start.4 = (f32[40,128]{1,0:T(8,128)S(1)}, f32[40,128]{1,0:T(8,128)S(1)}, u32[]{:S(2)}, u32[]{:S(2)}) collective-permute-start(f32[40,128]{1,0:T(8,128)S(1)} %get-tuple-element.28), channel_id=1, source_target_pairs={{0,32},{1,33},{2,34},{3,35},{4,36},{5,37},{6,38},{7,39},{8,40},{9,... | collective-permute-start | bytes 61448 | tf_op jit(solution)/shard_map/ppermute | solution.py:314
  38.2 3.4 %collective-permute-start.7 = (f32[40,128]{1,0:T(8,128)S(1)}, f32[40,128]{1,0:T(8,128)S(1)}, u32[]{:S(2)}, u32[]{:S(2)}) collective-permute-start(f32[40,128]{1,0:T(8,128)S(1)} %fusion.1), channel_id=1, source_target_pairs={{0,2},{1,3},{2,0},{3,1},{4,6},{5,7},{6,4},{7,5},{8,10},{9,11},{10,... | collective-permute-start | bytes 61448 | tf_op jit(solution)/shard_map/ppermute | solution.py:318
  41.5 7.9 %collective-permute-start.10 = (f32[40,128]{1,0:T(8,128)S(1)}, f32[40,128]{1,0:T(8,128)S(1)}, u32[]{:S(2)}, u32[]{:S(2)}) collective-permute-start(f32[40,128]{1,0:T(8,128)S(1)} %add.46), channel_id=1, source_target_pairs={{0,12},{1,13},{2,14},{3,15},{4,8},{5,9},{6,10},{7,11},{8,4},{9,5},... | collective-permute-start | bytes 61448 | tf_op jit(solution)/shard_map/ppermute | solution.py:318
  47.2 3.6 %collective-permute-start.9 = (f32[40,128]{1,0:T(8,128)S(1)}, f32[40,128]{1,0:T(8,128)S(1)}, u32[]{:S(2)}, u32[]{:S(2)}) collective-permute-start(f32[40,128]{1,0:T(8,128)S(1)} %add.46), channel_id=1, source_target_pairs={{0,4},{1,5},{2,6},{3,7},{4,0},{5,1},{6,2},{7,3},{8,12},{9,13},{10,... | collective-permute-start | bytes 61448 | tf_op jit(solution)/shard_map/ppermute | solution.py:318
  48.5 6.9 %collective-permute-start.8 = (f32[40,128]{1,0:T(8,128)S(1)}, f32[40,128]{1,0:T(8,128)S(1)}, u32[]{:S(2)}, u32[]{:S(2)}) collective-permute-start(f32[40,128]{1,0:T(8,128)S(1)} %add.46), channel_id=1, source_target_pairs={{0,8},{1,9},{2,10},{3,11},{4,12},{5,13},{6,14},{7,15},{8,0},{9,1},... | collective-permute-start | bytes 61448 | tf_op jit(solution)/shard_map/ppermute | solution.py:318
  55.4 3.5 %collective-permute-start.13 = (f32[40,128]{1,0:T(8,128)S(1)}, f32[40,128]{1,0:T(8,128)S(1)}, u32[]{:S(2)}, u32[]{:S(2)}) collective-permute-start(f32[40,128]{1,0:T(8,128)S(1)} %get-tuple-element.22), channel_id=1, source_target_pairs={{0,48},{1,49},{2,50},{3,51},{4,52},{5,53},{6,54},{7,55},{8,56},{9,... | collective-permute-start | bytes 61448 | tf_op jit(solution)/shard_map/ppermute | solution.py:314
  58.0 4.2 %collective-permute-start.12 = (f32[40,128]{1,0:T(8,128)S(1)}, f32[40,128]{1,0:T(8,128)S(1)}, u32[]{:S(2)}, u32[]{:S(2)}) collective-permute-start(f32[40,128]{1,0:T(8,128)S(1)} %get-tuple-element.22), channel_id=1, source_target_pairs={{0,32},{1,33},{2,34},{3,35},{4,36},{5,37},{6,38},{7,39},{8,40},{9,... | collective-permute-start | bytes 61448 | tf_op jit(solution)/shard_map/ppermute | solution.py:314
  58.1 4.1 %collective-permute-start.11 = (f32[40,128]{1,0:T(8,128)S(1)}, f32[40,128]{1,0:T(8,128)S(1)}, u32[]{:S(2)}, u32[]{:S(2)}) collective-permute-start(f32[40,128]{1,0:T(8,128)S(1)} %get-tuple-element.22), channel_id=1, source_target_pairs={{0,16},{1,17},{2,18},{3,19},{4,20},{5,21},{6,22},{7,23},{8,24},{9,... | collective-permute-start | bytes 61448 | tf_op jit(solution)/shard_map/ppermute | solution.py:314
  62.2 7.5 %collective-permute-start.16 = (f32[160,128]{1,0:T(8,128)S(1)}, f32[160,128]{1,0:T(8,128)S(1)}, u32[]{:S(2)}, u32[]{:S(2)}) collective-permute-start(f32[160,128]{1,0:T(8,128)S(1)} %pad_maximum_fusion), channel_id=1, source_target_pairs={{0,192},{64,0},{128,64},{192,128},{1,193},{65,1},{129,65},{193,129... | collective-permute-start | bytes 245768 | tf_op jit(solution)/shard_map/ppermute | solution.py:306
  63.9 5.8 %collective-permute-start.15 = (f32[160,128]{1,0:T(8,128)S(1)}, f32[160,128]{1,0:T(8,128)S(1)}, u32[]{:S(2)}, u32[]{:S(2)}) collective-permute-start(f32[160,128]{1,0:T(8,128)S(1)} %pad_maximum_fusion), channel_id=1, source_target_pairs={{0,128},{64,192},{128,0},{192,64},{1,129},{65,193},{129,1},{193,65... | collective-permute-start | bytes 245768 | tf_op jit(solution)/shard_map/ppermute | solution.py:306
  63.9 5.8 %collective-permute-start.14 = (f32[160,128]{1,0:T(8,128)S(1)}, f32[160,128]{1,0:T(8,128)S(1)}, u32[]{:S(2)}, u32[]{:S(2)}) collective-permute-start(f32[160,128]{1,0:T(8,128)S(1)} %pad_maximum_fusion), channel_id=1, source_target_pairs={{0,64},{64,128},{128,192},{192,0},{1,65},{65,129},{129,193},{193,1... | collective-permute-start | bytes 245768 | tf_op jit(solution)/shard_map/ppermute | solution.py:306
  69.8 14.7 %collective-permute-start.17 = (f32[640,128]{1,0:T(8,128)S(1)}, f32[640,128]{1,0:T(8,128)S(1)}, u32[]{:S(2)}, u32[]{:S(2)}) collective-permute-start(f32[640,128]{1,0:T(8,128)S(1)} %constant_dynamic-update-slice_fusion.own_ref), channel_id=1, source_target_pairs={{0,1},{1,0},{2,3},{3,2},{4,5},{5,4},{6,7},{7,6},{8,9},{9,8},{10,11... | collective-permute-start | bytes 983048 | tf_op jit(solution)/shard_map/ppermute | solution.py:322
  82.5 1.4 copy-start.7
  83.9 0.6 copy-start.8
  124.5 4.1 %collective-permute-start.18 = (bf16[128,512]{1,0:T(8,128)(2,1)}, bf16[128,512]{1,0:T(8,128)(2,1)S(1)}, u32[]{:S(2)}, u32[]{:S(2)}) collective-permute-start(bf16[128,512]{1,0:T(8,128)(2,1)} %get-tuple-element.18), channel_id=1, source_target_pairs={{0,64},{64,0},{128,192},{192,128},{1,65},{65,1},{129,193},{193,129... | collective-permute-start | bytes 393224 | tf_op jit(solution)/shard_map/ppermute | solution.py:310
  125.4 8.0 %collective-permute-start.20 = (bf16[128,512]{1,0:T(8,128)(2,1)}, bf16[128,512]{1,0:T(8,128)(2,1)S(1)}, u32[]{:S(2)}, u32[]{:S(2)}) collective-permute-start(bf16[128,512]{1,0:T(8,128)(2,1)} %get-tuple-element.19), channel_id=1, source_target_pairs={{0,192},{64,128},{128,64},{192,0},{1,193},{65,129},{129,65},{193,1... | collective-permute-start | bytes 393224 | tf_op jit(solution)/shard_map/ppermute | solution.py:310
  129.5 6.3 %collective-permute-start.19 = (bf16[128,512]{1,0:T(8,128)(2,1)S(1)}, bf16[128,512]{1,0:T(8,128)(2,1)S(1)}, u32[]{:S(2)}, u32[]{:S(2)}) collective-permute-start(bf16[128,512]{1,0:T(8,128)(2,1)S(1)} %add_convert_fusion.1.upper_ref), channel_id=1, source_target_pairs={{0,192},{64,128},{128,64},{192,0},{1,193},{65,129},{129,65},{193,1... | collective-permute-start | bytes 393224 | tf_op jit(solution)/shard_map/ppermute | solution.py:310
  134.4 3.9 %collective-permute-start.21 = (bf16[128,512]{1,0:T(8,128)(2,1)S(1)}, bf16[128,512]{1,0:T(8,128)(2,1)S(1)}, u32[]{:S(2)}, u32[]{:S(2)}) collective-permute-start(bf16[128,512]{1,0:T(8,128)(2,1)S(1)} %add_convert_fusion.lower_ref), channel_id=1, source_target_pairs={{0,64},{64,0},{128,192},{192,128},{1,65},{65,1},{129,193},{193,129... | collective-permute-start | bytes 393224 | tf_op jit(solution)/shard_map/ppermute | solution.py:310
Sparse Core Ops, SparseCore 0:
  10.1 104.3 all-gather.1

commit v4 on v3

--- a/solution.py
+++ b/solution.py
@@ -21,12 +21,16 @@
     return ent // 16, lax.axis_index("rel"), ent % 2
 
 
-def system_kernel(rows_ref, core_ref, out_ref, packed_ref, d0_ref, d1_ref, low_ref, c0_ref, c1_ref):
+def system_kernel(rows_ref, cores_ref, out_ref, core_ref, packed_ref, d0_ref, d1_ref, low_ref, c0_ref, c1_ref, sem):
+    fetch = lambda step: pltpu.make_async_copy(cores_ref.at[step], core_ref.at[step], sem.at[step])
+    for step in range(8):
+        fetch(step).start()
     rows = rows_ref[...]
     for ref in (d0_ref, d1_ref, low_ref, c0_ref, c1_ref):
         ref[...] = jnp.zeros_like(ref)
 
     def body(step, carry):
+        fetch(step).wait()
         core = core_ref[step]
         term = jnp.concatenate([product(rows, core, 1, 1), product(rows, core, 1, 0)], axis=0)
         high = term.astype(jnp.bfloat16)
@@ -64,10 +68,12 @@
     return pl.pallas_call(
         system_kernel,
         out_shape=jax.ShapeDtypeStruct((1280, 128), jnp.float32),
-        in_specs=[IN_VMEM] * 2,
+        in_specs=[IN_VMEM, pl.BlockSpec(memory_space=pltpu.HBM)],
         out_specs=IN_VMEM,
-        scratch_shapes=[pltpu.VMEM((1280, 128), jnp.float32)] + [pltpu.VMEM((256, 256), jnp.float32)] * 5,
-        compiler_params=pltpu.CompilerParams(vmem_limit_bytes=32 * MIB),
+        scratch_shapes=[pltpu.VMEM(cores.shape, cores.dtype), pltpu.VMEM((1280, 128), jnp.float32)]
+        + [pltpu.VMEM((256, 256), jnp.float32)] * 5
+        + [pltpu.SemaphoreType.DMA((8,))],
+        compiler_params=pltpu.CompilerParams(vmem_limit_bytes=52 * MIB),
         cost_estimate=pl.CostEstimate(flops=12000000000, bytes_accessed=5000000, transcendentals=0),
     )(factor, cores)
 
@@ -210,15 +216,12 @@
 
 
 def rows_kernel(
-    count_ref, place_ref, tiles_ref, cores_ref, panels_ref, upper_ref, lower_ref, sums_ref, panel_ref, core_ref, values_ref,
-    sem, core_sem, values_sem
+    count_ref, place_ref, values_ref, cores_ref, panels_ref, upper_ref, lower_ref, sums_ref, panel_ref, core_ref,
+    sem, core_sem
 ):
     def fetch(owner):
-        start = pl.multiple_of(place_ref[0, owner] * 128, 128)
-        return pltpu.make_async_copy(panels_ref.at[pl.ds(start, 128), :], panel_ref.at[owner], sem.at[owner])
-
-    values_copy = pltpu.make_async_copy(tiles_ref, values_ref, values_sem)
-    values_copy.start()
+        start = pl.multiple_of((place_ref[0, owner] % 2) * 128, 128)
+        return pltpu.make_async_copy(panels_ref.at[owner, pl.ds(start, 128), :], panel_ref.at[owner], sem.at[owner])
 
     def begin(step, carry):
         for i in range(8):
@@ -235,8 +238,6 @@
         term = product(values_ref[index], panel_ref[owner], 1, 0)
         where = (place_ref[1, index], pl.ds(place, 128), slice(None))
         sums_ref[where] = sums_ref[where] + term
-
-    values_copy.wait()
 
     def main(step, carry):
         for i in range(8):
@@ -267,18 +268,16 @@
     return pl.pallas_call(
         rows_kernel,
         out_shape=(jax.ShapeDtypeStruct((128, 512), jnp.bfloat16),) * 2,
-        in_specs=[IN_SMEM, IN_SMEM] + [pl.BlockSpec(memory_space=pltpu.HBM)] * 3,
+        in_specs=[IN_SMEM, IN_SMEM, IN_VMEM] + [pl.BlockSpec(memory_space=pltpu.HBM)] * 2,
         out_specs=(IN_VMEM,) * 2,
         scratch_shapes=[
             pltpu.VMEM((16, 256, 512), jnp.float32),
             pltpu.VMEM((64, 128, 512), jnp.bfloat16),
             pltpu.VMEM(cores.shape, cores.dtype),
-            pltpu.VMEM(values.shape, values.dtype),
             pltpu.SemaphoreType.DMA((64,)),
             pltpu.SemaphoreType.DMA,
-            pltpu.SemaphoreType.DMA,
         ],
-        compiler_params=pltpu.CompilerParams(vmem_limit_bytes=60 * MIB),
+        compiler_params=pltpu.CompilerParams(vmem_limit_bytes=49 * MIB),
         cost_estimate=pl.CostEstimate(flops=10000000000, bytes_accessed=16000000, transcendentals=0),
     )(count, place, values, cores, panels)
 
@@ -344,7 +343,7 @@
 
 
 def local(factor, core_tensors, tile_values, tile_rel, tile_block, tile_col, tile_flip, tile_count):
-    panels = lax.all_gather(factor, "ent", tiled=True)
+    panels = lax.all_gather(factor, "ent")
     inverted = inverse(*sum_everywhere(system_term(factor, core_tensors)))
     values, place = align(tile_rel[0], tile_block[0], tile_col[0], tile_flip[0], tile_values[0])
     panels, inverted, values, place = lax.optimization_barrier((panels, inverted, values, place))

time: 147 us -> 143 us (0.973)
  waiting for transfers between devices: 32.5 us -> 37.2 us
  local copies, waits for them, and re-layouts: 5.23 us -> 1.04 us
  starting transfers between devices: 41.6 us -> 39.4 us
  other arithmetic: 1.97 us -> 0.16 us
    unnamed x23 -> x17, local copies, waits for them, and re-layouts: 5.17 us -> 0.99 us
    all_gather x1, waiting for transfers between devices: 2.88 us -> 6.07 us  [local(): panels = lax.all_gather(factor, 'ent')]
    convert_element_type x2, other arithmetic: 1.87 us -> 0.07 us  [local(): (a.astype(jnp.float32) + b.astype(jnp.float32)).astype(jnp.bfloat16)]
    pallas_call x1, Pallas kernels: 9.96 us -> 8.35 us  [partial_rows(): pl.pallas_call(rows_kernel, out_shape=(jax.ShapeDtypeStruct((128, 512), j...]
  transfers between devices with their start and end apart: 23 -> 23, of which waited for: 16 -> 15; matrix products, arithmetic and copies ran while one was open for 1% -> 0% of each run, Pallas kernels for 27% -> 29%
where the time goes in v4:
time: 143 us
  Pallas kernels  51.1 us (36%)
  starting transfers between devices  39.4 us (28%)
  waiting for transfers between devices  37.2 us (26%)
  between operations  14.3 us (10%)
    pallas_call x1, Pallas kernels, inverse(): pl.pallas_call(inverse_kernel, out_shape=jax.ShapeDtypeStruct((512, 512),...  27.1 us
    ppermute x2, starting transfers between devices, swap_core(): return lax.ppermute(v, 'ent', [(e, e ^ 1) for e in range(64)])  11.4 us
    pallas_call x1, Pallas kernels, system_term(): pl.pallas_call(system_kernel, out_shape=jax.ShapeDtypeStruct((1280, 128),...  10.4 us
    ppermute x4, starting transfers between devices, swap_z(): return lax.ppermute(v, 'ent', [(e, e ^ 2 * bits) for e in range(64)])  9.61 us
    ppermute x6, waiting for transfers between devices, over_y(): return lax.ppermute(v, 'rel', [(y, (y + d) % 4) for y in range(4)])  8.99 us
    pallas_call x1, Pallas kernels, partial_rows(): pl.pallas_call(rows_kernel, out_shape=(jax.ShapeDtypeStruct((128, 512), j...  8.35 us
    ppermute x4, waiting for transfers between devices, swap_z(): return lax.ppermute(v, 'ent', [(e, e ^ 2 * bits) for e in range(64)])  7.75 us
    ppermute x6, starting transfers between devices, over_x(): return lax.ppermute(v, 'ent', [(e, (e + 16 * d) % 64) for e in range(64)])  7.74 us
  transfers between devices with their start and end apart: 23, of which 15 were waited for; matrix products, arithmetic and copies ran while one was open for 0% of the time, Pallas kernels for 29%

profile of v4, /device:TPU:1, one launch (start us, length us, event | category | flops | bytes accessed | tf_op | source)
XLA Modules:
  0.0 143.2 jit_solution(5412125596491667052)
XLA Ops:
  6.5 0.0 all-gather.3.cloned.1.call-start
  6.5 0.7 all-gather.3.cloned.1.call-update
  7.3 0.0 copy-start
  7.3 0.9 copy-done
  8.2 0.0 copy-start.1
  8.2 0.0 copy-start.2
  8.2 0.0 copy-start.3
  8.2 0.0 copy-start.4
  8.2 0.0 copy-start.5
  8.2 10.4 %shard_map.82 = f32[1280,128]{1,0:T(8,128)S(1)} custom-call(bf16[256,512]{1,0:T(8,128)(2,1)S(1)} %copy-done, bf16[8,512,512]{2,1,0:T(8,128)(2,1)} %cores_ref.3), custom_call_target="tpu_custom_call" | custom-call | flops 12000000000 | bytes 5000000 | tf_op jit(solution)/shard_map/pallas_call | solution.py:68
  18.7 3.3 %collective-permute-start = (f32[640,128]{1,0:T(8,128)S(1)}, f32[640,128]{1,0:T(8,128)S(1)}, u32[]{:S(2)}, u32[]{:S(2)}) collective-permute-start(f32[640,128]{1,0:T(8,128)S(1)} %slice.41), channel_id=1, source_target_pairs={{0,1},{1,0},{2,3},{3,2},{4,5},{5,4},{6,7},{7,6},{8,9},{9,8},{10,11... | collective-permute-start | bytes 983048 | tf_op jit(solution)/shard_map/ppermute | solution.py:321
  22.0 1.3 collective-permute-done
  23.3 1.1 collective-permute-start.3
  24.4 0.5 collective-permute-start.2
  24.9 1.2 collective-permute-start.1
  26.1 1.0 collective-permute-done.3
  27.1 2.0 %collective-permute-done.2 = f32[160,128]{1,0:T(8,128)S(1)} collective-permute-done((f32[160,128]{1,0:T(8,128)S(1)}, f32[160,128]{1,0:T(8,128)S(1)}, u32[]{:S(2)}, u32[]{:S(2)}) %collective-permute-start.2) | collective-permute-done | bytes 81952 | tf_op jit(solution)/shard_map/ppermute | solution.py:305
  29.1 0.9 collective-permute-done.1
  30.0 3.0 %collective-permute-start.6 = (f32[40,128]{1,0:T(8,128)S(1)}, f32[40,128]{1,0:T(8,128)S(1)}, u32[]{:S(2)}, u32[]{:S(2)}) collective-permute-start(f32[40,128]{1,0:T(8,128)S(1)} %get-tuple-element.26), channel_id=1, source_target_pairs={{0,48},{1,49},{2,50},{3,51},{4,52},{5,53},{6,54},{7,55},{8,56},{9,... | collective-permute-start | bytes 61448 | tf_op jit(solution)/shard_map/ppermute | solution.py:313
  33.0 0.0 collective-permute-start.5
  33.0 1.7 %collective-permute-start.4 = (f32[40,128]{1,0:T(8,128)S(1)}, f32[40,128]{1,0:T(8,128)S(1)}, u32[]{:S(2)}, u32[]{:S(2)}) collective-permute-start(f32[40,128]{1,0:T(8,128)S(1)} %get-tuple-element.28), channel_id=1, source_target_pairs={{0,32},{1,33},{2,34},{3,35},{4,36},{5,37},{6,38},{7,39},{8,40},{9,... | collective-permute-start | bytes 61448 | tf_op jit(solution)/shard_map/ppermute | solution.py:313
  34.7 0.0 collective-permute-done.6
  34.7 2.8 %collective-permute-done.5 = f32[40,128]{1,0:T(8,128)S(1)} collective-permute-done((f32[40,128]{1,0:T(8,128)S(1)}, f32[40,128]{1,0:T(8,128)S(1)}, u32[]{:S(2)}, u32[]{:S(2)}) %collective-permute-start.5) | collective-permute-done | bytes 20512 | tf_op jit(solution)/shard_map/ppermute | solution.py:313
  37.5 0.0 collective-permute-done.4
  37.6 1.3 collective-permute-start.7
  38.8 1.8 %collective-permute-done.7 = f32[40,128]{1,0:T(8,128)S(1)} collective-permute-done((f32[40,128]{1,0:T(8,128)S(1)}, f32[40,128]{1,0:T(8,128)S(1)}, u32[]{:S(2)}, u32[]{:S(2)}) %collective-permute-start.7) | collective-permute-done | bytes 20512 | tf_op jit(solution)/shard_map/ppermute | solution.py:317
  40.7 6.1 %collective-permute-start.10 = (f32[40,128]{1,0:T(8,128)S(1)}, f32[40,128]{1,0:T(8,128)S(1)}, u32[]{:S(2)}, u32[]{:S(2)}) collective-permute-start(f32[40,128]{1,0:T(8,128)S(1)} %add.46), channel_id=1, source_target_pairs={{0,12},{1,13},{2,14},{3,15},{4,8},{5,9},{6,10},{7,11},{8,4},{9,5},... | collective-permute-start | bytes 61448 | tf_op jit(solution)/shard_map/ppermute | solution.py:317
  46.8 1.1 collective-permute-start.9
  47.9 1.1 collective-permute-start.8
  49.0 0.0 collective-permute-done.10
  49.0 1.4 collective-permute-done.9
  50.4 4.6 %collective-permute-done.8 = f32[40,128]{1,0:T(8,128)S(1)} collective-permute-done((f32[40,128]{1,0:T(8,128)S(1)}, f32[40,128]{1,0:T(8,128)S(1)}, u32[]{:S(2)}, u32[]{:S(2)}) %collective-permute-start.8) | collective-permute-done | bytes 20512 | tf_op jit(solution)/shard_map/ppermute | solution.py:317
  54.9 2.3 %collective-permute-start.13 = (f32[40,128]{1,0:T(8,128)S(1)}, f32[40,128]{1,0:T(8,128)S(1)}, u32[]{:S(2)}, u32[]{:S(2)}) collective-permute-start(f32[40,128]{1,0:T(8,128)S(1)} %get-tuple-element.22), channel_id=1, source_target_pairs={{0,48},{1,49},{2,50},{3,51},{4,52},{5,53},{6,54},{7,55},{8,56},{9,... | collective-permute-start | bytes 61448 | tf_op jit(solution)/shard_map/ppermute | solution.py:313
  57.3 0.0 collective-permute-start.12
  57.3 0.7 collective-permute-start.11
  57.9 0.2 collective-permute-done.13
  58.2 3.2 %collective-permute-done.12 = f32[40,128]{1,0:T(8,128)S(1)} collective-permute-done((f32[40,128]{1,0:T(8,128)S(1)}, f32[40,128]{1,0:T(8,128)S(1)}, u32[]{:S(2)}, u32[]{:S(2)}) %collective-permute-start.12) | collective-permute-done | bytes 20512 | tf_op jit(solution)/shard_map/ppermute | solution.py:313
  61.4 0.0 collective-permute-done.11
  61.4 1.6 %collective-permute-start.16 = (f32[160,128]{1,0:T(8,128)S(1)}, f32[160,128]{1,0:T(8,128)S(1)}, u32[]{:S(2)}, u32[]{:S(2)}) collective-permute-start(f32[160,128]{1,0:T(8,128)S(1)} %pad_maximum_fusion), channel_id=1, source_target_pairs={{0,192},{64,0},{128,64},{192,128},{1,193},{65,1},{129,65},{193,129... | collective-permute-start | bytes 245768 | tf_op jit(solution)/shard_map/ppermute | solution.py:305
  63.0 0.4 collective-permute-start.15
  63.4 0.5 collective-permute-start.14
  64.0 5.1 %collective-permute-done.14 = f32[160,128]{1,0:T(8,128)S(1)} collective-permute-done((f32[160,128]{1,0:T(8,128)S(1)}, f32[160,128]{1,0:T(8,128)S(1)}, u32[]{:S(2)}, u32[]{:S(2)}) %collective-permute-start.14) | collective-permute-done | bytes 81952 | tf_op jit(solution)/shard_map/ppermute | solution.py:305
  69.1 0.0 collective-permute-done.15
  69.1 0.0 collective-permute-done.16
  69.1 8.0 %collective-permute-start.17 = (f32[640,128]{1,0:T(8,128)S(1)}, f32[640,128]{1,0:T(8,128)S(1)}, u32[]{:S(2)}, u32[]{:S(2)}) collective-permute-start(f32[640,128]{1,0:T(8,128)S(1)} %constant_dynamic-update-slice_fusion.own_ref), channel_id=1, source_target_pairs={{0,1},{1,0},{2,3},{3,2},{4,5},{5,4},{6,7},{7,6},{8,9},{9,8},{10,11... | collective-permute-start | bytes 983048 | tf_op jit(solution)/shard_map/ppermute | solution.py:321
  77.8 0.0 copy-done.1
  77.8 0.0 copy-done.2
  77.8 0.0 copy-done.3
  77.9 0.0 copy-done.4
  77.9 0.0 copy-done.5
  77.9 3.3 %shard_map.84 = (bf16[72,128,128]{2,1,0:T(8,128)(2,1)S(1)}, s32[3,72]{1,0:T(4,128)S(1)}) custom-call(s32[72]{0:T(128)S(1)} %bitcast.9, s32[72]{0:T(128)S(1)} %bitcast.10, s32[72]{0:T(128)S(1)} %bitcast.11, s32[72]{0:T(128)S(1)} %bitcast.12, bf16[72,128,128]{2,1,0:T(8,128)(2,1)S(1)} %bitcast.8), custom_call_target="tpu_custom_call" | custom-call | flops 3000000000 | bytes 4800000 | tf_op jit(solution)/shard_map/pallas_call | solution.py:204
  81.2 0.0 collective-permute-done.17.other_ref
  81.2 27.1 %shard_map.83.inverse_ref = f32[512,512]{1,0:T(8,128)S(1)} custom-call(f32[640,128]{1,0:T(8,128)S(1)} %constant_dynamic-update-slice_fusion.own_ref, f32[640,128]{1,0:T(8,128)S(1)} %collective-permute-done.17.other_ref), custom_call_target="tpu_custom_call" | custom-call | flops 30000001024 | bytes 2000000 | tf_op jit(solution)/shard_map/pallas_call | solution.py:169
  108.3 6.1 %all-gather.3.cloned.1.call-done = bf16[16384,512]{1,0:T(8,128)(2,1)} async-done(((bf16[256,512]{1,0:T(8,128)(2,1)}), bf16[16384,512]{1,0:T(8,128)(2,1)}) %all-gather.3.cloned.1.call-update) | async-done | bytes 16777232 | tf_op jit(solution)/shard_map/all_gather | solution.py:346
  114.4 8.3 %shard_map.85 = (bf16[128,512]{1,0:T(8,128)(2,1)S(1)}, bf16[128,512]{1,0:T(8,128)(2,1)S(1)}) custom-call(s32[1]{0:T(128)} %bitcast.7.count_ref, s32[3,72]{1,0:T(4,128)S(1)} %get-tuple-element.15.place_ref, bf16[72,128,128]{2,1,0:T(8,128)(2,1)S(1)} %get-tuple-element.16.values_ref, bf16[8,512,512]{2,1,0:T(8,128)(2,1)} %cores_ref.3, bf16[64,256,512]{2,1,0:T(8,128)(2,1)} %bitcast.13), custom_call_target="tpu_custom_call" | custom-call | flops 10000000000 | bytes 16000000 | tf_op jit(solution)/shard_map/pallas_call | solution.py:268
  122.8 1.9 %collective-permute-start.18 = (bf16[128,512]{1,0:T(8,128)(2,1)S(1)}, bf16[128,512]{1,0:T(8,128)(2,1)S(1)}, u32[]{:S(2)}, u32[]{:S(2)}) collective-permute-start(bf16[128,512]{1,0:T(8,128)(2,1)S(1)} %get-tuple-element.18), channel_id=1, source_target_pairs={{0,64},{64,0},{128,192},{192,128},{1,65},{65,1},{129,193},{193,129... | collective-permute-start | bytes 393224 | tf_op jit(solution)/shard_map/ppermute | solution.py:309
  124.6 1.2 collective-permute-start.20
  125.9 2.1 %collective-permute-done.18 = bf16[128,512]{1,0:T(8,128)(2,1)S(1)} collective-permute-done((bf16[128,512]{1,0:T(8,128)(2,1)S(1)}, bf16[128,512]{1,0:T(8,128)(2,1)S(1)}, u32[]{:S(2)}, u32[]{:S(2)}) %collective-permute-start.18) | collective-permute-done | bytes 131104 | tf_op jit(solution)/shard_map/ppermute | solution.py:309
  128.0 2.2 %collective-permute-start.19 = (bf16[128,512]{1,0:T(8,128)(2,1)S(1)}, bf16[128,512]{1,0:T(8,128)(2,1)S(1)}, u32[]{:S(2)}, u32[]{:S(2)}) collective-permute-start(bf16[128,512]{1,0:T(8,128)(2,1)S(1)} %add_convert_fusion.1.upper_ref), channel_id=1, source_target_pairs={{0,192},{64,128},{128,64},{192,0},{1,193},{65,129},{129,65},{193,1... | collective-permute-start | bytes 393224 | tf_op jit(solution)/shard_map/ppermute | solution.py:309
  130.2 0.0 collective-permute-done.20
  130.2 0.1 collective-permute-start.21
  130.3 2.7 %collective-permute-done.19.upper_other_ref = bf16[128,512]{1,0:T(8,128)(2,1)S(1)} collective-permute-done((bf16[128,512]{1,0:T(8,128)(2,1)S(1)}, bf16[128,512]{1,0:T(8,128)(2,1)S(1)}, u32[]{:S(2)}, u32[]{:S(2)}) %collective-permute-start.19) | collective-permute-done | bytes 131104 | tf_op jit(solution)/shard_map/ppermute | solution.py:309
  133.1 1.4 collective-permute-done.21.lower_other_ref
  134.4 1.9 %shard_map.86 = f32[256,512]{1,0:T(8,128)} custom-call(bf16[128,512]{1,0:T(8,128)(2,1)S(1)} %add_convert_fusion.1.upper_ref, bf16[128,512]{1,0:T(8,128)(2,1)S(1)} %collective-permute-done.19.upper_other_ref, bf16[128,512]{1,0:T(8,128)(2,1)S(1)} %add_convert_fusion.lower_ref, bf16[128,512]{1,0:T(8,128)(2,1)S(1)} %collective-permute-done.21.lower_other_ref, ...), custom_call_target="tpu_custom_call" | custom-call | flops 1000000000 | bytes 2500000 | tf_op jit(solution)/shard_map/pallas_call | solution.py:294
  (17 shorter events, 0.2 us)
Async XLA Ops:
  6.5 107.9 %all-gather.3.cloned.1.call-start = ((), (), s32[]{:S(2)}) async-start(), calls=%async_computation | async-start | bytes 17039360 | tf_op jit(solution)/shard_map/all_gather | solution.py:346
  7.3 1.0 copy-start
  8.2 69.6 %copy-start.1 = (bf16[1,72,128,128]{3,2,1,0:T(8,128)(2,1)S(1)}, bf16[1,72,128,128]{3,2,1,0:T(8,128)(2,1)}, u32[]{:S(2)}) copy-start(bf16[1,72,128,128]{3,2,1,0:T(8,128)(2,1)} %param.10) | copy-start | bytes 7077892
  8.2 69.6 %copy-start.2 = (s32[1,72]{1,0:T(1,128)S(1)}, s32[1,72]{1,0:T(1,128)}, u32[]{:S(2)}) copy-start(s32[1,72]{1,0:T(1,128)} %param.11) | copy-start | bytes 868
  8.2 69.6 %copy-start.3 = (s32[1,72]{1,0:T(1,128)S(1)}, s32[1,72]{1,0:T(1,128)}, u32[]{:S(2)}) copy-start(s32[1,72]{1,0:T(1,128)} %param.12) | copy-start | bytes 868
  8.2 69.6 %copy-start.4 = (s32[1,72]{1,0:T(1,128)S(1)}, s32[1,72]{1,0:T(1,128)}, u32[]{:S(2)}) copy-start(s32[1,72]{1,0:T(1,128)} %param.13) | copy-start | bytes 868
  8.2 69.7 %copy-start.5 = (s32[1,72]{1,0:T(1,128)S(1)}, s32[1,72]{1,0:T(1,128)}, u32[]{:S(2)}) copy-start(s32[1,72]{1,0:T(1,128)} %param.14) | copy-start | bytes 868
  18.7 4.6 %collective-permute-start = (f32[640,128]{1,0:T(8,128)S(1)}, f32[640,128]{1,0:T(8,128)S(1)}, u32[]{:S(2)}, u32[]{:S(2)}) collective-permute-start(f32[640,128]{1,0:T(8,128)S(1)} %slice.41), channel_id=1, source_target_pairs={{0,1},{1,0},{2,3},{3,2},{4,5},{5,4},{6,7},{7,6},{8,9},{9,8},{10,11... | collective-permute-start | bytes 983048 | tf_op jit(solution)/shard_map/ppermute | solution.py:321
  23.3 3.7 %collective-permute-start.3 = (f32[160,128]{1,0:T(8,128)S(1)}, f32[160,128]{1,0:T(8,128)S(1)}, u32[]{:S(2)}, u32[]{:S(2)}) collective-permute-start(f32[160,128]{1,0:T(8,128)S(1)} %get-tuple-element.23), channel_id=1, source_target_pairs={{0,192},{64,0},{128,64},{192,128},{1,193},{65,1},{129,65},{193,129... | collective-permute-start | bytes 245768 | tf_op jit(solution)/shard_map/ppermute | solution.py:305
  24.4 4.7 %collective-permute-start.2 = (f32[160,128]{1,0:T(8,128)S(1)}, f32[160,128]{1,0:T(8,128)S(1)}, u32[]{:S(2)}, u32[]{:S(2)}) collective-permute-start(f32[160,128]{1,0:T(8,128)S(1)} %get-tuple-element.24), channel_id=1, source_target_pairs={{0,64},{64,128},{128,192},{192,0},{1,65},{65,129},{129,193},{193,1... | collective-permute-start | bytes 245768 | tf_op jit(solution)/shard_map/ppermute | solution.py:305
  24.9 5.1 %collective-permute-start.1 = (f32[160,128]{1,0:T(8,128)S(1)}, f32[160,128]{1,0:T(8,128)S(1)}, u32[]{:S(2)}, u32[]{:S(2)}) collective-permute-start(f32[160,128]{1,0:T(8,128)S(1)} %get-tuple-element.25), channel_id=1, source_target_pairs={{0,128},{64,192},{128,0},{192,64},{1,129},{65,193},{129,1},{193,65... | collective-permute-start | bytes 245768 | tf_op jit(solution)/shard_map/ppermute | solution.py:305
  30.0 4.7 %collective-permute-start.6 = (f32[40,128]{1,0:T(8,128)S(1)}, f32[40,128]{1,0:T(8,128)S(1)}, u32[]{:S(2)}, u32[]{:S(2)}) collective-permute-start(f32[40,128]{1,0:T(8,128)S(1)} %get-tuple-element.26), channel_id=1, source_target_pairs={{0,48},{1,49},{2,50},{3,51},{4,52},{5,53},{6,54},{7,55},{8,56},{9,... | collective-permute-start | bytes 61448 | tf_op jit(solution)/shard_map/ppermute | solution.py:313
  33.0 4.6 %collective-permute-start.5 = (f32[40,128]{1,0:T(8,128)S(1)}, f32[40,128]{1,0:T(8,128)S(1)}, u32[]{:S(2)}, u32[]{:S(2)}) collective-permute-start(f32[40,128]{1,0:T(8,128)S(1)} %get-tuple-element.27), channel_id=1, source_target_pairs={{0,16},{1,17},{2,18},{3,19},{4,20},{5,21},{6,22},{7,23},{8,24},{9,... | collective-permute-start | bytes 61448 | tf_op jit(solution)/shard_map/ppermute | solution.py:313
  33.0 4.6 %collective-permute-start.4 = (f32[40,128]{1,0:T(8,128)S(1)}, f32[40,128]{1,0:T(8,128)S(1)}, u32[]{:S(2)}, u32[]{:S(2)}) collective-permute-start(f32[40,128]{1,0:T(8,128)S(1)} %get-tuple-element.28), channel_id=1, source_target_pairs={{0,32},{1,33},{2,34},{3,35},{4,36},{5,37},{6,38},{7,39},{8,40},{9,... | collective-permute-start | bytes 61448 | tf_op jit(solution)/shard_map/ppermute | solution.py:313
  37.6 3.1 %collective-permute-start.7 = (f32[40,128]{1,0:T(8,128)S(1)}, f32[40,128]{1,0:T(8,128)S(1)}, u32[]{:S(2)}, u32[]{:S(2)}) collective-permute-start(f32[40,128]{1,0:T(8,128)S(1)} %fusion.1), channel_id=1, source_target_pairs={{0,2},{1,3},{2,0},{3,1},{4,6},{5,7},{6,4},{7,5},{8,10},{9,11},{10,... | collective-permute-start | bytes 61448 | tf_op jit(solution)/shard_map/ppermute | solution.py:317
  40.7 8.3 %collective-permute-start.10 = (f32[40,128]{1,0:T(8,128)S(1)}, f32[40,128]{1,0:T(8,128)S(1)}, u32[]{:S(2)}, u32[]{:S(2)}) collective-permute-start(f32[40,128]{1,0:T(8,128)S(1)} %add.46), channel_id=1, source_target_pairs={{0,12},{1,13},{2,14},{3,15},{4,8},{5,9},{6,10},{7,11},{8,4},{9,5},... | collective-permute-start | bytes 61448 | tf_op jit(solution)/shard_map/ppermute | solution.py:317
  46.8 3.5 %collective-permute-start.9 = (f32[40,128]{1,0:T(8,128)S(1)}, f32[40,128]{1,0:T(8,128)S(1)}, u32[]{:S(2)}, u32[]{:S(2)}) collective-permute-start(f32[40,128]{1,0:T(8,128)S(1)} %add.46), channel_id=1, source_target_pairs={{0,4},{1,5},{2,6},{3,7},{4,0},{5,1},{6,2},{7,3},{8,12},{9,13},{10,... | collective-permute-start | bytes 61448 | tf_op jit(solution)/shard_map/ppermute | solution.py:317
  47.9 7.0 %collective-permute-start.8 = (f32[40,128]{1,0:T(8,128)S(1)}, f32[40,128]{1,0:T(8,128)S(1)}, u32[]{:S(2)}, u32[]{:S(2)}) collective-permute-start(f32[40,128]{1,0:T(8,128)S(1)} %add.46), channel_id=1, source_target_pairs={{0,8},{1,9},{2,10},{3,11},{4,12},{5,13},{6,14},{7,15},{8,0},{9,1},... | collective-permute-start | bytes 61448 | tf_op jit(solution)/shard_map/ppermute | solution.py:317
  54.9 3.2 %collective-permute-start.13 = (f32[40,128]{1,0:T(8,128)S(1)}, f32[40,128]{1,0:T(8,128)S(1)}, u32[]{:S(2)}, u32[]{:S(2)}) collective-permute-start(f32[40,128]{1,0:T(8,128)S(1)} %get-tuple-element.22), channel_id=1, source_target_pairs={{0,48},{1,49},{2,50},{3,51},{4,52},{5,53},{6,54},{7,55},{8,56},{9,... | collective-permute-start | bytes 61448 | tf_op jit(solution)/shard_map/ppermute | solution.py:313
  57.3 4.1 %collective-permute-start.12 = (f32[40,128]{1,0:T(8,128)S(1)}, f32[40,128]{1,0:T(8,128)S(1)}, u32[]{:S(2)}, u32[]{:S(2)}) collective-permute-start(f32[40,128]{1,0:T(8,128)S(1)} %get-tuple-element.22), channel_id=1, source_target_pairs={{0,32},{1,33},{2,34},{3,35},{4,36},{5,37},{6,38},{7,39},{8,40},{9,... | collective-permute-start | bytes 61448 | tf_op jit(solution)/shard_map/ppermute | solution.py:313
  57.3 4.1 %collective-permute-start.11 = (f32[40,128]{1,0:T(8,128)S(1)}, f32[40,128]{1,0:T(8,128)S(1)}, u32[]{:S(2)}, u32[]{:S(2)}) collective-permute-start(f32[40,128]{1,0:T(8,128)S(1)} %get-tuple-element.22), channel_id=1, source_target_pairs={{0,16},{1,17},{2,18},{3,19},{4,20},{5,21},{6,22},{7,23},{8,24},{9,... | collective-permute-start | bytes 61448 | tf_op jit(solution)/shard_map/ppermute | solution.py:313
  61.4 7.7 %collective-permute-start.16 = (f32[160,128]{1,0:T(8,128)S(1)}, f32[160,128]{1,0:T(8,128)S(1)}, u32[]{:S(2)}, u32[]{:S(2)}) collective-permute-start(f32[160,128]{1,0:T(8,128)S(1)} %pad_maximum_fusion), channel_id=1, source_target_pairs={{0,192},{64,0},{128,64},{192,128},{1,193},{65,1},{129,65},{193,129... | collective-permute-start | bytes 245768 | tf_op jit(solution)/shard_map/ppermute | solution.py:305
  63.0 6.1 %collective-permute-start.15 = (f32[160,128]{1,0:T(8,128)S(1)}, f32[160,128]{1,0:T(8,128)S(1)}, u32[]{:S(2)}, u32[]{:S(2)}) collective-permute-start(f32[160,128]{1,0:T(8,128)S(1)} %pad_maximum_fusion), channel_id=1, source_target_pairs={{0,128},{64,192},{128,0},{192,64},{1,129},{65,193},{129,1},{193,65... | collective-permute-start | bytes 245768 | tf_op jit(solution)/shard_map/ppermute | solution.py:305
  63.4 5.7 %collective-permute-start.14 = (f32[160,128]{1,0:T(8,128)S(1)}, f32[160,128]{1,0:T(8,128)S(1)}, u32[]{:S(2)}, u32[]{:S(2)}) collective-permute-start(f32[160,128]{1,0:T(8,128)S(1)} %pad_maximum_fusion), channel_id=1, source_target_pairs={{0,64},{64,128},{128,192},{192,0},{1,65},{65,129},{129,193},{193,1... | collective-permute-start | bytes 245768 | tf_op jit(solution)/shard_map/ppermute | solution.py:305
  69.1 12.0 %collective-permute-start.17 = (f32[640,128]{1,0:T(8,128)S(1)}, f32[640,128]{1,0:T(8,128)S(1)}, u32[]{:S(2)}, u32[]{:S(2)}) collective-permute-start(f32[640,128]{1,0:T(8,128)S(1)} %constant_dynamic-update-slice_fusion.own_ref), channel_id=1, source_target_pairs={{0,1},{1,0},{2,3},{3,2},{4,5},{5,4},{6,7},{7,6},{8,9},{9,8},{10,11... | collective-permute-start | bytes 983048 | tf_op jit(solution)/shard_map/ppermute | solution.py:321
  122.8 5.2 %collective-permute-start.18 = (bf16[128,512]{1,0:T(8,128)(2,1)S(1)}, bf16[128,512]{1,0:T(8,128)(2,1)S(1)}, u32[]{:S(2)}, u32[]{:S(2)}) collective-permute-start(bf16[128,512]{1,0:T(8,128)(2,1)S(1)} %get-tuple-element.18), channel_id=1, source_target_pairs={{0,64},{64,0},{128,192},{192,128},{1,65},{65,1},{129,193},{193,129... | collective-permute-start | bytes 393224 | tf_op jit(solution)/shard_map/ppermute | solution.py:309
  124.6 5.6 %collective-permute-start.20 = (bf16[128,512]{1,0:T(8,128)(2,1)S(1)}, bf16[128,512]{1,0:T(8,128)(2,1)S(1)}, u32[]{:S(2)}, u32[]{:S(2)}) collective-permute-start(bf16[128,512]{1,0:T(8,128)(2,1)S(1)} %get-tuple-element.19), channel_id=1, source_target_pairs={{0,192},{64,128},{128,64},{192,0},{1,193},{65,129},{129,65},{193,1... | collective-permute-start | bytes 393224 | tf_op jit(solution)/shard_map/ppermute | solution.py:309
  128.0 5.1 %collective-permute-start.19 = (bf16[128,512]{1,0:T(8,128)(2,1)S(1)}, bf16[128,512]{1,0:T(8,128)(2,1)S(1)}, u32[]{:S(2)}, u32[]{:S(2)}) collective-permute-start(bf16[128,512]{1,0:T(8,128)(2,1)S(1)} %add_convert_fusion.1.upper_ref), channel_id=1, source_target_pairs={{0,192},{64,128},{128,64},{192,0},{1,193},{65,129},{129,65},{193,1... | collective-permute-start | bytes 393224 | tf_op jit(solution)/shard_map/ppermute | solution.py:309
  130.2 4.2 %collective-permute-start.21 = (bf16[128,512]{1,0:T(8,128)(2,1)S(1)}, bf16[128,512]{1,0:T(8,128)(2,1)S(1)}, u32[]{:S(2)}, u32[]{:S(2)}) collective-permute-start(bf16[128,512]{1,0:T(8,128)(2,1)S(1)} %add_convert_fusion.lower_ref), channel_id=1, source_target_pairs={{0,64},{64,0},{128,192},{192,128},{1,65},{65,1},{129,193},{193,129... | collective-permute-start | bytes 393224 | tf_op jit(solution)/shard_map/ppermute | solution.py:309
Sparse Core Ops, SparseCore 0:
  10.1 104.2 all-gather.2

commit v5 on v4

--- a/solution.py
+++ b/solution.py
@@ -216,8 +216,8 @@
 
 
 def rows_kernel(
-    count_ref, place_ref, values_ref, cores_ref, panels_ref, upper_ref, lower_ref, sums_ref, panel_ref, core_ref,
-    sem, core_sem
+    count_ref, place_ref, values_ref, cores_ref, panels_ref, own_ref, first_ref, second_ref, third_ref, sums_ref,
+    panel_ref, core_ref, total_ref, sem, core_sem
 ):
     def fetch(owner):
         start = pl.multiple_of((place_ref[0, owner] % 2) * 128, 128)
@@ -259,21 +259,24 @@
         core = core_ref[k]
         total += product(sums_ref[k].astype(jnp.bfloat16), core, 1, 1)
         total += product(sums_ref[k + 8].astype(jnp.bfloat16), core, 1, 0)
-    rounded = total.astype(jnp.bfloat16)
-    upper_ref[...] = rounded[:128]
-    lower_ref[...] = rounded[128:]
+    total_ref[...] = total
+    for d, ref in enumerate((own_ref, first_ref, second_ref, third_ref)):
+        start = pl.multiple_of(((lax.axis_index("rel") + d) % 4) * 64, 64)
+        ref[...] = total_ref[pl.ds(start, 64), :].astype(ref.dtype)
 
 
 def partial_rows(count, place, values, cores, panels):
     return pl.pallas_call(
         rows_kernel,
-        out_shape=(jax.ShapeDtypeStruct((128, 512), jnp.bfloat16),) * 2,
+        out_shape=(jax.ShapeDtypeStruct((64, 512), jnp.float32),)
+        + (jax.ShapeDtypeStruct((64, 512), jnp.bfloat16),) * 3,
         in_specs=[IN_SMEM, IN_SMEM, IN_VMEM] + [pl.BlockSpec(memory_space=pltpu.HBM)] * 2,
-        out_specs=(IN_VMEM,) * 2,
+        out_specs=(IN_VMEM,) * 4,
         scratch_shapes=[
             pltpu.VMEM((16, 256, 512), jnp.float32),
             pltpu.VMEM((64, 128, 512), jnp.bfloat16),
             pltpu.VMEM(cores.shape, cores.dtype),
+            pltpu.VMEM((256, 512), jnp.float32),
             pltpu.SemaphoreType.DMA((64,)),
             pltpu.SemaphoreType.DMA,
         ],
@@ -282,31 +285,43 @@
     )(count, place, values, cores, panels)
 
 
-def finish_kernel(upper_ref, upper_other_ref, lower_ref, lower_other_ref, inverse_ref, out_ref):
+def finish_kernel(own_ref, first_ref, second_ref, third_ref, inverse_ref, out_ref):
     wide = lambda ref: ref[...].astype(jnp.float32)
-    upper = wide(upper_ref) + wide(upper_other_ref)
-    lower = wide(lower_ref) + wide(lower_other_ref)
-    rows = jnp.concatenate([upper, lower], axis=0)
-    out_ref[...] = jnp.dot(rows, inverse_ref[...], precision=HIGHEST, preferred_element_type=jnp.float32)
-
-
-def finish(upper, upper_other, lower, lower_other, inverted):
+    rows = (wide(own_ref) + wide(second_ref)) + (wide(first_ref) + wide(third_ref))
+    solved = jnp.dot(rows, inverse_ref[...], precision=HIGHEST, preferred_element_type=jnp.float32)
+    out_ref[...] = solved.astype(jnp.bfloat16)
+
+
+def finish(own, arrived, inverted):
     return pl.pallas_call(
         finish_kernel,
-        out_shape=jax.ShapeDtypeStruct((256, 512), jnp.float32),
+        out_shape=jax.ShapeDtypeStruct(own.shape, jnp.bfloat16),
         in_specs=[IN_VMEM] * 5,
         out_specs=IN_VMEM,
         compiler_params=pltpu.CompilerParams(vmem_limit_bytes=16 * MIB),
-        cost_estimate=pl.CostEstimate(flops=1000000000, bytes_accessed=2500000, transcendentals=0),
-    )(upper, upper_other, lower, lower_other, inverted)
+        cost_estimate=pl.CostEstimate(flops=300000000, bytes_accessed=1500000, transcendentals=0),
+    )(own, *arrived, inverted)
+
+
+def assemble_kernel(own_ref, first_ref, second_ref, third_ref, out_ref):
+    for d, ref in enumerate((own_ref, first_ref, second_ref, third_ref)):
+        start = pl.multiple_of(((lax.axis_index("rel") - d + 4) % 4) * 64, 64)
+        out_ref[pl.ds(start, 64), :] = ref[...].astype(jnp.float32)
+
+
+def assemble(own, arrived):
+    return pl.pallas_call(
+        assemble_kernel,
+        out_shape=jax.ShapeDtypeStruct((256, 512), jnp.float32),
+        in_specs=[IN_VMEM] * 4,
+        out_specs=IN_VMEM,
+        compiler_params=pltpu.CompilerParams(vmem_limit_bytes=16 * MIB),
+        cost_estimate=pl.CostEstimate(flops=100000, bytes_accessed=800000, transcendentals=0),
+    )(own, *arrived)
 
 
 def over_y(v, d):
     return lax.ppermute(v, "rel", [(y, (y + d) % 4) for y in range(4)])
-
-
-def swap_y(v, bits):
-    return lax.ppermute(v, "rel", [(y, y ^ bits) for y in range(4)])
 
 
 def over_x(v, d):
@@ -347,10 +362,9 @@
     inverted = inverse(*sum_everywhere(system_term(factor, core_tensors)))
     values, place = align(tile_rel[0], tile_block[0], tile_col[0], tile_flip[0], tile_values[0])
     panels, inverted, values, place = lax.optimization_barrier((panels, inverted, values, place))
-    upper, lower = partial_rows(tile_count[0], place, values, core_tensors, panels)
-    add = lambda a, b: (a.astype(jnp.float32) + b.astype(jnp.float32)).astype(jnp.bfloat16)
-    upper, lower = add(upper, swap_y(upper, 1)), add(lower, swap_y(lower, 3))
-    return finish(upper, swap_y(upper, 3), lower, swap_y(lower, 1), inverted)
+    own, *others = partial_rows(tile_count[0], place, values, core_tensors, panels)
+    own = finish(own, [over_y(other, d + 1) for d, other in enumerate(others)], inverted)
+    return assemble(own, [over_y(own, d) for d in (1, 2, 3)])
 
 
 def solution(mesh):

time: 143 us -> 147 us (1.028); the launches traced: 143 us -> 146 us
  starting transfers between devices: 39.4 us -> 41.7 us
    ppermute x6 -> x12, starting transfers between devices: 5.27 us -> 13 us  [over_y(): return lax.ppermute(v, 'rel', [(y, (y + d) % 4) for y in range(4)])]
    ppermute x6 -> x12, waiting for transfers between devices: 8.99 us -> 15.7 us  [over_y(): return lax.ppermute(v, 'rel', [(y, (y + d) % 4) for y in range(4)])]
    ppermute x4 -> x0, waiting for transfers between devices: 6.16 us -> none  [swap_y(): return lax.ppermute(v, 'rel', [(y, y ^ bits) for y in range(4)])]
    ppermute x4 -> x0, starting transfers between devices: 5.43 us -> none  [swap_y(): return lax.ppermute(v, 'rel', [(y, y ^ bits) for y in range(4)])]
    pallas_call x2 -> x3, Pallas kernels: 10.2 us -> 9.94 us  [the longest x1 8.37 us: partial_rows(): pl.pallas_call(rows_kernel, out_shape=(jax.ShapeDtypeStruct((64, 512), jn...]
  transfers between devices with their start and end apart: 23 -> 25, of which waited for: 15 -> 17; matrix products, arithmetic and copies ran while one was open for 0% -> 0% of each run, Pallas kernels for 29% -> 28%
where the time goes in v5:
time: 147 us; the launch traced here: 146 us
  Pallas kernels  50.8 us (35%)
  starting transfers between devices  41.7 us (28%)
  waiting for transfers between devices  37.7 us (26%)
  between operations  14.2 us (10%)
    pallas_call x1, Pallas kernels, inverse(): pl.pallas_call(inverse_kernel, out_shape=jax.ShapeDtypeStruct((512, 512),...  27.1 us
    ppermute x12, waiting for transfers between devices, over_y(): return lax.ppermute(v, 'rel', [(y, (y + d) % 4) for y in range(4)])  15.7 us
    ppermute x12, starting transfers between devices, over_y(): return lax.ppermute(v, 'rel', [(y, (y + d) % 4) for y in range(4)])  13 us
    ppermute x2, starting transfers between devices, swap_core(): return lax.ppermute(v, 'ent', [(e, e ^ 1) for e in range(64)])  11.4 us
    pallas_call x1, Pallas kernels, system_term(): pl.pallas_call(system_kernel, out_shape=jax.ShapeDtypeStruct((1280, 128),...  10.4 us
    ppermute x4, starting transfers between devices, swap_z(): return lax.ppermute(v, 'ent', [(e, e ^ 2 * bits) for e in range(64)])  9.61 us
    pallas_call x1, Pallas kernels, partial_rows(): pl.pallas_call(rows_kernel, out_shape=(jax.ShapeDtypeStruct((64, 512), jn...  8.37 us
    ppermute x4, waiting for transfers between devices, swap_z(): return lax.ppermute(v, 'ent', [(e, e ^ 2 * bits) for e in range(64)])  7.75 us
  transfers between devices with their start and end apart: 25, of which 17 were waited for; matrix products, arithmetic and copies ran while one was open for 0% of the time, Pallas kernels for 28%

profile of v5, /device:TPU:1, one launch (start us, length us, event | category | flops | bytes accessed | tf_op | source)
XLA Modules:
  0.0 145.6 jit_solution(2731239045480951011)
XLA Ops:
  6.5 0.0 all-gather.3.cloned.1.call-start
  6.5 0.7 all-gather.3.cloned.1.call-update
  7.3 0.0 copy-start
  7.3 0.9 copy-done
  8.2 10.4 %shard_map.82 = f32[1280,128]{1,0:T(8,128)S(1)} custom-call(bf16[256,512]{1,0:T(8,128)(2,1)S(1)} %copy-done, bf16[8,512,512]{2,1,0:T(8,128)(2,1)} %cores_ref.3), custom_call_target="tpu_custom_call" | custom-call | flops 12000000000 | bytes 5000000 | tf_op jit(solution)/shard_map/pallas_call | solution.py:68
  18.7 3.3 %collective-permute-start = (f32[640,128]{1,0:T(8,128)S(1)}, f32[640,128]{1,0:T(8,128)S(1)}, u32[]{:S(2)}, u32[]{:S(2)}) collective-permute-start(f32[640,128]{1,0:T(8,128)S(1)} %slice.41), channel_id=1, source_target_pairs={{0,1},{1,0},{2,3},{3,2},{4,5},{5,4},{6,7},{7,6},{8,9},{9,8},{10,11... | collective-permute-start | bytes 983048 | tf_op jit(solution)/shard_map/ppermute | solution.py:336
  22.0 1.3 collective-permute-done
  23.3 1.1 collective-permute-start.3
  24.4 0.5 collective-permute-start.2
  24.9 1.2 collective-permute-start.1
  26.1 1.0 collective-permute-done.3
  27.1 2.0 %collective-permute-done.2 = f32[160,128]{1,0:T(8,128)S(1)} collective-permute-done((f32[160,128]{1,0:T(8,128)S(1)}, f32[160,128]{1,0:T(8,128)S(1)}, u32[]{:S(2)}, u32[]{:S(2)}) %collective-permute-start.2) | collective-permute-done | bytes 81952 | tf_op jit(solution)/shard_map/ppermute | solution.py:324
  29.1 0.9 collective-permute-done.1
  30.0 3.0 %collective-permute-start.6 = (f32[40,128]{1,0:T(8,128)S(1)}, f32[40,128]{1,0:T(8,128)S(1)}, u32[]{:S(2)}, u32[]{:S(2)}) collective-permute-start(f32[40,128]{1,0:T(8,128)S(1)} %get-tuple-element.30), channel_id=1, source_target_pairs={{0,48},{1,49},{2,50},{3,51},{4,52},{5,53},{6,54},{7,55},{8,56},{9,... | collective-permute-start | bytes 61448 | tf_op jit(solution)/shard_map/ppermute | solution.py:328
  33.0 0.0 collective-permute-start.5
  33.0 1.7 %collective-permute-start.4 = (f32[40,128]{1,0:T(8,128)S(1)}, f32[40,128]{1,0:T(8,128)S(1)}, u32[]{:S(2)}, u32[]{:S(2)}) collective-permute-start(f32[40,128]{1,0:T(8,128)S(1)} %get-tuple-element.32), channel_id=1, source_target_pairs={{0,32},{1,33},{2,34},{3,35},{4,36},{5,37},{6,38},{7,39},{8,40},{9,... | collective-permute-start | bytes 61448 | tf_op jit(solution)/shard_map/ppermute | solution.py:328
  34.7 0.0 collective-permute-done.6
  34.7 2.8 %collective-permute-done.5 = f32[40,128]{1,0:T(8,128)S(1)} collective-permute-done((f32[40,128]{1,0:T(8,128)S(1)}, f32[40,128]{1,0:T(8,128)S(1)}, u32[]{:S(2)}, u32[]{:S(2)}) %collective-permute-start.5) | collective-permute-done | bytes 20512 | tf_op jit(solution)/shard_map/ppermute | solution.py:328
  37.5 0.0 collective-permute-done.4
  37.6 1.3 collective-permute-start.7
  38.8 1.8 %collective-permute-done.7 = f32[40,128]{1,0:T(8,128)S(1)} collective-permute-done((f32[40,128]{1,0:T(8,128)S(1)}, f32[40,128]{1,0:T(8,128)S(1)}, u32[]{:S(2)}, u32[]{:S(2)}) %collective-permute-start.7) | collective-permute-done | bytes 20512 | tf_op jit(solution)/shard_map/ppermute | solution.py:332
  40.7 6.1 %collective-permute-start.10 = (f32[40,128]{1,0:T(8,128)S(1)}, f32[40,128]{1,0:T(8,128)S(1)}, u32[]{:S(2)}, u32[]{:S(2)}) collective-permute-start(f32[40,128]{1,0:T(8,128)S(1)} %add.40), channel_id=1, source_target_pairs={{0,12},{1,13},{2,14},{3,15},{4,8},{5,9},{6,10},{7,11},{8,4},{9,5},... | collective-permute-start | bytes 61448 | tf_op jit(solution)/shard_map/ppermute | solution.py:332
  46.8 1.1 collective-permute-start.9
  47.9 1.1 collective-permute-start.8
  49.0 0.0 collective-permute-done.10
  49.0 1.4 collective-permute-done.9
  50.4 4.6 %collective-permute-done.8 = f32[40,128]{1,0:T(8,128)S(1)} collective-permute-done((f32[40,128]{1,0:T(8,128)S(1)}, f32[40,128]{1,0:T(8,128)S(1)}, u32[]{:S(2)}, u32[]{:S(2)}) %collective-permute-start.8) | collective-permute-done | bytes 20512 | tf_op jit(solution)/shard_map/ppermute | solution.py:332
  54.9 2.3 %collective-permute-start.13 = (f32[40,128]{1,0:T(8,128)S(1)}, f32[40,128]{1,0:T(8,128)S(1)}, u32[]{:S(2)}, u32[]{:S(2)}) collective-permute-start(f32[40,128]{1,0:T(8,128)S(1)} %get-tuple-element.26), channel_id=1, source_target_pairs={{0,48},{1,49},{2,50},{3,51},{4,52},{5,53},{6,54},{7,55},{8,56},{9,... | collective-permute-start | bytes 61448 | tf_op jit(solution)/shard_map/ppermute | solution.py:328
  57.3 0.0 collective-permute-start.12
  57.3 0.7 collective-permute-start.11
  57.9 0.2 collective-permute-done.13
  58.2 3.2 %collective-permute-done.12 = f32[40,128]{1,0:T(8,128)S(1)} collective-permute-done((f32[40,128]{1,0:T(8,128)S(1)}, f32[40,128]{1,0:T(8,128)S(1)}, u32[]{:S(2)}, u32[]{:S(2)}) %collective-permute-start.12) | collective-permute-done | bytes 20512 | tf_op jit(solution)/shard_map/ppermute | solution.py:328
  61.4 0.0 collective-permute-done.11
  61.4 1.6 %collective-permute-start.16 = (f32[160,128]{1,0:T(8,128)S(1)}, f32[160,128]{1,0:T(8,128)S(1)}, u32[]{:S(2)}, u32[]{:S(2)}) collective-permute-start(f32[160,128]{1,0:T(8,128)S(1)} %pad_maximum_fusion), channel_id=1, source_target_pairs={{0,192},{64,0},{128,64},{192,128},{1,193},{65,1},{129,65},{193,129... | collective-permute-start | bytes 245768 | tf_op jit(solution)/shard_map/ppermute | solution.py:324
  63.0 0.4 collective-permute-start.15
  63.4 0.5 collective-permute-start.14
  64.0 5.1 %collective-permute-done.14 = f32[160,128]{1,0:T(8,128)S(1)} collective-permute-done((f32[160,128]{1,0:T(8,128)S(1)}, f32[160,128]{1,0:T(8,128)S(1)}, u32[]{:S(2)}, u32[]{:S(2)}) %collective-permute-start.14) | collective-permute-done | bytes 81952 | tf_op jit(solution)/shard_map/ppermute | solution.py:324
  69.1 0.0 collective-permute-done.15
  69.1 0.0 collective-permute-done.16
  69.1 8.0 %collective-permute-start.17 = (f32[640,128]{1,0:T(8,128)S(1)}, f32[640,128]{1,0:T(8,128)S(1)}, u32[]{:S(2)}, u32[]{:S(2)}) collective-permute-start(f32[640,128]{1,0:T(8,128)S(1)} %constant_dynamic-update-slice_fusion.own_ref), channel_id=1, source_target_pairs={{0,1},{1,0},{2,3},{3,2},{4,5},{5,4},{6,7},{7,6},{8,9},{9,8},{10,11... | collective-permute-start | bytes 983048 | tf_op jit(solution)/shard_map/ppermute | solution.py:336
  77.8 0.0 copy-done.1
  77.8 0.0 copy-done.2
  77.8 0.0 copy-done.3
  77.9 0.0 copy-done.4
  77.9 0.0 copy-done.5
  77.9 3.3 %shard_map.84 = (bf16[72,128,128]{2,1,0:T(8,128)(2,1)S(1)}, s32[3,72]{1,0:T(4,128)S(1)}) custom-call(s32[72]{0:T(128)S(1)} %bitcast.9, s32[72]{0:T(128)S(1)} %bitcast.10, s32[72]{0:T(128)S(1)} %bitcast.11, s32[72]{0:T(128)S(1)} %bitcast.12, bf16[72,128,128]{2,1,0:T(8,128)(2,1)S(1)} %bitcast.8), custom_call_target="tpu_custom_call" | custom-call | flops 3000000000 | bytes 4800000 | tf_op jit(solution)/shard_map/pallas_call | solution.py:204
  81.2 0.0 collective-permute-done.17.other_ref
  81.2 27.1 %shard_map.83.inverse_ref = f32[512,512]{1,0:T(8,128)S(1)} custom-call(f32[640,128]{1,0:T(8,128)S(1)} %constant_dynamic-update-slice_fusion.own_ref, f32[640,128]{1,0:T(8,128)S(1)} %collective-permute-done.17.other_ref), custom_call_target="tpu_custom_call" | custom-call | flops 30000001024 | bytes 2000000 | tf_op jit(solution)/shard_map/pallas_call | solution.py:169
  108.3 6.1 %all-gather.3.cloned.1.call-done = bf16[16384,512]{1,0:T(8,128)(2,1)} async-done(((bf16[256,512]{1,0:T(8,128)(2,1)}), bf16[16384,512]{1,0:T(8,128)(2,1)}) %all-gather.3.cloned.1.call-update) | async-done | bytes 16777232 | tf_op jit(solution)/shard_map/all_gather | solution.py:361
  114.4 8.4 %shard_map.85 = (f32[64,512]{1,0:T(8,128)S(1)}, bf16[64,512]{1,0:T(8,128)(2,1)S(1)}, bf16[64,512]{1,0:T(8,128)(2,1)S(1)}, bf16[64,512]{1,0:T(8,128)(2,1)S(1)}) custom-call(s32[1]{0:T(128)} %bitcast.7.count_ref, s32[3,72]{1,0:T(4,128)S(1)} %get-tuple-element.17.place_ref, bf16[72,128,128]{2,1,0:T(8,128)(2,1)S(1)} %get-tuple-element.18.values_ref, ...), custom_call_target="tpu_custom_call" | custom-call | flops 10000000000 | bytes 16000000 | tf_op jit(solution)/shard_map/pallas_call | solution.py:269
  122.8 1.7 %collective-permute-start.18 = (bf16[64,512]{1,0:T(8,128)(2,1)S(1)}, bf16[64,512]{1,0:T(8,128)(2,1)S(1)}, u32[]{:S(2)}, u32[]{:S(2)}) collective-permute-start(bf16[64,512]{1,0:T(8,128)(2,1)S(1)} %get-tuple-element.21), channel_id=1, source_target_pairs={{0,64},{64,128},{128,192},{192,0},{1,65},{65,129},{129,193},{193,1... | collective-permute-start | bytes 196616 | tf_op jit(solution)/shard_map/ppermute | solution.py:324
  124.5 2.1 %collective-permute-start.19 = (bf16[64,512]{1,0:T(8,128)(2,1)S(1)}, bf16[64,512]{1,0:T(8,128)(2,1)S(1)}, u32[]{:S(2)}, u32[]{:S(2)}) collective-permute-start(bf16[64,512]{1,0:T(8,128)(2,1)S(1)} %get-tuple-element.22), channel_id=1, source_target_pairs={{0,128},{64,192},{128,0},{192,64},{1,129},{65,193},{129,1},{193,65... | collective-permute-start | bytes 196616 | tf_op jit(solution)/shard_map/ppermute | solution.py:324
  126.6 1.1 collective-permute-start.20
  127.7 0.0 collective-permute-done.18.first_ref
  127.7 2.1 %collective-permute-done.19.second_ref = bf16[64,512]{1,0:T(8,128)(2,1)S(1)} collective-permute-done((bf16[64,512]{1,0:T(8,128)(2,1)S(1)}, bf16[64,512]{1,0:T(8,128)(2,1)S(1)}, u32[]{:S(2)}, u32[]{:S(2)}) %collective-permute-start.19) | collective-permute-done | bytes 65568 | tf_op jit(solution)/shard_map/ppermute | solution.py:324
  129.8 0.2 collective-permute-done.20.third_ref
  130.0 0.7 shard_map.86.own_ref
  130.7 2.2 %collective-permute-start.23 = (bf16[64,512]{1,0:T(8,128)(2,1)S(1)}, bf16[64,512]{1,0:T(8,128)(2,1)S(1)}, u32[]{:S(2)}, u32[]{:S(2)}) collective-permute-start(bf16[64,512]{1,0:T(8,128)(2,1)S(1)} %shard_map.86.own_ref), channel_id=1, source_target_pairs={{0,192},{64,0},{128,64},{192,128},{1,193},{65,1},{129,65},{193,129... | collective-permute-start | bytes 196616 | tf_op jit(solution)/shard_map/ppermute | solution.py:324
  132.9 0.0 collective-permute-start.22
  132.9 0.7 collective-permute-start.21
  133.6 0.7 collective-permute-done.23.third_ref
  134.2 3.4 %collective-permute-done.22.second_ref = bf16[64,512]{1,0:T(8,128)(2,1)S(1)} collective-permute-done((bf16[64,512]{1,0:T(8,128)(2,1)S(1)}, bf16[64,512]{1,0:T(8,128)(2,1)S(1)}, u32[]{:S(2)}, u32[]{:S(2)}) %collective-permute-start.22) | collective-permute-done | bytes 65568 | tf_op jit(solution)/shard_map/ppermute | solution.py:324
  137.6 0.3 collective-permute-done.21.first_ref
  137.9 0.8 shard_map.87
  (20 shorter events, 0.2 us)
Async XLA Ops:
  6.5 107.9 %all-gather.3.cloned.1.call-start = ((), (), s32[]{:S(2)}) async-start(), calls=%async_computation | async-start | bytes 17039360 | tf_op jit(solution)/shard_map/all_gather | solution.py:361
  7.3 1.0 copy-start
  8.2 69.6 %copy-start.1 = (bf16[1,72,128,128]{3,2,1,0:T(8,128)(2,1)S(1)}, bf16[1,72,128,128]{3,2,1,0:T(8,128)(2,1)}, u32[]{:S(2)}) copy-start(bf16[1,72,128,128]{3,2,1,0:T(8,128)(2,1)} %param.10) | copy-start | bytes 7077892
  8.2 69.6 %copy-start.2 = (s32[1,72]{1,0:T(1,128)S(1)}, s32[1,72]{1,0:T(1,128)}, u32[]{:S(2)}) copy-start(s32[1,72]{1,0:T(1,128)} %param.11) | copy-start | bytes 868
  8.2 69.6 %copy-start.3 = (s32[1,72]{1,0:T(1,128)S(1)}, s32[1,72]{1,0:T(1,128)}, u32[]{:S(2)}) copy-start(s32[1,72]{1,0:T(1,128)} %param.12) | copy-start | bytes 868
  8.2 69.6 %copy-start.4 = (s32[1,72]{1,0:T(1,128)S(1)}, s32[1,72]{1,0:T(1,128)}, u32[]{:S(2)}) copy-start(s32[1,72]{1,0:T(1,128)} %param.13) | copy-start | bytes 868
  8.2 69.7 %copy-start.5 = (s32[1,72]{1,0:T(1,128)S(1)}, s32[1,72]{1,0:T(1,128)}, u32[]{:S(2)}) copy-start(s32[1,72]{1,0:T(1,128)} %param.14) | copy-start | bytes 868
  18.7 4.6 %collective-permute-start = (f32[640,128]{1,0:T(8,128)S(1)}, f32[640,128]{1,0:T(8,128)S(1)}, u32[]{:S(2)}, u32[]{:S(2)}) collective-permute-start(f32[640,128]{1,0:T(8,128)S(1)} %slice.41), channel_id=1, source_target_pairs={{0,1},{1,0},{2,3},{3,2},{4,5},{5,4},{6,7},{7,6},{8,9},{9,8},{10,11... | collective-permute-start | bytes 983048 | tf_op jit(solution)/shard_map/ppermute | solution.py:336
  23.3 3.7 %collective-permute-start.3 = (f32[160,128]{1,0:T(8,128)S(1)}, f32[160,128]{1,0:T(8,128)S(1)}, u32[]{:S(2)}, u32[]{:S(2)}) collective-permute-start(f32[160,128]{1,0:T(8,128)S(1)} %get-tuple-element.27), channel_id=1, source_target_pairs={{0,192},{64,0},{128,64},{192,128},{1,193},{65,1},{129,65},{193,129... | collective-permute-start | bytes 245768 | tf_op jit(solution)/shard_map/ppermute | solution.py:324
  24.4 4.7 %collective-permute-start.2 = (f32[160,128]{1,0:T(8,128)S(1)}, f32[160,128]{1,0:T(8,128)S(1)}, u32[]{:S(2)}, u32[]{:S(2)}) collective-permute-start(f32[160,128]{1,0:T(8,128)S(1)} %get-tuple-element.28), channel_id=1, source_target_pairs={{0,64},{64,128},{128,192},{192,0},{1,65},{65,129},{129,193},{193,1... | collective-permute-start | bytes 245768 | tf_op jit(solution)/shard_map/ppermute | solution.py:324
  24.9 5.1 %collective-permute-start.1 = (f32[160,128]{1,0:T(8,128)S(1)}, f32[160,128]{1,0:T(8,128)S(1)}, u32[]{:S(2)}, u32[]{:S(2)}) collective-permute-start(f32[160,128]{1,0:T(8,128)S(1)} %get-tuple-element.29), channel_id=1, source_target_pairs={{0,128},{64,192},{128,0},{192,64},{1,129},{65,193},{129,1},{193,65... | collective-permute-start | bytes 245768 | tf_op jit(solution)/shard_map/ppermute | solution.py:324
  30.0 4.7 %collective-permute-start.6 = (f32[40,128]{1,0:T(8,128)S(1)}, f32[40,128]{1,0:T(8,128)S(1)}, u32[]{:S(2)}, u32[]{:S(2)}) collective-permute-start(f32[40,128]{1,0:T(8,128)S(1)} %get-tuple-element.30), channel_id=1, source_target_pairs={{0,48},{1,49},{2,50},{3,51},{4,52},{5,53},{6,54},{7,55},{8,56},{9,... | collective-permute-start | bytes 61448 | tf_op jit(solution)/shard_map/ppermute | solution.py:328
  33.0 4.6 %collective-permute-start.5 = (f32[40,128]{1,0:T(8,128)S(1)}, f32[40,128]{1,0:T(8,128)S(1)}, u32[]{:S(2)}, u32[]{:S(2)}) collective-permute-start(f32[40,128]{1,0:T(8,128)S(1)} %get-tuple-element.31), channel_id=1, source_target_pairs={{0,16},{1,17},{2,18},{3,19},{4,20},{5,21},{6,22},{7,23},{8,24},{9,... | collective-permute-start | bytes 61448 | tf_op jit(solution)/shard_map/ppermute | solution.py:328
  33.0 4.6 %collective-permute-start.4 = (f32[40,128]{1,0:T(8,128)S(1)}, f32[40,128]{1,0:T(8,128)S(1)}, u32[]{:S(2)}, u32[]{:S(2)}) collective-permute-start(f32[40,128]{1,0:T(8,128)S(1)} %get-tuple-element.32), channel_id=1, source_target_pairs={{0,32},{1,33},{2,34},{3,35},{4,36},{5,37},{6,38},{7,39},{8,40},{9,... | collective-permute-start | bytes 61448 | tf_op jit(solution)/shard_map/ppermute | solution.py:328
  37.6 3.1 %collective-permute-start.7 = (f32[40,128]{1,0:T(8,128)S(1)}, f32[40,128]{1,0:T(8,128)S(1)}, u32[]{:S(2)}, u32[]{:S(2)}) collective-permute-start(f32[40,128]{1,0:T(8,128)S(1)} %fusion.1), channel_id=1, source_target_pairs={{0,2},{1,3},{2,0},{3,1},{4,6},{5,7},{6,4},{7,5},{8,10},{9,11},{10,... | collective-permute-start | bytes 61448 | tf_op jit(solution)/shard_map/ppermute | solution.py:332
  40.7 8.3 %collective-permute-start.10 = (f32[40,128]{1,0:T(8,128)S(1)}, f32[40,128]{1,0:T(8,128)S(1)}, u32[]{:S(2)}, u32[]{:S(2)}) collective-permute-start(f32[40,128]{1,0:T(8,128)S(1)} %add.40), channel_id=1, source_target_pairs={{0,12},{1,13},{2,14},{3,15},{4,8},{5,9},{6,10},{7,11},{8,4},{9,5},... | collective-permute-start | bytes 61448 | tf_op jit(solution)/shard_map/ppermute | solution.py:332
  46.8 3.5 %collective-permute-start.9 = (f32[40,128]{1,0:T(8,128)S(1)}, f32[40,128]{1,0:T(8,128)S(1)}, u32[]{:S(2)}, u32[]{:S(2)}) collective-permute-start(f32[40,128]{1,0:T(8,128)S(1)} %add.40), channel_id=1, source_target_pairs={{0,4},{1,5},{2,6},{3,7},{4,0},{5,1},{6,2},{7,3},{8,12},{9,13},{10,... | collective-permute-start | bytes 61448 | tf_op jit(solution)/shard_map/ppermute | solution.py:332
  47.9 7.0 %collective-permute-start.8 = (f32[40,128]{1,0:T(8,128)S(1)}, f32[40,128]{1,0:T(8,128)S(1)}, u32[]{:S(2)}, u32[]{:S(2)}) collective-permute-start(f32[40,128]{1,0:T(8,128)S(1)} %add.40), channel_id=1, source_target_pairs={{0,8},{1,9},{2,10},{3,11},{4,12},{5,13},{6,14},{7,15},{8,0},{9,1},... | collective-permute-start | bytes 61448 | tf_op jit(solution)/shard_map/ppermute | solution.py:332
  54.9 3.2 %collective-permute-start.13 = (f32[40,128]{1,0:T(8,128)S(1)}, f32[40,128]{1,0:T(8,128)S(1)}, u32[]{:S(2)}, u32[]{:S(2)}) collective-permute-start(f32[40,128]{1,0:T(8,128)S(1)} %get-tuple-element.26), channel_id=1, source_target_pairs={{0,48},{1,49},{2,50},{3,51},{4,52},{5,53},{6,54},{7,55},{8,56},{9,... | collective-permute-start | bytes 61448 | tf_op jit(solution)/shard_map/ppermute | solution.py:328
  57.3 4.1 %collective-permute-start.12 = (f32[40,128]{1,0:T(8,128)S(1)}, f32[40,128]{1,0:T(8,128)S(1)}, u32[]{:S(2)}, u32[]{:S(2)}) collective-permute-start(f32[40,128]{1,0:T(8,128)S(1)} %get-tuple-element.26), channel_id=1, source_target_pairs={{0,32},{1,33},{2,34},{3,35},{4,36},{5,37},{6,38},{7,39},{8,40},{9,... | collective-permute-start | bytes 61448 | tf_op jit(solution)/shard_map/ppermute | solution.py:328
  57.3 4.1 %collective-permute-start.11 = (f32[40,128]{1,0:T(8,128)S(1)}, f32[40,128]{1,0:T(8,128)S(1)}, u32[]{:S(2)}, u32[]{:S(2)}) collective-permute-start(f32[40,128]{1,0:T(8,128)S(1)} %get-tuple-element.26), channel_id=1, source_target_pairs={{0,16},{1,17},{2,18},{3,19},{4,20},{5,21},{6,22},{7,23},{8,24},{9,... | collective-permute-start | bytes 61448 | tf_op jit(solution)/shard_map/ppermute | solution.py:328
  61.4 7.7 %collective-permute-start.16 = (f32[160,128]{1,0:T(8,128)S(1)}, f32[160,128]{1,0:T(8,128)S(1)}, u32[]{:S(2)}, u32[]{:S(2)}) collective-permute-start(f32[160,128]{1,0:T(8,128)S(1)} %pad_maximum_fusion), channel_id=1, source_target_pairs={{0,192},{64,0},{128,64},{192,128},{1,193},{65,1},{129,65},{193,129... | collective-permute-start | bytes 245768 | tf_op jit(solution)/shard_map/ppermute | solution.py:324
  63.0 6.1 %collective-permute-start.15 = (f32[160,128]{1,0:T(8,128)S(1)}, f32[160,128]{1,0:T(8,128)S(1)}, u32[]{:S(2)}, u32[]{:S(2)}) collective-permute-start(f32[160,128]{1,0:T(8,128)S(1)} %pad_maximum_fusion), channel_id=1, source_target_pairs={{0,128},{64,192},{128,0},{192,64},{1,129},{65,193},{129,1},{193,65... | collective-permute-start | bytes 245768 | tf_op jit(solution)/shard_map/ppermute | solution.py:324
  63.4 5.7 %collective-permute-start.14 = (f32[160,128]{1,0:T(8,128)S(1)}, f32[160,128]{1,0:T(8,128)S(1)}, u32[]{:S(2)}, u32[]{:S(2)}) collective-permute-start(f32[160,128]{1,0:T(8,128)S(1)} %pad_maximum_fusion), channel_id=1, source_target_pairs={{0,64},{64,128},{128,192},{192,0},{1,65},{65,129},{129,193},{193,1... | collective-permute-start | bytes 245768 | tf_op jit(solution)/shard_map/ppermute | solution.py:324
  69.1 12.0 %collective-permute-start.17 = (f32[640,128]{1,0:T(8,128)S(1)}, f32[640,128]{1,0:T(8,128)S(1)}, u32[]{:S(2)}, u32[]{:S(2)}) collective-permute-start(f32[640,128]{1,0:T(8,128)S(1)} %constant_dynamic-update-slice_fusion.own_ref), channel_id=1, source_target_pairs={{0,1},{1,0},{2,3},{3,2},{4,5},{5,4},{6,7},{7,6},{8,9},{9,8},{10,11... | collective-permute-start | bytes 983048 | tf_op jit(solution)/shard_map/ppermute | solution.py:336
  122.8 4.9 %collective-permute-start.18 = (bf16[64,512]{1,0:T(8,128)(2,1)S(1)}, bf16[64,512]{1,0:T(8,128)(2,1)S(1)}, u32[]{:S(2)}, u32[]{:S(2)}) collective-permute-start(bf16[64,512]{1,0:T(8,128)(2,1)S(1)} %get-tuple-element.21), channel_id=1, source_target_pairs={{0,64},{64,128},{128,192},{192,0},{1,65},{65,129},{129,193},{193,1... | collective-permute-start | bytes 196616 | tf_op jit(solution)/shard_map/ppermute | solution.py:324
  124.5 5.3 %collective-permute-start.19 = (bf16[64,512]{1,0:T(8,128)(2,1)S(1)}, bf16[64,512]{1,0:T(8,128)(2,1)S(1)}, u32[]{:S(2)}, u32[]{:S(2)}) collective-permute-start(bf16[64,512]{1,0:T(8,128)(2,1)S(1)} %get-tuple-element.22), channel_id=1, source_target_pairs={{0,128},{64,192},{128,0},{192,64},{1,129},{65,193},{129,1},{193,65... | collective-permute-start | bytes 196616 | tf_op jit(solution)/shard_map/ppermute | solution.py:324
  126.6 3.4 %collective-permute-start.20 = (bf16[64,512]{1,0:T(8,128)(2,1)S(1)}, bf16[64,512]{1,0:T(8,128)(2,1)S(1)}, u32[]{:S(2)}, u32[]{:S(2)}) collective-permute-start(bf16[64,512]{1,0:T(8,128)(2,1)S(1)} %get-tuple-element.23), channel_id=1, source_target_pairs={{0,192},{64,0},{128,64},{192,128},{1,193},{65,1},{129,65},{193,129... | collective-permute-start | bytes 196616 | tf_op jit(solution)/shard_map/ppermute | solution.py:324
  130.7 3.5 %collective-permute-start.23 = (bf16[64,512]{1,0:T(8,128)(2,1)S(1)}, bf16[64,512]{1,0:T(8,128)(2,1)S(1)}, u32[]{:S(2)}, u32[]{:S(2)}) collective-permute-start(bf16[64,512]{1,0:T(8,128)(2,1)S(1)} %shard_map.86.own_ref), channel_id=1, source_target_pairs={{0,192},{64,0},{128,64},{192,128},{1,193},{65,1},{129,65},{193,129... | collective-permute-start | bytes 196616 | tf_op jit(solution)/shard_map/ppermute | solution.py:324
  132.9 4.7 %collective-permute-start.22 = (bf16[64,512]{1,0:T(8,128)(2,1)S(1)}, bf16[64,512]{1,0:T(8,128)(2,1)S(1)}, u32[]{:S(2)}, u32[]{:S(2)}) collective-permute-start(bf16[64,512]{1,0:T(8,128)(2,1)S(1)} %shard_map.86.own_ref), channel_id=1, source_target_pairs={{0,128},{64,192},{128,0},{192,64},{1,129},{65,193},{129,1},{193,65... | collective-permute-start | bytes 196616 | tf_op jit(solution)/shard_map/ppermute | solution.py:324
  132.9 5.0 %collective-permute-start.21 = (bf16[64,512]{1,0:T(8,128)(2,1)S(1)}, bf16[64,512]{1,0:T(8,128)(2,1)S(1)}, u32[]{:S(2)}, u32[]{:S(2)}) collective-permute-start(bf16[64,512]{1,0:T(8,128)(2,1)S(1)} %shard_map.86.own_ref), channel_id=1, source_target_pairs={{0,64},{64,128},{128,192},{192,0},{1,65},{65,129},{129,193},{193,1... | collective-permute-start | bytes 196616 | tf_op jit(solution)/shard_map/ppermute | solution.py:324
Sparse Core Ops, SparseCore 0:
  10.1 104.2 all-gather.2

commit v6 on v4

--- a/solution.py
+++ b/solution.py
@@ -14,6 +14,11 @@
 
 def product(a, b, a_dim, b_dim):
     return lax.dot_general(a, b, (((a_dim,), (b_dim,)), ((), ())), preferred_element_type=jnp.float32)
+
+
+def split(value):
+    high = value.astype(jnp.bfloat16)
+    return high, (value - high.astype(jnp.float32)).astype(jnp.bfloat16)
 
 
 def position():
@@ -240,13 +245,13 @@
         sums_ref[where] = sums_ref[where] + term
 
     def main(step, carry):
-        for i in range(8):
-            fetch(step * 8 + i).wait()
-        for i in range(8):
-            add(step * 8 + i, step * 8 + i)
-        return carry
-
-    lax.fori_loop(0, 8, main, 0)
+        for i in range(16):
+            fetch(step * 16 + i).wait()
+        for i in range(16):
+            add(step * 16 + i, step * 16 + i)
+        return carry
+
+    lax.fori_loop(0, 4, main, 0)
 
     def extra(index, carry):
         add(index, place_ref[0, index] // 2)
@@ -287,7 +292,10 @@
     upper = wide(upper_ref) + wide(upper_other_ref)
     lower = wide(lower_ref) + wide(lower_other_ref)
     rows = jnp.concatenate([upper, lower], axis=0)
-    out_ref[...] = jnp.dot(rows, inverse_ref[...], precision=HIGHEST, preferred_element_type=jnp.float32)
+    high, low = split(rows)
+    inverse_high, inverse_low = split(inverse_ref[...])
+    small = product(low, inverse_high, 1, 0) + product(high, inverse_low, 1, 0)
+    out_ref[...] = product(high, inverse_high, 1, 0) + small
 
 
 def finish(upper, upper_other, lower, lower_other, inverted):

time: 143 us -> 143 us (level)
  transfers between devices with their start and end apart: 23 -> 23, of which waited for: 15 -> 16; matrix products, arithmetic and copies ran while one was open for 0% -> 0% of each run, Pallas kernels for 29% -> 29%
where the time goes in v6:
time: 143 us; the launch traced here: 142 us
  Pallas kernels  50.6 us (35%)
  starting transfers between devices  39.6 us (28%)
  waiting for transfers between devices  36.4 us (25%)
  between operations  14.2 us (10%)
    pallas_call x1, Pallas kernels, inverse(): pl.pallas_call(inverse_kernel, out_shape=jax.ShapeDtypeStruct((512, 512),...  27.1 us
    ppermute x2, starting transfers between devices, swap_core(): return lax.ppermute(v, 'ent', [(e, e ^ 1) for e in range(64)])  11.4 us
    pallas_call x1, Pallas kernels, system_term(): pl.pallas_call(system_kernel, out_shape=jax.ShapeDtypeStruct((1280, 128),...  10.4 us
    ppermute x4, starting transfers between devices, swap_z(): return lax.ppermute(v, 'ent', [(e, e ^ 2 * bits) for e in range(64)])  9.61 us
    ppermute x6, waiting for transfers between devices, over_y(): return lax.ppermute(v, 'rel', [(y, (y + d) % 4) for y in range(4)])  8.99 us
    pallas_call x1, Pallas kernels, partial_rows(): pl.pallas_call(rows_kernel, out_shape=(jax.ShapeDtypeStruct((128, 512), j...  8.35 us
    ppermute x4, waiting for transfers between devices, swap_z(): return lax.ppermute(v, 'ent', [(e, e ^ 2 * bits) for e in range(64)])  7.75 us
    ppermute x6, starting transfers between devices, over_x(): return lax.ppermute(v, 'ent', [(e, (e + 16 * d) % 64) for e in range(64)])  7.74 us
  transfers between devices with their start and end apart: 23, of which 16 were waited for; matrix products, arithmetic and copies ran while one was open for 0% of the time, Pallas kernels for 29%

profile of v6, /device:TPU:1, one launch (start us, length us, event | category | flops | bytes accessed | tf_op | source)
XLA Modules:
  0.0 142.1 jit_solution(15200865980846672173)
XLA Ops:
  6.5 0.0 all-gather.3.cloned.1.call-start
  6.5 0.7 all-gather.3.cloned.1.call-update
  7.3 0.0 copy-start
  7.3 0.9 copy-done
  8.2 0.0 copy-start.1
  8.2 0.0 copy-start.2
  8.2 0.0 copy-start.3
  8.2 0.0 copy-start.4
  8.2 0.0 copy-start.5
  8.2 10.4 %shard_map.82 = f32[1280,128]{1,0:T(8,128)S(1)} custom-call(bf16[256,512]{1,0:T(8,128)(2,1)S(1)} %copy-done, bf16[8,512,512]{2,1,0:T(8,128)(2,1)} %cores_ref.3), custom_call_target="tpu_custom_call" | custom-call | flops 12000000000 | bytes 5000000 | tf_op jit(solution)/shard_map/pallas_call | solution.py:73
  18.7 3.3 %collective-permute-start = (f32[640,128]{1,0:T(8,128)S(1)}, f32[640,128]{1,0:T(8,128)S(1)}, u32[]{:S(2)}, u32[]{:S(2)}) collective-permute-start(f32[640,128]{1,0:T(8,128)S(1)} %slice.41), channel_id=1, source_target_pairs={{0,1},{1,0},{2,3},{3,2},{4,5},{5,4},{6,7},{7,6},{8,9},{9,8},{10,11... | collective-permute-start | bytes 983048 | tf_op jit(solution)/shard_map/ppermute | solution.py:329
  22.0 1.3 collective-permute-done
  23.3 1.1 collective-permute-start.3
  24.4 0.5 collective-permute-start.2
  24.9 1.2 collective-permute-start.1
  26.1 1.0 collective-permute-done.3
  27.1 2.0 %collective-permute-done.2 = f32[160,128]{1,0:T(8,128)S(1)} collective-permute-done((f32[160,128]{1,0:T(8,128)S(1)}, f32[160,128]{1,0:T(8,128)S(1)}, u32[]{:S(2)}, u32[]{:S(2)}) %collective-permute-start.2) | collective-permute-done | bytes 81952 | tf_op jit(solution)/shard_map/ppermute | solution.py:313
  29.1 0.9 collective-permute-done.1
  30.0 3.0 %collective-permute-start.6 = (f32[40,128]{1,0:T(8,128)S(1)}, f32[40,128]{1,0:T(8,128)S(1)}, u32[]{:S(2)}, u32[]{:S(2)}) collective-permute-start(f32[40,128]{1,0:T(8,128)S(1)} %get-tuple-element.26), channel_id=1, source_target_pairs={{0,48},{1,49},{2,50},{3,51},{4,52},{5,53},{6,54},{7,55},{8,56},{9,... | collective-permute-start | bytes 61448 | tf_op jit(solution)/shard_map/ppermute | solution.py:321
  33.0 0.0 collective-permute-start.5
  33.0 1.7 %collective-permute-start.4 = (f32[40,128]{1,0:T(8,128)S(1)}, f32[40,128]{1,0:T(8,128)S(1)}, u32[]{:S(2)}, u32[]{:S(2)}) collective-permute-start(f32[40,128]{1,0:T(8,128)S(1)} %get-tuple-element.28), channel_id=1, source_target_pairs={{0,32},{1,33},{2,34},{3,35},{4,36},{5,37},{6,38},{7,39},{8,40},{9,... | collective-permute-start | bytes 61448 | tf_op jit(solution)/shard_map/ppermute | solution.py:321
  34.7 0.0 collective-permute-done.6
  34.7 2.8 %collective-permute-done.5 = f32[40,128]{1,0:T(8,128)S(1)} collective-permute-done((f32[40,128]{1,0:T(8,128)S(1)}, f32[40,128]{1,0:T(8,128)S(1)}, u32[]{:S(2)}, u32[]{:S(2)}) %collective-permute-start.5) | collective-permute-done | bytes 20512 | tf_op jit(solution)/shard_map/ppermute | solution.py:321
  37.5 0.0 collective-permute-done.4
  37.6 1.3 collective-permute-start.7
  38.8 1.8 %collective-permute-done.7 = f32[40,128]{1,0:T(8,128)S(1)} collective-permute-done((f32[40,128]{1,0:T(8,128)S(1)}, f32[40,128]{1,0:T(8,128)S(1)}, u32[]{:S(2)}, u32[]{:S(2)}) %collective-permute-start.7) | collective-permute-done | bytes 20512 | tf_op jit(solution)/shard_map/ppermute | solution.py:325
  40.7 6.1 %collective-permute-start.10 = (f32[40,128]{1,0:T(8,128)S(1)}, f32[40,128]{1,0:T(8,128)S(1)}, u32[]{:S(2)}, u32[]{:S(2)}) collective-permute-start(f32[40,128]{1,0:T(8,128)S(1)} %add.46), channel_id=1, source_target_pairs={{0,12},{1,13},{2,14},{3,15},{4,8},{5,9},{6,10},{7,11},{8,4},{9,5},... | collective-permute-start | bytes 61448 | tf_op jit(solution)/shard_map/ppermute | solution.py:325
  46.8 1.1 collective-permute-start.9
  47.9 1.1 collective-permute-start.8
  49.0 0.0 collective-permute-done.10
  49.0 1.4 collective-permute-done.9
  50.4 4.6 %collective-permute-done.8 = f32[40,128]{1,0:T(8,128)S(1)} collective-permute-done((f32[40,128]{1,0:T(8,128)S(1)}, f32[40,128]{1,0:T(8,128)S(1)}, u32[]{:S(2)}, u32[]{:S(2)}) %collective-permute-start.8) | collective-permute-done | bytes 20512 | tf_op jit(solution)/shard_map/ppermute | solution.py:325
  54.9 2.3 %collective-permute-start.13 = (f32[40,128]{1,0:T(8,128)S(1)}, f32[40,128]{1,0:T(8,128)S(1)}, u32[]{:S(2)}, u32[]{:S(2)}) collective-permute-start(f32[40,128]{1,0:T(8,128)S(1)} %get-tuple-element.22), channel_id=1, source_target_pairs={{0,48},{1,49},{2,50},{3,51},{4,52},{5,53},{6,54},{7,55},{8,56},{9,... | collective-permute-start | bytes 61448 | tf_op jit(solution)/shard_map/ppermute | solution.py:321
  57.3 0.0 collective-permute-start.12
  57.3 0.7 collective-permute-start.11
  57.9 0.2 collective-permute-done.13
  58.2 3.2 %collective-permute-done.12 = f32[40,128]{1,0:T(8,128)S(1)} collective-permute-done((f32[40,128]{1,0:T(8,128)S(1)}, f32[40,128]{1,0:T(8,128)S(1)}, u32[]{:S(2)}, u32[]{:S(2)}) %collective-permute-start.12) | collective-permute-done | bytes 20512 | tf_op jit(solution)/shard_map/ppermute | solution.py:321
  61.4 0.0 collective-permute-done.11
  61.4 1.6 %collective-permute-start.16 = (f32[160,128]{1,0:T(8,128)S(1)}, f32[160,128]{1,0:T(8,128)S(1)}, u32[]{:S(2)}, u32[]{:S(2)}) collective-permute-start(f32[160,128]{1,0:T(8,128)S(1)} %pad_maximum_fusion), channel_id=1, source_target_pairs={{0,192},{64,0},{128,64},{192,128},{1,193},{65,1},{129,65},{193,129... | collective-permute-start | bytes 245768 | tf_op jit(solution)/shard_map/ppermute | solution.py:313
  63.0 0.4 collective-permute-start.15
  63.4 0.5 collective-permute-start.14
  64.0 5.1 %collective-permute-done.14 = f32[160,128]{1,0:T(8,128)S(1)} collective-permute-done((f32[160,128]{1,0:T(8,128)S(1)}, f32[160,128]{1,0:T(8,128)S(1)}, u32[]{:S(2)}, u32[]{:S(2)}) %collective-permute-start.14) | collective-permute-done | bytes 81952 | tf_op jit(solution)/shard_map/ppermute | solution.py:313
  69.1 0.0 collective-permute-done.15
  69.1 0.0 collective-permute-done.16
  69.1 8.0 %collective-permute-start.17 = (f32[640,128]{1,0:T(8,128)S(1)}, f32[640,128]{1,0:T(8,128)S(1)}, u32[]{:S(2)}, u32[]{:S(2)}) collective-permute-start(f32[640,128]{1,0:T(8,128)S(1)} %constant_dynamic-update-slice_fusion.own_ref), channel_id=1, source_target_pairs={{0,1},{1,0},{2,3},{3,2},{4,5},{5,4},{6,7},{7,6},{8,9},{9,8},{10,11... | collective-permute-start | bytes 983048 | tf_op jit(solution)/shard_map/ppermute | solution.py:329
  77.8 0.0 copy-done.1
  77.8 0.0 copy-done.2
  77.8 0.0 copy-done.3
  77.9 0.0 copy-done.4
  77.9 0.0 copy-done.5
  77.9 3.3 %shard_map.84 = (bf16[72,128,128]{2,1,0:T(8,128)(2,1)S(1)}, s32[3,72]{1,0:T(4,128)S(1)}) custom-call(s32[72]{0:T(128)S(1)} %bitcast.9, s32[72]{0:T(128)S(1)} %bitcast.10, s32[72]{0:T(128)S(1)} %bitcast.11, s32[72]{0:T(128)S(1)} %bitcast.12, bf16[72,128,128]{2,1,0:T(8,128)(2,1)S(1)} %bitcast.8), custom_call_target="tpu_custom_call" | custom-call | flops 3000000000 | bytes 4800000 | tf_op jit(solution)/shard_map/pallas_call | solution.py:209
  81.2 0.0 collective-permute-done.17.other_ref
  81.2 27.1 %shard_map.83.inverse_ref = f32[512,512]{1,0:T(8,128)S(1)} custom-call(f32[640,128]{1,0:T(8,128)S(1)} %constant_dynamic-update-slice_fusion.own_ref, f32[640,128]{1,0:T(8,128)S(1)} %collective-permute-done.17.other_ref), custom_call_target="tpu_custom_call" | custom-call | flops 30000001024 | bytes 2000000 | tf_op jit(solution)/shard_map/pallas_call | solution.py:174
  108.3 6.1 %all-gather.3.cloned.1.call-done = bf16[16384,512]{1,0:T(8,128)(2,1)} async-done(((bf16[256,512]{1,0:T(8,128)(2,1)}), bf16[16384,512]{1,0:T(8,128)(2,1)}) %all-gather.3.cloned.1.call-update) | async-done | bytes 16777232 | tf_op jit(solution)/shard_map/all_gather | solution.py:354
  114.4 8.3 %shard_map.85 = (bf16[128,512]{1,0:T(8,128)(2,1)S(1)}, bf16[128,512]{1,0:T(8,128)(2,1)S(1)}) custom-call(s32[1]{0:T(128)} %bitcast.7.count_ref, s32[3,72]{1,0:T(4,128)S(1)} %get-tuple-element.15.place_ref, bf16[72,128,128]{2,1,0:T(8,128)(2,1)S(1)} %get-tuple-element.16.values_ref, bf16[8,512,512]{2,1,0:T(8,128)(2,1)} %cores_ref.3, bf16[64,256,512]{2,1,0:T(8,128)(2,1)} %bitcast.13), custom_call_target="tpu_custom_call" | custom-call | flops 10000000000 | bytes 16000000 | tf_op jit(solution)/shard_map/pallas_call | solution.py:273
  122.8 1.3 collective-permute-start.18
  124.0 1.8 %collective-permute-start.20 = (bf16[128,512]{1,0:T(8,128)(2,1)S(1)}, bf16[128,512]{1,0:T(8,128)(2,1)S(1)}, u32[]{:S(2)}, u32[]{:S(2)}) collective-permute-start(bf16[128,512]{1,0:T(8,128)(2,1)S(1)} %get-tuple-element.19), channel_id=1, source_target_pairs={{0,192},{64,128},{128,64},{192,0},{1,193},{65,129},{129,65},{193,1... | collective-permute-start | bytes 393224 | tf_op jit(solution)/shard_map/ppermute | solution.py:317
  125.9 1.5 %collective-permute-done.18 = bf16[128,512]{1,0:T(8,128)(2,1)S(1)} collective-permute-done((bf16[128,512]{1,0:T(8,128)(2,1)S(1)}, bf16[128,512]{1,0:T(8,128)(2,1)S(1)}, u32[]{:S(2)}, u32[]{:S(2)}) %collective-permute-start.18) | collective-permute-done | bytes 131104 | tf_op jit(solution)/shard_map/ppermute | solution.py:317
  127.4 1.9 %collective-permute-start.19 = (bf16[128,512]{1,0:T(8,128)(2,1)S(1)}, bf16[128,512]{1,0:T(8,128)(2,1)S(1)}, u32[]{:S(2)}, u32[]{:S(2)}) collective-permute-start(bf16[128,512]{1,0:T(8,128)(2,1)S(1)} %add_convert_fusion.1.upper_ref), channel_id=1, source_target_pairs={{0,192},{64,128},{128,64},{192,0},{1,193},{65,129},{129,65},{193,1... | collective-permute-start | bytes 393224 | tf_op jit(solution)/shard_map/ppermute | solution.py:317
  129.2 0.4 collective-permute-done.20
  129.7 0.7 collective-permute-start.21
  130.4 2.1 %collective-permute-done.19.upper_other_ref = bf16[128,512]{1,0:T(8,128)(2,1)S(1)} collective-permute-done((bf16[128,512]{1,0:T(8,128)(2,1)S(1)}, bf16[128,512]{1,0:T(8,128)(2,1)S(1)}, u32[]{:S(2)}, u32[]{:S(2)}) %collective-permute-start.19) | collective-permute-done | bytes 131104 | tf_op jit(solution)/shard_map/ppermute | solution.py:317
  132.5 1.4 collective-permute-done.21.lower_other_ref
  133.9 1.4 shard_map.86
  (17 shorter events, 0.2 us)
Async XLA Ops:
  6.5 107.9 %all-gather.3.cloned.1.call-start = ((), (), s32[]{:S(2)}) async-start(), calls=%async_computation | async-start | bytes 17039360 | tf_op jit(solution)/shard_map/all_gather | solution.py:354
  7.3 1.0 copy-start
  8.2 69.6 %copy-start.1 = (bf16[1,72,128,128]{3,2,1,0:T(8,128)(2,1)S(1)}, bf16[1,72,128,128]{3,2,1,0:T(8,128)(2,1)}, u32[]{:S(2)}) copy-start(bf16[1,72,128,128]{3,2,1,0:T(8,128)(2,1)} %param.10) | copy-start | bytes 7077892
  8.2 69.6 %copy-start.2 = (s32[1,72]{1,0:T(1,128)S(1)}, s32[1,72]{1,0:T(1,128)}, u32[]{:S(2)}) copy-start(s32[1,72]{1,0:T(1,128)} %param.11) | copy-start | bytes 868
  8.2 69.6 %copy-start.3 = (s32[1,72]{1,0:T(1,128)S(1)}, s32[1,72]{1,0:T(1,128)}, u32[]{:S(2)}) copy-start(s32[1,72]{1,0:T(1,128)} %param.12) | copy-start | bytes 868
  8.2 69.6 %copy-start.4 = (s32[1,72]{1,0:T(1,128)S(1)}, s32[1,72]{1,0:T(1,128)}, u32[]{:S(2)}) copy-start(s32[1,72]{1,0:T(1,128)} %param.13) | copy-start | bytes 868
  8.2 69.7 %copy-start.5 = (s32[1,72]{1,0:T(1,128)S(1)}, s32[1,72]{1,0:T(1,128)}, u32[]{:S(2)}) copy-start(s32[1,72]{1,0:T(1,128)} %param.14) | copy-start | bytes 868
  18.7 4.6 %collective-permute-start = (f32[640,128]{1,0:T(8,128)S(1)}, f32[640,128]{1,0:T(8,128)S(1)}, u32[]{:S(2)}, u32[]{:S(2)}) collective-permute-start(f32[640,128]{1,0:T(8,128)S(1)} %slice.41), channel_id=1, source_target_pairs={{0,1},{1,0},{2,3},{3,2},{4,5},{5,4},{6,7},{7,6},{8,9},{9,8},{10,11... | collective-permute-start | bytes 983048 | tf_op jit(solution)/shard_map/ppermute | solution.py:329
  23.3 3.7 %collective-permute-start.3 = (f32[160,128]{1,0:T(8,128)S(1)}, f32[160,128]{1,0:T(8,128)S(1)}, u32[]{:S(2)}, u32[]{:S(2)}) collective-permute-start(f32[160,128]{1,0:T(8,128)S(1)} %get-tuple-element.23), channel_id=1, source_target_pairs={{0,192},{64,0},{128,64},{192,128},{1,193},{65,1},{129,65},{193,129... | collective-permute-start | bytes 245768 | tf_op jit(solution)/shard_map/ppermute | solution.py:313
  24.4 4.7 %collective-permute-start.2 = (f32[160,128]{1,0:T(8,128)S(1)}, f32[160,128]{1,0:T(8,128)S(1)}, u32[]{:S(2)}, u32[]{:S(2)}) collective-permute-start(f32[160,128]{1,0:T(8,128)S(1)} %get-tuple-element.24), channel_id=1, source_target_pairs={{0,64},{64,128},{128,192},{192,0},{1,65},{65,129},{129,193},{193,1... | collective-permute-start | bytes 245768 | tf_op jit(solution)/shard_map/ppermute | solution.py:313
  24.9 5.1 %collective-permute-start.1 = (f32[160,128]{1,0:T(8,128)S(1)}, f32[160,128]{1,0:T(8,128)S(1)}, u32[]{:S(2)}, u32[]{:S(2)}) collective-permute-start(f32[160,128]{1,0:T(8,128)S(1)} %get-tuple-element.25), channel_id=1, source_target_pairs={{0,128},{64,192},{128,0},{192,64},{1,129},{65,193},{129,1},{193,65... | collective-permute-start | bytes 245768 | tf_op jit(solution)/shard_map/ppermute | solution.py:313
  30.0 4.7 %collective-permute-start.6 = (f32[40,128]{1,0:T(8,128)S(1)}, f32[40,128]{1,0:T(8,128)S(1)}, u32[]{:S(2)}, u32[]{:S(2)}) collective-permute-start(f32[40,128]{1,0:T(8,128)S(1)} %get-tuple-element.26), channel_id=1, source_target_pairs={{0,48},{1,49},{2,50},{3,51},{4,52},{5,53},{6,54},{7,55},{8,56},{9,... | collective-permute-start | bytes 61448 | tf_op jit(solution)/shard_map/ppermute | solution.py:321
  33.0 4.6 %collective-permute-start.5 = (f32[40,128]{1,0:T(8,128)S(1)}, f32[40,128]{1,0:T(8,128)S(1)}, u32[]{:S(2)}, u32[]{:S(2)}) collective-permute-start(f32[40,128]{1,0:T(8,128)S(1)} %get-tuple-element.27), channel_id=1, source_target_pairs={{0,16},{1,17},{2,18},{3,19},{4,20},{5,21},{6,22},{7,23},{8,24},{9,... | collective-permute-start | bytes 61448 | tf_op jit(solution)/shard_map/ppermute | solution.py:321
  33.0 4.6 %collective-permute-start.4 = (f32[40,128]{1,0:T(8,128)S(1)}, f32[40,128]{1,0:T(8,128)S(1)}, u32[]{:S(2)}, u32[]{:S(2)}) collective-permute-start(f32[40,128]{1,0:T(8,128)S(1)} %get-tuple-element.28), channel_id=1, source_target_pairs={{0,32},{1,33},{2,34},{3,35},{4,36},{5,37},{6,38},{7,39},{8,40},{9,... | collective-permute-start | bytes 61448 | tf_op jit(solution)/shard_map/ppermute | solution.py:321
  37.6 3.1 %collective-permute-start.7 = (f32[40,128]{1,0:T(8,128)S(1)}, f32[40,128]{1,0:T(8,128)S(1)}, u32[]{:S(2)}, u32[]{:S(2)}) collective-permute-start(f32[40,128]{1,0:T(8,128)S(1)} %fusion.1), channel_id=1, source_target_pairs={{0,2},{1,3},{2,0},{3,1},{4,6},{5,7},{6,4},{7,5},{8,10},{9,11},{10,... | collective-permute-start | bytes 61448 | tf_op jit(solution)/shard_map/ppermute | solution.py:325
  40.7 8.3 %collective-permute-start.10 = (f32[40,128]{1,0:T(8,128)S(1)}, f32[40,128]{1,0:T(8,128)S(1)}, u32[]{:S(2)}, u32[]{:S(2)}) collective-permute-start(f32[40,128]{1,0:T(8,128)S(1)} %add.46), channel_id=1, source_target_pairs={{0,12},{1,13},{2,14},{3,15},{4,8},{5,9},{6,10},{7,11},{8,4},{9,5},... | collective-permute-start | bytes 61448 | tf_op jit(solution)/shard_map/ppermute | solution.py:325
  46.8 3.5 %collective-permute-start.9 = (f32[40,128]{1,0:T(8,128)S(1)}, f32[40,128]{1,0:T(8,128)S(1)}, u32[]{:S(2)}, u32[]{:S(2)}) collective-permute-start(f32[40,128]{1,0:T(8,128)S(1)} %add.46), channel_id=1, source_target_pairs={{0,4},{1,5},{2,6},{3,7},{4,0},{5,1},{6,2},{7,3},{8,12},{9,13},{10,... | collective-permute-start | bytes 61448 | tf_op jit(solution)/shard_map/ppermute | solution.py:325
  47.9 7.0 %collective-permute-start.8 = (f32[40,128]{1,0:T(8,128)S(1)}, f32[40,128]{1,0:T(8,128)S(1)}, u32[]{:S(2)}, u32[]{:S(2)}) collective-permute-start(f32[40,128]{1,0:T(8,128)S(1)} %add.46), channel_id=1, source_target_pairs={{0,8},{1,9},{2,10},{3,11},{4,12},{5,13},{6,14},{7,15},{8,0},{9,1},... | collective-permute-start | bytes 61448 | tf_op jit(solution)/shard_map/ppermute | solution.py:325
  54.9 3.2 %collective-permute-start.13 = (f32[40,128]{1,0:T(8,128)S(1)}, f32[40,128]{1,0:T(8,128)S(1)}, u32[]{:S(2)}, u32[]{:S(2)}) collective-permute-start(f32[40,128]{1,0:T(8,128)S(1)} %get-tuple-element.22), channel_id=1, source_target_pairs={{0,48},{1,49},{2,50},{3,51},{4,52},{5,53},{6,54},{7,55},{8,56},{9,... | collective-permute-start | bytes 61448 | tf_op jit(solution)/shard_map/ppermute | solution.py:321
  57.3 4.1 %collective-permute-start.12 = (f32[40,128]{1,0:T(8,128)S(1)}, f32[40,128]{1,0:T(8,128)S(1)}, u32[]{:S(2)}, u32[]{:S(2)}) collective-permute-start(f32[40,128]{1,0:T(8,128)S(1)} %get-tuple-element.22), channel_id=1, source_target_pairs={{0,32},{1,33},{2,34},{3,35},{4,36},{5,37},{6,38},{7,39},{8,40},{9,... | collective-permute-start | bytes 61448 | tf_op jit(solution)/shard_map/ppermute | solution.py:321
  57.3 4.1 %collective-permute-start.11 = (f32[40,128]{1,0:T(8,128)S(1)}, f32[40,128]{1,0:T(8,128)S(1)}, u32[]{:S(2)}, u32[]{:S(2)}) collective-permute-start(f32[40,128]{1,0:T(8,128)S(1)} %get-tuple-element.22), channel_id=1, source_target_pairs={{0,16},{1,17},{2,18},{3,19},{4,20},{5,21},{6,22},{7,23},{8,24},{9,... | collective-permute-start | bytes 61448 | tf_op jit(solution)/shard_map/ppermute | solution.py:321
  61.4 7.7 %collective-permute-start.16 = (f32[160,128]{1,0:T(8,128)S(1)}, f32[160,128]{1,0:T(8,128)S(1)}, u32[]{:S(2)}, u32[]{:S(2)}) collective-permute-start(f32[160,128]{1,0:T(8,128)S(1)} %pad_maximum_fusion), channel_id=1, source_target_pairs={{0,192},{64,0},{128,64},{192,128},{1,193},{65,1},{129,65},{193,129... | collective-permute-start | bytes 245768 | tf_op jit(solution)/shard_map/ppermute | solution.py:313
  63.0 6.1 %collective-permute-start.15 = (f32[160,128]{1,0:T(8,128)S(1)}, f32[160,128]{1,0:T(8,128)S(1)}, u32[]{:S(2)}, u32[]{:S(2)}) collective-permute-start(f32[160,128]{1,0:T(8,128)S(1)} %pad_maximum_fusion), channel_id=1, source_target_pairs={{0,128},{64,192},{128,0},{192,64},{1,129},{65,193},{129,1},{193,65... | collective-permute-start | bytes 245768 | tf_op jit(solution)/shard_map/ppermute | solution.py:313
  63.4 5.7 %collective-permute-start.14 = (f32[160,128]{1,0:T(8,128)S(1)}, f32[160,128]{1,0:T(8,128)S(1)}, u32[]{:S(2)}, u32[]{:S(2)}) collective-permute-start(f32[160,128]{1,0:T(8,128)S(1)} %pad_maximum_fusion), channel_id=1, source_target_pairs={{0,64},{64,128},{128,192},{192,0},{1,65},{65,129},{129,193},{193,1... | collective-permute-start | bytes 245768 | tf_op jit(solution)/shard_map/ppermute | solution.py:313
  69.1 12.0 %collective-permute-start.17 = (f32[640,128]{1,0:T(8,128)S(1)}, f32[640,128]{1,0:T(8,128)S(1)}, u32[]{:S(2)}, u32[]{:S(2)}) collective-permute-start(f32[640,128]{1,0:T(8,128)S(1)} %constant_dynamic-update-slice_fusion.own_ref), channel_id=1, source_target_pairs={{0,1},{1,0},{2,3},{3,2},{4,5},{5,4},{6,7},{7,6},{8,9},{9,8},{10,11... | collective-permute-start | bytes 983048 | tf_op jit(solution)/shard_map/ppermute | solution.py:329
  122.8 4.6 %collective-permute-start.18 = (bf16[128,512]{1,0:T(8,128)(2,1)S(1)}, bf16[128,512]{1,0:T(8,128)(2,1)S(1)}, u32[]{:S(2)}, u32[]{:S(2)}) collective-permute-start(bf16[128,512]{1,0:T(8,128)(2,1)S(1)} %get-tuple-element.18), channel_id=1, source_target_pairs={{0,64},{64,0},{128,192},{192,128},{1,65},{65,1},{129,193},{193,129... | collective-permute-start | bytes 393224 | tf_op jit(solution)/shard_map/ppermute | solution.py:317
  124.0 5.6 %collective-permute-start.20 = (bf16[128,512]{1,0:T(8,128)(2,1)S(1)}, bf16[128,512]{1,0:T(8,128)(2,1)S(1)}, u32[]{:S(2)}, u32[]{:S(2)}) collective-permute-start(bf16[128,512]{1,0:T(8,128)(2,1)S(1)} %get-tuple-element.19), channel_id=1, source_target_pairs={{0,192},{64,128},{128,64},{192,0},{1,193},{65,129},{129,65},{193,1... | collective-permute-start | bytes 393224 | tf_op jit(solution)/shard_map/ppermute | solution.py:317
  127.4 5.1 %collective-permute-start.19 = (bf16[128,512]{1,0:T(8,128)(2,1)S(1)}, bf16[128,512]{1,0:T(8,128)(2,1)S(1)}, u32[]{:S(2)}, u32[]{:S(2)}) collective-permute-start(bf16[128,512]{1,0:T(8,128)(2,1)S(1)} %add_convert_fusion.1.upper_ref), channel_id=1, source_target_pairs={{0,192},{64,128},{128,64},{192,0},{1,193},{65,129},{129,65},{193,1... | collective-permute-start | bytes 393224 | tf_op jit(solution)/shard_map/ppermute | solution.py:317
  129.7 4.2 %collective-permute-start.21 = (bf16[128,512]{1,0:T(8,128)(2,1)S(1)}, bf16[128,512]{1,0:T(8,128)(2,1)S(1)}, u32[]{:S(2)}, u32[]{:S(2)}) collective-permute-start(bf16[128,512]{1,0:T(8,128)(2,1)S(1)} %add_convert_fusion.lower_ref), channel_id=1, source_target_pairs={{0,64},{64,0},{128,192},{192,128},{1,65},{65,1},{129,193},{193,129... | collective-permute-start | bytes 393224 | tf_op jit(solution)/shard_map/ppermute | solution.py:317
Sparse Core Ops, SparseCore 0:
  10.1 104.2 all-gather.2

commit v7 on v6

--- a/solution.py
+++ b/solution.py
@@ -251,7 +251,7 @@
             add(step * 16 + i, step * 16 + i)
         return carry
 
-    lax.fori_loop(0, 4, main, 0)
+    lax.fori_loop(0, 4, main, 0, unroll=True)
 
     def extra(index, carry):
         add(index, place_ref[0, index] // 2)

time: 143 us -> 143 us (level)
  waiting for transfers between devices: 36.4 us -> 38.3 us
  starting transfers between devices: 39.6 us -> 37.9 us
    ppermute x4, waiting for transfers between devices: 5.36 us -> 7.21 us  [swap_y(): return lax.ppermute(v, 'rel', [(y, y ^ bits) for y in range(4)])]
    ppermute x4, starting transfers between devices: 5.66 us -> 3.93 us  [swap_y(): return lax.ppermute(v, 'rel', [(y, y ^ bits) for y in range(4)])]
  transfers between devices with their start and end apart: 23 -> 23, of which waited for: 16 -> 14; matrix products, arithmetic and copies ran while one was open for 0% -> 0% of each run, Pallas kernels for 29% -> 29%
where the time goes in v7:
time: 143 us
  Pallas kernels  51.2 us (36%)
  waiting for transfers between devices  38.3 us (27%)
  starting transfers between devices  37.9 us (27%)
  between operations  14.2 us (10%)
    pallas_call x1, Pallas kernels, inverse(): pl.pallas_call(inverse_kernel, out_shape=jax.ShapeDtypeStruct((512, 512),...  27.1 us
    ppermute x2, starting transfers between devices, swap_core(): return lax.ppermute(v, 'ent', [(e, e ^ 1) for e in range(64)])  11.4 us
    pallas_call x1, Pallas kernels, system_term(): pl.pallas_call(system_kernel, out_shape=jax.ShapeDtypeStruct((1280, 128),...  10.4 us
    ppermute x4, starting transfers between devices, swap_z(): return lax.ppermute(v, 'ent', [(e, e ^ 2 * bits) for e in range(64)])  9.61 us
    pallas_call x1, Pallas kernels, partial_rows(): pl.pallas_call(rows_kernel, out_shape=(jax.ShapeDtypeStruct((128, 512), j...  9 us
    ppermute x6, waiting for transfers between devices, over_y(): return lax.ppermute(v, 'rel', [(y, (y + d) % 4) for y in range(4)])  8.99 us
    ppermute x4, waiting for transfers between devices, swap_z(): return lax.ppermute(v, 'ent', [(e, e ^ 2 * bits) for e in range(64)])  7.75 us
    ppermute x6, starting transfers between devices, over_x(): return lax.ppermute(v, 'ent', [(e, (e + 16 * d) % 64) for e in range(64)])  7.74 us
  transfers between devices with their start and end apart: 23, of which 14 were waited for; matrix products, arithmetic and copies ran while one was open for 0% of the time, Pallas kernels for 29%

profile of v7, /device:TPU:1, one launch (start us, length us, event | category | flops | bytes accessed | tf_op | source)
XLA Modules:
  0.0 142.9 jit_solution(2300786717094791773)
XLA Ops:
  6.5 0.0 all-gather.3.cloned.1.call-start
  6.5 0.7 all-gather.3.cloned.1.call-update
  7.3 0.0 copy-start
  7.3 0.9 copy-done
  8.2 0.0 copy-start.1
  8.2 0.0 copy-start.2
  8.2 0.0 copy-start.3
  8.2 0.0 copy-start.4
  8.2 0.0 copy-start.5
  8.2 10.4 %shard_map.82 = f32[1280,128]{1,0:T(8,128)S(1)} custom-call(bf16[256,512]{1,0:T(8,128)(2,1)S(1)} %copy-done, bf16[8,512,512]{2,1,0:T(8,128)(2,1)} %cores_ref.3), custom_call_target="tpu_custom_call" | custom-call | flops 12000000000 | bytes 5000000 | tf_op jit(solution)/shard_map/pallas_call | solution.py:73
  18.7 3.3 %collective-permute-start = (f32[640,128]{1,0:T(8,128)S(1)}, f32[640,128]{1,0:T(8,128)S(1)}, u32[]{:S(2)}, u32[]{:S(2)}) collective-permute-start(f32[640,128]{1,0:T(8,128)S(1)} %slice.41), channel_id=1, source_target_pairs={{0,1},{1,0},{2,3},{3,2},{4,5},{5,4},{6,7},{7,6},{8,9},{9,8},{10,11... | collective-permute-start | bytes 983048 | tf_op jit(solution)/shard_map/ppermute | solution.py:329
  22.0 1.3 collective-permute-done
  23.3 1.1 collective-permute-start.3
  24.4 0.5 collective-permute-start.2
  24.9 1.2 collective-permute-start.1
  26.1 1.0 collective-permute-done.3
  27.1 2.0 %collective-permute-done.2 = f32[160,128]{1,0:T(8,128)S(1)} collective-permute-done((f32[160,128]{1,0:T(8,128)S(1)}, f32[160,128]{1,0:T(8,128)S(1)}, u32[]{:S(2)}, u32[]{:S(2)}) %collective-permute-start.2) | collective-permute-done | bytes 81952 | tf_op jit(solution)/shard_map/ppermute | solution.py:313
  29.1 0.9 collective-permute-done.1
  30.0 3.0 %collective-permute-start.6 = (f32[40,128]{1,0:T(8,128)S(1)}, f32[40,128]{1,0:T(8,128)S(1)}, u32[]{:S(2)}, u32[]{:S(2)}) collective-permute-start(f32[40,128]{1,0:T(8,128)S(1)} %get-tuple-element.26), channel_id=1, source_target_pairs={{0,48},{1,49},{2,50},{3,51},{4,52},{5,53},{6,54},{7,55},{8,56},{9,... | collective-permute-start | bytes 61448 | tf_op jit(solution)/shard_map/ppermute | solution.py:321
  33.0 0.0 collective-permute-start.5
  33.0 1.7 %collective-permute-start.4 = (f32[40,128]{1,0:T(8,128)S(1)}, f32[40,128]{1,0:T(8,128)S(1)}, u32[]{:S(2)}, u32[]{:S(2)}) collective-permute-start(f32[40,128]{1,0:T(8,128)S(1)} %get-tuple-element.28), channel_id=1, source_target_pairs={{0,32},{1,33},{2,34},{3,35},{4,36},{5,37},{6,38},{7,39},{8,40},{9,... | collective-permute-start | bytes 61448 | tf_op jit(solution)/shard_map/ppermute | solution.py:321
  34.7 0.0 collective-permute-done.6
  34.7 2.8 %collective-permute-done.5 = f32[40,128]{1,0:T(8,128)S(1)} collective-permute-done((f32[40,128]{1,0:T(8,128)S(1)}, f32[40,128]{1,0:T(8,128)S(1)}, u32[]{:S(2)}, u32[]{:S(2)}) %collective-permute-start.5) | collective-permute-done | bytes 20512 | tf_op jit(solution)/shard_map/ppermute | solution.py:321
  37.5 0.0 collective-permute-done.4
  37.6 1.3 collective-permute-start.7
  38.8 1.8 %collective-permute-done.7 = f32[40,128]{1,0:T(8,128)S(1)} collective-permute-done((f32[40,128]{1,0:T(8,128)S(1)}, f32[40,128]{1,0:T(8,128)S(1)}, u32[]{:S(2)}, u32[]{:S(2)}) %collective-permute-start.7) | collective-permute-done | bytes 20512 | tf_op jit(solution)/shard_map/ppermute | solution.py:325
  40.7 6.1 %collective-permute-start.10 = (f32[40,128]{1,0:T(8,128)S(1)}, f32[40,128]{1,0:T(8,128)S(1)}, u32[]{:S(2)}, u32[]{:S(2)}) collective-permute-start(f32[40,128]{1,0:T(8,128)S(1)} %add.46), channel_id=1, source_target_pairs={{0,12},{1,13},{2,14},{3,15},{4,8},{5,9},{6,10},{7,11},{8,4},{9,5},... | collective-permute-start | bytes 61448 | tf_op jit(solution)/shard_map/ppermute | solution.py:325
  46.8 1.1 collective-permute-start.9
  47.9 1.1 collective-permute-start.8
  49.0 0.0 collective-permute-done.10
  49.0 1.4 collective-permute-done.9
  50.4 4.6 %collective-permute-done.8 = f32[40,128]{1,0:T(8,128)S(1)} collective-permute-done((f32[40,128]{1,0:T(8,128)S(1)}, f32[40,128]{1,0:T(8,128)S(1)}, u32[]{:S(2)}, u32[]{:S(2)}) %collective-permute-start.8) | collective-permute-done | bytes 20512 | tf_op jit(solution)/shard_map/ppermute | solution.py:325
  54.9 2.3 %collective-permute-start.13 = (f32[40,128]{1,0:T(8,128)S(1)}, f32[40,128]{1,0:T(8,128)S(1)}, u32[]{:S(2)}, u32[]{:S(2)}) collective-permute-start(f32[40,128]{1,0:T(8,128)S(1)} %get-tuple-element.22), channel_id=1, source_target_pairs={{0,48},{1,49},{2,50},{3,51},{4,52},{5,53},{6,54},{7,55},{8,56},{9,... | collective-permute-start | bytes 61448 | tf_op jit(solution)/shard_map/ppermute | solution.py:321
  57.3 0.0 collective-permute-start.12
  57.3 0.7 collective-permute-start.11
  57.9 0.2 collective-permute-done.13
  58.2 3.2 %collective-permute-done.12 = f32[40,128]{1,0:T(8,128)S(1)} collective-permute-done((f32[40,128]{1,0:T(8,128)S(1)}, f32[40,128]{1,0:T(8,128)S(1)}, u32[]{:S(2)}, u32[]{:S(2)}) %collective-permute-start.12) | collective-permute-done | bytes 20512 | tf_op jit(solution)/shard_map/ppermute | solution.py:321
  61.4 0.0 collective-permute-done.11
  61.4 1.6 %collective-permute-start.16 = (f32[160,128]{1,0:T(8,128)S(1)}, f32[160,128]{1,0:T(8,128)S(1)}, u32[]{:S(2)}, u32[]{:S(2)}) collective-permute-start(f32[160,128]{1,0:T(8,128)S(1)} %pad_maximum_fusion), channel_id=1, source_target_pairs={{0,192},{64,0},{128,64},{192,128},{1,193},{65,1},{129,65},{193,129... | collective-permute-start | bytes 245768 | tf_op jit(solution)/shard_map/ppermute | solution.py:313
  63.0 0.4 collective-permute-start.15
  63.4 0.5 collective-permute-start.14
  64.0 5.1 %collective-permute-done.14 = f32[160,128]{1,0:T(8,128)S(1)} collective-permute-done((f32[160,128]{1,0:T(8,128)S(1)}, f32[160,128]{1,0:T(8,128)S(1)}, u32[]{:S(2)}, u32[]{:S(2)}) %collective-permute-start.14) | collective-permute-done | bytes 81952 | tf_op jit(solution)/shard_map/ppermute | solution.py:313
  69.1 0.0 collective-permute-done.15
  69.1 0.0 collective-permute-done.16
  69.1 8.0 %collective-permute-start.17 = (f32[640,128]{1,0:T(8,128)S(1)}, f32[640,128]{1,0:T(8,128)S(1)}, u32[]{:S(2)}, u32[]{:S(2)}) collective-permute-start(f32[640,128]{1,0:T(8,128)S(1)} %constant_dynamic-update-slice_fusion.own_ref), channel_id=1, source_target_pairs={{0,1},{1,0},{2,3},{3,2},{4,5},{5,4},{6,7},{7,6},{8,9},{9,8},{10,11... | collective-permute-start | bytes 983048 | tf_op jit(solution)/shard_map/ppermute | solution.py:329
  77.8 0.0 copy-done.1
  77.8 0.0 copy-done.2
  77.8 0.0 copy-done.3
  77.9 0.0 copy-done.4
  77.9 0.0 copy-done.5
  77.9 3.3 %shard_map.84 = (bf16[72,128,128]{2,1,0:T(8,128)(2,1)S(1)}, s32[3,72]{1,0:T(4,128)S(1)}) custom-call(s32[72]{0:T(128)S(1)} %bitcast.9, s32[72]{0:T(128)S(1)} %bitcast.10, s32[72]{0:T(128)S(1)} %bitcast.11, s32[72]{0:T(128)S(1)} %bitcast.12, bf16[72,128,128]{2,1,0:T(8,128)(2,1)S(1)} %bitcast.8), custom_call_target="tpu_custom_call" | custom-call | flops 3000000000 | bytes 4800000 | tf_op jit(solution)/shard_map/pallas_call | solution.py:209
  81.2 0.0 collective-permute-done.17.other_ref
  81.2 27.1 %shard_map.83.inverse_ref = f32[512,512]{1,0:T(8,128)S(1)} custom-call(f32[640,128]{1,0:T(8,128)S(1)} %constant_dynamic-update-slice_fusion.own_ref, f32[640,128]{1,0:T(8,128)S(1)} %collective-permute-done.17.other_ref), custom_call_target="tpu_custom_call" | custom-call | flops 30000001024 | bytes 2000000 | tf_op jit(solution)/shard_map/pallas_call | solution.py:174
  108.3 6.1 %all-gather.3.cloned.1.call-done = bf16[16384,512]{1,0:T(8,128)(2,1)} async-done(((bf16[256,512]{1,0:T(8,128)(2,1)}), bf16[16384,512]{1,0:T(8,128)(2,1)}) %all-gather.3.cloned.1.call-update) | async-done | bytes 16777232 | tf_op jit(solution)/shard_map/all_gather | solution.py:354
  114.4 9.0 %shard_map.85 = (bf16[128,512]{1,0:T(8,128)(2,1)S(1)}, bf16[128,512]{1,0:T(8,128)(2,1)S(1)}) custom-call(s32[1]{0:T(128)} %bitcast.7.count_ref, s32[3,72]{1,0:T(4,128)S(1)} %get-tuple-element.15.place_ref, bf16[72,128,128]{2,1,0:T(8,128)(2,1)S(1)} %get-tuple-element.16.values_ref, bf16[8,512,512]{2,1,0:T(8,128)(2,1)} %cores_ref.3, bf16[64,256,512]{2,1,0:T(8,128)(2,1)} %bitcast.13), custom_call_target="tpu_custom_call" | custom-call | flops 10000000000 | bytes 16000000 | tf_op jit(solution)/shard_map/pallas_call | solution.py:273
  123.4 0.6 collective-permute-start.18
  124.0 1.8 %collective-permute-start.20 = (bf16[128,512]{1,0:T(8,128)(2,1)S(1)}, bf16[128,512]{1,0:T(8,128)(2,1)S(1)}, u32[]{:S(2)}, u32[]{:S(2)}) collective-permute-start(bf16[128,512]{1,0:T(8,128)(2,1)S(1)} %get-tuple-element.19), channel_id=1, source_target_pairs={{0,192},{64,128},{128,64},{192,0},{1,193},{65,129},{129,65},{193,1... | collective-permute-start | bytes 393224 | tf_op jit(solution)/shard_map/ppermute | solution.py:317
  125.9 3.0 %collective-permute-done.18 = bf16[128,512]{1,0:T(8,128)(2,1)S(1)} collective-permute-done((bf16[128,512]{1,0:T(8,128)(2,1)S(1)}, bf16[128,512]{1,0:T(8,128)(2,1)S(1)}, u32[]{:S(2)}, u32[]{:S(2)}) %collective-permute-start.18) | collective-permute-done | bytes 131104 | tf_op jit(solution)/shard_map/ppermute | solution.py:317
  128.9 1.4 collective-permute-start.19
  130.3 0.0 collective-permute-done.20
  130.3 0.1 collective-permute-start.21
  130.4 4.2 %collective-permute-done.19.upper_other_ref = bf16[128,512]{1,0:T(8,128)(2,1)S(1)} collective-permute-done((bf16[128,512]{1,0:T(8,128)(2,1)S(1)}, bf16[128,512]{1,0:T(8,128)(2,1)S(1)}, u32[]{:S(2)}, u32[]{:S(2)}) %collective-permute-start.19) | collective-permute-done | bytes 131104 | tf_op jit(solution)/shard_map/ppermute | solution.py:317
  134.6 0.0 collective-permute-done.21.lower_other_ref
  134.6 1.4 shard_map.86
  (17 shorter events, 0.2 us)
Async XLA Ops:
  6.5 107.9 %all-gather.3.cloned.1.call-start = ((), (), s32[]{:S(2)}) async-start(), calls=%async_computation | async-start | bytes 17039360 | tf_op jit(solution)/shard_map/all_gather | solution.py:354
  7.3 1.0 copy-start
  8.2 69.6 %copy-start.1 = (bf16[1,72,128,128]{3,2,1,0:T(8,128)(2,1)S(1)}, bf16[1,72,128,128]{3,2,1,0:T(8,128)(2,1)}, u32[]{:S(2)}) copy-start(bf16[1,72,128,128]{3,2,1,0:T(8,128)(2,1)} %param.10) | copy-start | bytes 7077892
  8.2 69.6 %copy-start.2 = (s32[1,72]{1,0:T(1,128)S(1)}, s32[1,72]{1,0:T(1,128)}, u32[]{:S(2)}) copy-start(s32[1,72]{1,0:T(1,128)} %param.11) | copy-start | bytes 868
  8.2 69.6 %copy-start.3 = (s32[1,72]{1,0:T(1,128)S(1)}, s32[1,72]{1,0:T(1,128)}, u32[]{:S(2)}) copy-start(s32[1,72]{1,0:T(1,128)} %param.12) | copy-start | bytes 868
  8.2 69.6 %copy-start.4 = (s32[1,72]{1,0:T(1,128)S(1)}, s32[1,72]{1,0:T(1,128)}, u32[]{:S(2)}) copy-start(s32[1,72]{1,0:T(1,128)} %param.13) | copy-start | bytes 868
  8.2 69.7 %copy-start.5 = (s32[1,72]{1,0:T(1,128)S(1)}, s32[1,72]{1,0:T(1,128)}, u32[]{:S(2)}) copy-start(s32[1,72]{1,0:T(1,128)} %param.14) | copy-start | bytes 868
  18.7 4.6 %collective-permute-start = (f32[640,128]{1,0:T(8,128)S(1)}, f32[640,128]{1,0:T(8,128)S(1)}, u32[]{:S(2)}, u32[]{:S(2)}) collective-permute-start(f32[640,128]{1,0:T(8,128)S(1)} %slice.41), channel_id=1, source_target_pairs={{0,1},{1,0},{2,3},{3,2},{4,5},{5,4},{6,7},{7,6},{8,9},{9,8},{10,11... | collective-permute-start | bytes 983048 | tf_op jit(solution)/shard_map/ppermute | solution.py:329
  23.3 3.7 %collective-permute-start.3 = (f32[160,128]{1,0:T(8,128)S(1)}, f32[160,128]{1,0:T(8,128)S(1)}, u32[]{:S(2)}, u32[]{:S(2)}) collective-permute-start(f32[160,128]{1,0:T(8,128)S(1)} %get-tuple-element.23), channel_id=1, source_target_pairs={{0,192},{64,0},{128,64},{192,128},{1,193},{65,1},{129,65},{193,129... | collective-permute-start | bytes 245768 | tf_op jit(solution)/shard_map/ppermute | solution.py:313
  24.4 4.7 %collective-permute-start.2 = (f32[160,128]{1,0:T(8,128)S(1)}, f32[160,128]{1,0:T(8,128)S(1)}, u32[]{:S(2)}, u32[]{:S(2)}) collective-permute-start(f32[160,128]{1,0:T(8,128)S(1)} %get-tuple-element.24), channel_id=1, source_target_pairs={{0,64},{64,128},{128,192},{192,0},{1,65},{65,129},{129,193},{193,1... | collective-permute-start | bytes 245768 | tf_op jit(solution)/shard_map/ppermute | solution.py:313
  24.9 5.1 %collective-permute-start.1 = (f32[160,128]{1,0:T(8,128)S(1)}, f32[160,128]{1,0:T(8,128)S(1)}, u32[]{:S(2)}, u32[]{:S(2)}) collective-permute-start(f32[160,128]{1,0:T(8,128)S(1)} %get-tuple-element.25), channel_id=1, source_target_pairs={{0,128},{64,192},{128,0},{192,64},{1,129},{65,193},{129,1},{193,65... | collective-permute-start | bytes 245768 | tf_op jit(solution)/shard_map/ppermute | solution.py:313
  30.0 4.7 %collective-permute-start.6 = (f32[40,128]{1,0:T(8,128)S(1)}, f32[40,128]{1,0:T(8,128)S(1)}, u32[]{:S(2)}, u32[]{:S(2)}) collective-permute-start(f32[40,128]{1,0:T(8,128)S(1)} %get-tuple-element.26), channel_id=1, source_target_pairs={{0,48},{1,49},{2,50},{3,51},{4,52},{5,53},{6,54},{7,55},{8,56},{9,... | collective-permute-start | bytes 61448 | tf_op jit(solution)/shard_map/ppermute | solution.py:321
  33.0 4.6 %collective-permute-start.5 = (f32[40,128]{1,0:T(8,128)S(1)}, f32[40,128]{1,0:T(8,128)S(1)}, u32[]{:S(2)}, u32[]{:S(2)}) collective-permute-start(f32[40,128]{1,0:T(8,128)S(1)} %get-tuple-element.27), channel_id=1, source_target_pairs={{0,16},{1,17},{2,18},{3,19},{4,20},{5,21},{6,22},{7,23},{8,24},{9,... | collective-permute-start | bytes 61448 | tf_op jit(solution)/shard_map/ppermute | solution.py:321
  33.0 4.6 %collective-permute-start.4 = (f32[40,128]{1,0:T(8,128)S(1)}, f32[40,128]{1,0:T(8,128)S(1)}, u32[]{:S(2)}, u32[]{:S(2)}) collective-permute-start(f32[40,128]{1,0:T(8,128)S(1)} %get-tuple-element.28), channel_id=1, source_target_pairs={{0,32},{1,33},{2,34},{3,35},{4,36},{5,37},{6,38},{7,39},{8,40},{9,... | collective-permute-start | bytes 61448 | tf_op jit(solution)/shard_map/ppermute | solution.py:321
  37.6 3.1 %collective-permute-start.7 = (f32[40,128]{1,0:T(8,128)S(1)}, f32[40,128]{1,0:T(8,128)S(1)}, u32[]{:S(2)}, u32[]{:S(2)}) collective-permute-start(f32[40,128]{1,0:T(8,128)S(1)} %fusion.1), channel_id=1, source_target_pairs={{0,2},{1,3},{2,0},{3,1},{4,6},{5,7},{6,4},{7,5},{8,10},{9,11},{10,... | collective-permute-start | bytes 61448 | tf_op jit(solution)/shard_map/ppermute | solution.py:325
  40.7 8.3 %collective-permute-start.10 = (f32[40,128]{1,0:T(8,128)S(1)}, f32[40,128]{1,0:T(8,128)S(1)}, u32[]{:S(2)}, u32[]{:S(2)}) collective-permute-start(f32[40,128]{1,0:T(8,128)S(1)} %add.46), channel_id=1, source_target_pairs={{0,12},{1,13},{2,14},{3,15},{4,8},{5,9},{6,10},{7,11},{8,4},{9,5},... | collective-permute-start | bytes 61448 | tf_op jit(solution)/shard_map/ppermute | solution.py:325
  46.8 3.5 %collective-permute-start.9 = (f32[40,128]{1,0:T(8,128)S(1)}, f32[40,128]{1,0:T(8,128)S(1)}, u32[]{:S(2)}, u32[]{:S(2)}) collective-permute-start(f32[40,128]{1,0:T(8,128)S(1)} %add.46), channel_id=1, source_target_pairs={{0,4},{1,5},{2,6},{3,7},{4,0},{5,1},{6,2},{7,3},{8,12},{9,13},{10,... | collective-permute-start | bytes 61448 | tf_op jit(solution)/shard_map/ppermute | solution.py:325
  47.9 7.0 %collective-permute-start.8 = (f32[40,128]{1,0:T(8,128)S(1)}, f32[40,128]{1,0:T(8,128)S(1)}, u32[]{:S(2)}, u32[]{:S(2)}) collective-permute-start(f32[40,128]{1,0:T(8,128)S(1)} %add.46), channel_id=1, source_target_pairs={{0,8},{1,9},{2,10},{3,11},{4,12},{5,13},{6,14},{7,15},{8,0},{9,1},... | collective-permute-start | bytes 61448 | tf_op jit(solution)/shard_map/ppermute | solution.py:325
  54.9 3.2 %collective-permute-start.13 = (f32[40,128]{1,0:T(8,128)S(1)}, f32[40,128]{1,0:T(8,128)S(1)}, u32[]{:S(2)}, u32[]{:S(2)}) collective-permute-start(f32[40,128]{1,0:T(8,128)S(1)} %get-tuple-element.22), channel_id=1, source_target_pairs={{0,48},{1,49},{2,50},{3,51},{4,52},{5,53},{6,54},{7,55},{8,56},{9,... | collective-permute-start | bytes 61448 | tf_op jit(solution)/shard_map/ppermute | solution.py:321
  57.3 4.1 %collective-permute-start.12 = (f32[40,128]{1,0:T(8,128)S(1)}, f32[40,128]{1,0:T(8,128)S(1)}, u32[]{:S(2)}, u32[]{:S(2)}) collective-permute-start(f32[40,128]{1,0:T(8,128)S(1)} %get-tuple-element.22), channel_id=1, source_target_pairs={{0,32},{1,33},{2,34},{3,35},{4,36},{5,37},{6,38},{7,39},{8,40},{9,... | collective-permute-start | bytes 61448 | tf_op jit(solution)/shard_map/ppermute | solution.py:321
  57.3 4.1 %collective-permute-start.11 = (f32[40,128]{1,0:T(8,128)S(1)}, f32[40,128]{1,0:T(8,128)S(1)}, u32[]{:S(2)}, u32[]{:S(2)}) collective-permute-start(f32[40,128]{1,0:T(8,128)S(1)} %get-tuple-element.22), channel_id=1, source_target_pairs={{0,16},{1,17},{2,18},{3,19},{4,20},{5,21},{6,22},{7,23},{8,24},{9,... | collective-permute-start | bytes 61448 | tf_op jit(solution)/shard_map/ppermute | solution.py:321
  61.4 7.7 %collective-permute-start.16 = (f32[160,128]{1,0:T(8,128)S(1)}, f32[160,128]{1,0:T(8,128)S(1)}, u32[]{:S(2)}, u32[]{:S(2)}) collective-permute-start(f32[160,128]{1,0:T(8,128)S(1)} %pad_maximum_fusion), channel_id=1, source_target_pairs={{0,192},{64,0},{128,64},{192,128},{1,193},{65,1},{129,65},{193,129... | collective-permute-start | bytes 245768 | tf_op jit(solution)/shard_map/ppermute | solution.py:313
  63.0 6.1 %collective-permute-start.15 = (f32[160,128]{1,0:T(8,128)S(1)}, f32[160,128]{1,0:T(8,128)S(1)}, u32[]{:S(2)}, u32[]{:S(2)}) collective-permute-start(f32[160,128]{1,0:T(8,128)S(1)} %pad_maximum_fusion), channel_id=1, source_target_pairs={{0,128},{64,192},{128,0},{192,64},{1,129},{65,193},{129,1},{193,65... | collective-permute-start | bytes 245768 | tf_op jit(solution)/shard_map/ppermute | solution.py:313
  63.4 5.7 %collective-permute-start.14 = (f32[160,128]{1,0:T(8,128)S(1)}, f32[160,128]{1,0:T(8,128)S(1)}, u32[]{:S(2)}, u32[]{:S(2)}) collective-permute-start(f32[160,128]{1,0:T(8,128)S(1)} %pad_maximum_fusion), channel_id=1, source_target_pairs={{0,64},{64,128},{128,192},{192,0},{1,65},{65,129},{129,193},{193,1... | collective-permute-start | bytes 245768 | tf_op jit(solution)/shard_map/ppermute | solution.py:313
  69.1 12.0 %collective-permute-start.17 = (f32[640,128]{1,0:T(8,128)S(1)}, f32[640,128]{1,0:T(8,128)S(1)}, u32[]{:S(2)}, u32[]{:S(2)}) collective-permute-start(f32[640,128]{1,0:T(8,128)S(1)} %constant_dynamic-update-slice_fusion.own_ref), channel_id=1, source_target_pairs={{0,1},{1,0},{2,3},{3,2},{4,5},{5,4},{6,7},{7,6},{8,9},{9,8},{10,11... | collective-permute-start | bytes 983048 | tf_op jit(solution)/shard_map/ppermute | solution.py:329
  123.4 5.4 %collective-permute-start.18 = (bf16[128,512]{1,0:T(8,128)(2,1)S(1)}, bf16[128,512]{1,0:T(8,128)(2,1)S(1)}, u32[]{:S(2)}, u32[]{:S(2)}) collective-permute-start(bf16[128,512]{1,0:T(8,128)(2,1)S(1)} %get-tuple-element.18), channel_id=1, source_target_pairs={{0,64},{64,0},{128,192},{192,128},{1,65},{65,1},{129,193},{193,129... | collective-permute-start | bytes 393224 | tf_op jit(solution)/shard_map/ppermute | solution.py:317
  124.0 6.2 %collective-permute-start.20 = (bf16[128,512]{1,0:T(8,128)(2,1)S(1)}, bf16[128,512]{1,0:T(8,128)(2,1)S(1)}, u32[]{:S(2)}, u32[]{:S(2)}) collective-permute-start(bf16[128,512]{1,0:T(8,128)(2,1)S(1)} %get-tuple-element.19), channel_id=1, source_target_pairs={{0,192},{64,128},{128,64},{192,0},{1,193},{65,129},{129,65},{193,1... | collective-permute-start | bytes 393224 | tf_op jit(solution)/shard_map/ppermute | solution.py:317
  128.9 5.8 %collective-permute-start.19 = (bf16[128,512]{1,0:T(8,128)(2,1)S(1)}, bf16[128,512]{1,0:T(8,128)(2,1)S(1)}, u32[]{:S(2)}, u32[]{:S(2)}) collective-permute-start(bf16[128,512]{1,0:T(8,128)(2,1)S(1)} %add_convert_fusion.1.upper_ref), channel_id=1, source_target_pairs={{0,192},{64,128},{128,64},{192,0},{1,193},{65,129},{129,65},{193,1... | collective-permute-start | bytes 393224 | tf_op jit(solution)/shard_map/ppermute | solution.py:317
  130.3 4.3 %collective-permute-start.21 = (bf16[128,512]{1,0:T(8,128)(2,1)S(1)}, bf16[128,512]{1,0:T(8,128)(2,1)S(1)}, u32[]{:S(2)}, u32[]{:S(2)}) collective-permute-start(bf16[128,512]{1,0:T(8,128)(2,1)S(1)} %add_convert_fusion.lower_ref), channel_id=1, source_target_pairs={{0,64},{64,0},{128,192},{192,128},{1,65},{65,1},{129,193},{193,129... | collective-permute-start | bytes 393224 | tf_op jit(solution)/shard_map/ppermute | solution.py:317
Sparse Core Ops, SparseCore 0:
  10.1 104.2 all-gather.2
